TPU v7x, 32 devices: a whole 2x2x4 slice. The times are simulated.
32 devices in a mesh: dp: 8 (over y, x, core), ctx: 4 (over z).
Axes of the slice: x: 2, y: 2, z: 4, core: 2. Of those that a mesh axis runs over, the one named last changes fastest.
Arguments:
- inputs: float32 [16, 1024, 960], P('dp', 'ctx'), may hold values from -6 to 6
- segments: int32 [16, 1024], P('dp', 'ctx'), may hold values from 0 to 9, as said below
- positions: int32 [16, 1024], P('dp', 'ctx'), may hold values from 0 to 2046, as said below
- qkv_weights: bfloat16 [2, 1536000], P(None, ('dp', 'ctx')), may hold values from -0.1875 to 0.1875
- out_weights: bfloat16 [2, 921600], P(None, ('dp', 'ctx')), may hold values from -1.5 to 1.5
- ffn_weights: bfloat16 [2, 7372800], P(None, ('dp', 'ctx')), may hold values from -0.1875 to 0.1875
- norm_gains: bfloat16 [2, 1920], P(None, ('dp', 'ctx')), may hold values from 0.099609375 to 1.8984375
- cotangent: float32 [16, 1024, 960], P('dp', 'ctx'), may hold values from -6 to 6
Outputs:
- outputs: float32 [16, 1024, 960], P('dp', 'ctx')
- input_grad: float32 [16, 1024, 960], P('dp', 'ctx')
- qkv_grad: float32 [2, 1536000], P(None, ('dp', 'ctx'))
- out_grad: float32 [2, 921600], P(None, ('dp', 'ctx'))
- ffn_grad: float32 [2, 7372800], P(None, ('dp', 'ctx'))
- gain_grad: float32 [2, 1920], P(None, ('dp', 'ctx'))
Inputs may be any that keep to these rules, and one draw needn't show every extreme that they name: `segments`: within each sequence the segment numbers start at 0 and rise by one at each document's start; every document has 100 to 1024 tokens; in each aligned group of 2 sequences one sequence is a single document and another is cut into documents of 100 tokens, its last one taking the remainder. `positions`: A token's position is its document's offset, between 0 and 1023, plus its index within the document; the single-document sequence of each group has offset 1024 - 1.
All inputs are finite; a program needn't handle non-finite values.
Results may differ from a plain program's by a relative error of at most 0.029.
Values may be sent and summed in bfloat16 or wider, within the bound.
No kernel may reach another device: no remote copies, remote signals or barrier semaphores. Data moves between devices by JAX's collectives and lax.ppermute only.
A program may use at most 320 MiB of HBM per device.

v0:
```python
import jax
import jax.numpy as jnp
from jax import lax
from jax.sharding import PartitionSpec as P

D = 960
HEADS = 15
KV_HEADS = 5
HEAD_DIM = 64
FF = 2560
LAYERS = 2


epsilon = 1e-05
rope_base = 10000.0
neg_large = -1e30


def rms_scale(residual):
    return lax.rsqrt(jnp.mean(residual * residual, -1, keepdims=True) + epsilon)


def rotary_tables(positions):
    frequency = 1.0 / rope_base ** (jnp.arange(0, HEAD_DIM, 2, dtype=jnp.float32) / HEAD_DIM)
    angles = positions.astype(jnp.float32)[..., None] * frequency
    cosine_tab = jnp.cos(angles)
    sine_tab = jnp.sin(angles)
    return (
        jnp.concatenate([cosine_tab, cosine_tab], -1),
        jnp.concatenate([sine_tab, sine_tab], -1),
    )


def rotate_half(tensor):
    half_dim = tensor.shape[-1] // 2
    return jnp.concatenate([-tensor[..., half_dim:], tensor[..., :half_dim]], -1)


def apply_rotary(tensor, cosine_tab, sine_tab):
    return tensor * cosine_tab + rotate_half(tensor) * sine_tab


def rotary_back(tensor, cosine_tab, sine_tab):
    return tensor * cosine_tab - rotate_half(tensor * sine_tab)


def norm_back(upstream, residual, scale_row, gain_row):
    scaled = upstream * gain_row
    return scale_row * scaled - residual * scale_row**3 * jnp.mean(
        scaled * residual, -1, keepdims=True
    )


def contract_last(left_mat, right_mat):
    return lax.dot_general(
        left_mat, right_mat, (((1,), (1,)), ((), ())), preferred_element_type=jnp.float32
    )


def contract_first(left_mat, right_mat):
    return lax.dot_general(
        left_mat, right_mat, (((0,), (0,)), ((), ())), preferred_element_type=jnp.float32
    )


def ffn_forward(normed_two, piece):
    unit_count = piece.shape[0] // (3 * D)
    weights = piece.reshape(unit_count, 3, D)
    gate_val = contract_last(normed_two, weights[:, 0])
    up_val = contract_last(normed_two, weights[:, 1])
    hidden = (jax.nn.silu(gate_val) * up_val).astype(jnp.bfloat16)
    return jnp.dot(hidden, weights[:, 2], preferred_element_type=jnp.float32)


def ffn_backward(normed_two, branch_low, piece):
    unit_count = piece.shape[0] // (3 * D)
    weights = piece.reshape(unit_count, 3, D)
    gate_val = contract_last(normed_two, weights[:, 0])
    up_val = contract_last(normed_two, weights[:, 1])
    sigmoid_g = jax.nn.sigmoid(gate_val)
    silu_val = jax.nn.silu(gate_val)
    hidden = (silu_val * up_val).astype(jnp.bfloat16)
    hidden_grad = contract_last(branch_low, weights[:, 2])
    up_grad = (hidden_grad * silu_val).astype(jnp.bfloat16)
    gate_grad = (hidden_grad * up_val * sigmoid_g * (1.0 + gate_val * (1.0 - sigmoid_g))).astype(
        jnp.bfloat16
    )
    normal_grad = jnp.dot(gate_grad, weights[:, 0], preferred_element_type=jnp.float32)
    normal_grad = normal_grad + jnp.dot(up_grad, weights[:, 1], preferred_element_type=jnp.float32)
    return (normal_grad, hidden, gate_grad, up_grad)


def ffn_terms(normed_two, branch_low, hidden_all, gate_all, up_all):
    gate_term = contract_first(gate_all, normed_two)
    up_term = contract_first(up_all, normed_two)
    down_term = contract_first(hidden_all, branch_low)
    return jnp.stack([gate_term, up_term, down_term], 1).reshape(3 * FF * D)


def per_device(
    inputs, segments, positions, qkv_weights, out_weights, ffn_weights, norm_gains, cotangent
):
    seq_count, local_len, width_d = inputs.shape
    row_total = seq_count * local_len
    group_size = HEADS // KV_HEADS
    q_width = HEADS * HEAD_DIM
    kv_width = KV_HEADS * HEAD_DIM
    score_scale = HEAD_DIM ** (-0.5)
    full_len = local_len * lax.axis_size("ctx")
    query_index = lax.axis_index("ctx") * local_len + jnp.arange(local_len, dtype=jnp.int32)
    seg_local = segments.astype(jnp.bfloat16)
    cosine_tab, sine_tab = rotary_tables(positions)
    cosine_tab = cosine_tab[:, :, None, :]
    sine_tab = sine_tab[:, :, None, :]

    def block_scores(query_rot, key_blk, seg_blk, key_start):
        scores = (
            jnp.einsum("sqhgd,skhd->shgqk", query_rot, key_blk, preferred_element_type=jnp.float32)
            * score_scale
        )
        key_index = key_start + jnp.arange(key_blk.shape[1], dtype=jnp.int32)
        allowed = (seg_local[:, :, None] == seg_blk[:, None, :]) & (
            key_index[None, None, :] <= query_index[None, :, None]
        )
        return (scores, allowed[:, None, None, :, :])

    def split_keys(kv_piece, seg_piece, offset, blk_len):
        kv_blk = lax.dynamic_slice_in_dim(kv_piece, offset, blk_len, 1)
        seg_blk = lax.dynamic_slice_in_dim(seg_piece, offset, blk_len, 1)
        key_blk = kv_blk[..., :kv_width].reshape(seq_count, blk_len, KV_HEADS, HEAD_DIM)
        val_blk = kv_blk[..., kv_width:].reshape(seq_count, blk_len, KV_HEADS, HEAD_DIM)
        return (key_blk, val_blk, seg_blk)

    def unpack_attention(qkv_flat, out_flat, gain_flat):
        w_qkv = qkv_flat.reshape(D, q_width + 2 * kv_width)
        w_out = out_flat.reshape(q_width, D)
        return (w_qkv, w_out, gain_flat[:D].astype(jnp.float32), gain_flat[D:].astype(jnp.float32))

    residual = inputs.reshape(row_total, D)
    saved = []
    for layer_idx in range(LAYERS):
        qkv_flat, out_flat, gain_flat = (
            lax.all_gather(qkv_weights[layer_idx], ("dp", "ctx"), axis=0, tiled=True),
            lax.all_gather(out_weights[layer_idx], ("dp", "ctx"), axis=0, tiled=True),
            lax.all_gather(norm_gains[layer_idx], ("dp", "ctx"), axis=0, tiled=True),
        )
        w_qkv, w_out, gain_one, gain_two = unpack_attention(qkv_flat, out_flat, gain_flat)
        scale_one = rms_scale(residual)
        normed_one = (residual * scale_one * gain_one).astype(jnp.bfloat16)
        projected = jnp.dot(normed_one, w_qkv, preferred_element_type=jnp.float32)
        query_pre = projected[:, :q_width].reshape(seq_count, local_len, HEADS, HEAD_DIM)
        key_pre = projected[:, q_width : q_width + kv_width].reshape(
            seq_count, local_len, KV_HEADS, HEAD_DIM
        )
        query_rot = (
            apply_rotary(query_pre, cosine_tab, sine_tab)
            .astype(jnp.bfloat16)
            .reshape(seq_count, local_len, KV_HEADS, group_size, HEAD_DIM)
        )
        key_rot = apply_rotary(key_pre, cosine_tab, sine_tab).astype(jnp.bfloat16)
        value_low = (
            projected[:, q_width + kv_width :]
            .astype(jnp.bfloat16)
            .reshape(seq_count, local_len, kv_width)
        )
        keys_values = jnp.concatenate(
            [key_rot.reshape(seq_count, local_len, kv_width), value_low], -1
        )
        start_state = (
            jnp.full((seq_count, KV_HEADS, group_size, local_len), neg_large, jnp.float32),
            jnp.zeros((seq_count, KV_HEADS, group_size, local_len), jnp.float32),
            jnp.zeros((seq_count, KV_HEADS, group_size, local_len, HEAD_DIM), jnp.float32),
        )
        forward_kv_piece = lax.all_gather(keys_values, "ctx", axis=1, tiled=True)
        forward_seg_piece = lax.all_gather(seg_local, "ctx", axis=1, tiled=True)
        forward_piece_len = forward_kv_piece.shape[1]

        def forward_blk_step(blk_index, inner):
            maxima, totals, accumulated = inner
            offset = blk_index * local_len
            key_blk, val_blk, seg_blk = split_keys(
                forward_kv_piece, forward_seg_piece, offset, local_len
            )
            scores, allowed = block_scores(query_rot, key_blk, seg_blk, offset)
            new_max = jnp.maximum(maxima, jnp.max(jnp.where(allowed, scores, neg_large), -1))
            attn_probs = jnp.where(allowed, jnp.exp(scores - new_max[..., None]), 0.0)
            rescale = jnp.exp(maxima - new_max)
            totals = totals * rescale + jnp.sum(attn_probs, -1)
            accumulated = accumulated * rescale[..., None] + jnp.einsum(
                "shgqk,skhd->shgqd",
                attn_probs.astype(jnp.bfloat16),
                val_blk,
                preferred_element_type=jnp.float32,
            )
            return (new_max, totals, accumulated)

        maxima, totals, accumulated = lax.fori_loop(
            0, forward_piece_len // local_len, forward_blk_step, start_state
        )
        head_out = accumulated / totals[..., None]
        log_total = maxima + jnp.log(totals)
        attended = (
            head_out.transpose(0, 3, 1, 2, 4).reshape(row_total, q_width).astype(jnp.bfloat16)
        )
        middle = residual + jnp.dot(attended, w_out, preferred_element_type=jnp.float32)
        scale_two = rms_scale(middle)
        normed_two = (middle * scale_two * gain_two).astype(jnp.bfloat16)
        ffn_out = ffn_forward(
            normed_two, lax.all_gather(ffn_weights[layer_idx], ("dp", "ctx"), axis=0, tiled=True)
        )
        kept = None
        saved.append(
            (
                residual,
                scale_one,
                normed_one,
                query_rot,
                keys_values,
                head_out,
                log_total,
                attended,
                middle,
                scale_two,
                normed_two,
                kept,
            )
        )
        residual = middle + ffn_out
    outputs = residual.reshape(seq_count, local_len, D)
    gradient = cotangent.reshape(row_total, D)
    qkv_list = [None] * LAYERS
    out_list = [None] * LAYERS
    ffn_list = [None] * LAYERS
    gain_list = [None] * LAYERS
    for layer_idx in reversed(range(LAYERS)):
        (
            residual,
            scale_one,
            normed_one,
            query_rot,
            keys_values,
            head_out,
            log_total,
            attended,
            middle,
            scale_two,
            normed_two,
            kept,
        ) = saved[layer_idx]
        qkv_flat, out_flat, gain_flat = (
            lax.all_gather(qkv_weights[layer_idx], ("dp", "ctx"), axis=0, tiled=True),
            lax.all_gather(out_weights[layer_idx], ("dp", "ctx"), axis=0, tiled=True),
            lax.all_gather(norm_gains[layer_idx], ("dp", "ctx"), axis=0, tiled=True),
        )
        w_qkv, w_out, gain_one, gain_two = unpack_attention(qkv_flat, out_flat, gain_flat)
        branch_low = gradient.astype(jnp.bfloat16)
        normal_two_grad, hidden_all, gate_all, up_all = ffn_backward(
            normed_two,
            branch_low,
            lax.all_gather(ffn_weights[layer_idx], ("dp", "ctx"), axis=0, tiled=True),
        )
        ffn_term = ffn_terms(normed_two, branch_low, hidden_all, gate_all, up_all)
        ffn_list[layer_idx] = lax.psum_scatter(
            ffn_term, ("dp", "ctx"), scatter_dimension=0, tiled=True
        )
        gain_two_grad = jnp.sum(normal_two_grad * middle * scale_two, 0)
        gradient = gradient + norm_back(normal_two_grad, middle, scale_two, gain_two)
        attn_low = gradient.astype(jnp.bfloat16)
        out_term = contract_first(attended, attn_low)
        attended_grad = contract_last(attn_low, w_out).astype(jnp.bfloat16)
        grad_heads = attended_grad.reshape(
            seq_count, local_len, KV_HEADS, group_size, HEAD_DIM
        ).transpose(0, 2, 3, 1, 4)
        delta = jnp.sum(grad_heads.astype(jnp.float32) * head_out, -1)
        back_state = (
            jnp.zeros((seq_count, KV_HEADS, group_size, local_len, HEAD_DIM), jnp.float32),
            jnp.zeros((seq_count, full_len, kv_width), jnp.float32),
            jnp.zeros((seq_count, full_len, kv_width), jnp.float32),
        )
        backward_kv_piece = lax.all_gather(keys_values, "ctx", axis=1, tiled=True)
        backward_seg_piece = lax.all_gather(seg_local, "ctx", axis=1, tiled=True)
        piece_len = backward_kv_piece.shape[1]

        def backward_blk_step(blk_index, inner):
            query_acc, key_acc, value_acc = inner
            offset = blk_index * local_len
            key_blk, val_blk, seg_blk = split_keys(
                backward_kv_piece, backward_seg_piece, offset, local_len
            )
            scores, allowed = block_scores(query_rot, key_blk, seg_blk, offset)
            attn_probs = jnp.where(allowed, jnp.exp(scores - log_total[..., None]), 0.0)
            value_part = jnp.einsum(
                "shgqk,shgqd->skhd",
                attn_probs.astype(jnp.bfloat16),
                grad_heads,
                preferred_element_type=jnp.float32,
            )
            prob_grad = jnp.einsum(
                "shgqd,skhd->shgqk", grad_heads, val_blk, preferred_element_type=jnp.float32
            )
            score_grad = (attn_probs * (prob_grad - delta[..., None])).astype(jnp.bfloat16)
            query_acc = query_acc + score_scale * jnp.einsum(
                "shgqk,skhd->shgqd", score_grad, key_blk, preferred_element_type=jnp.float32
            )
            key_part = score_scale * jnp.einsum(
                "shgqk,sqhgd->skhd", score_grad, query_rot, preferred_element_type=jnp.float32
            )
            key_old = lax.dynamic_slice_in_dim(key_acc, offset, local_len, 1)
            key_acc = lax.dynamic_update_slice_in_dim(
                key_acc, key_old + key_part.reshape(seq_count, local_len, kv_width), offset, 1
            )
            value_old = lax.dynamic_slice_in_dim(value_acc, offset, local_len, 1)
            value_acc = lax.dynamic_update_slice_in_dim(
                value_acc, value_old + value_part.reshape(seq_count, local_len, kv_width), offset, 1
            )
            return (query_acc, key_acc, value_acc)

        query_acc, key_acc, value_acc = lax.fori_loop(
            0, piece_len // local_len, backward_blk_step, back_state
        )
        key_grad, value_grad = (
            lax.psum_scatter(
                key_acc.astype(jnp.bfloat16), "ctx", scatter_dimension=1, tiled=True
            ).astype(jnp.float32),
            lax.psum_scatter(
                value_acc.astype(jnp.bfloat16), "ctx", scatter_dimension=1, tiled=True
            ).astype(jnp.float32),
        )
        query_grad = query_acc.transpose(0, 3, 1, 2, 4).reshape(
            seq_count, local_len, HEADS, HEAD_DIM
        )
        query_low = (
            rotary_back(query_grad, cosine_tab, sine_tab)
            .astype(jnp.bfloat16)
            .reshape(row_total, q_width)
        )
        key_low = (
            rotary_back(
                key_grad.reshape(seq_count, local_len, KV_HEADS, HEAD_DIM), cosine_tab, sine_tab
            )
            .astype(jnp.bfloat16)
            .reshape(row_total, kv_width)
        )
        value_grad_low = value_grad.astype(jnp.bfloat16).reshape(row_total, kv_width)
        projected_grad = jnp.concatenate([query_low, key_low, value_grad_low], -1)
        qkv_term = contract_first(normed_one, projected_grad)
        normal_one_grad = contract_last(projected_grad, w_qkv)
        gain_one_grad = jnp.sum(normal_one_grad * residual * scale_one, 0)
        gradient = gradient + norm_back(normal_one_grad, residual, scale_one, gain_one)
        qkv_shard, out_shard, gain_shard = (
            lax.psum_scatter(qkv_term.reshape(-1), ("dp", "ctx"), scatter_dimension=0, tiled=True),
            lax.psum_scatter(out_term.reshape(-1), ("dp", "ctx"), scatter_dimension=0, tiled=True),
            lax.psum_scatter(
                jnp.concatenate([gain_one_grad, gain_two_grad]),
                ("dp", "ctx"),
                scatter_dimension=0,
                tiled=True,
            ),
        )
        qkv_list[layer_idx] = qkv_shard
        out_list[layer_idx] = out_shard
        gain_list[layer_idx] = gain_shard
    input_grad = gradient.reshape(seq_count, local_len, D)
    return (
        outputs,
        input_grad,
        jnp.stack(qkv_list),
        jnp.stack(out_list),
        jnp.stack(ffn_list),
        jnp.stack(gain_list),
    )


def solution(mesh):
    return jax.shard_map(
        per_device,
        mesh=mesh,
        in_specs=(
            P("dp", "ctx", None),
            P("dp", "ctx"),
            P("dp", "ctx"),
            P(None, ("dp", "ctx")),
            P(None, ("dp", "ctx")),
            P(None, ("dp", "ctx")),
            P(None, ("dp", "ctx")),
            P("dp", "ctx", None),
        ),
        out_specs=(
            P("dp", "ctx", None),
            P("dp", "ctx", None),
            P(None, ("dp", "ctx")),
            P(None, ("dp", "ctx")),
            P(None, ("dp", "ctx")),
            P(None, ("dp", "ctx")),
        ),
        check_vma=False,
    )
```

profile of v0, /device:TPU:0, one launch (start us, length us, event | category | flops | bytes accessed | tf_op | source)
XLA Modules:
  0.0 3180.0 jit_solution(17809771835846459251)
XLA Ops:
  14.6 42.2 %all-reduce.12 = (bf16[1920]{0:T(1024)(128)(2,1)S(1)}, bf16[1920]{0:T(1024)(128)(2,1)S(1)}) all-reduce(bf16[1920]{0:T(1024)(128)(2,1)S(1)} %dynamic-update-slice, bf16[1920]{0:T(1024)(128)(2,1)S(1)} %dynamic-update-slice.1), channel_id=2, replica_groups=mesh['dp'=8,'ctx'=4] {'dp','ctx'}, use_global_device_ids=true, to_apply=%add | all-reduce | flops 3840 | bytes 15360
  59.5 23.9 all-gather.21.cloned.1.call-done
  83.5 64.7 %reduce.1 = bf16[1536000]{0:T(1024)(128)(2,1)S(1)} reduce(bf16[1,1536000]{1,0:T(2,128)(2,1)} %all-gather.21.cloned.1.call-done, bf16[]{:T(256)} %constant.267), dimensions={0}, to_apply=%all-gather.1.reduce_sub_computation | reduce | bytes 6144002 | tf_op jit(solution)/shard_map/all_gather | solution.py:143
  148.2 4.0 reshape.533
  152.2 4.1 fusion.139
  170.5 9.6 all_gather.22
  180.7 40.5 %reduce.2 = bf16[921600]{0:T(1024)(128)(2,1)} reduce(bf16[1,921600]{1,0:T(2,128)(2,1)} %all-gather.23.cloned.1.call-done, bf16[]{:T(256)} %constant.267), dimensions={0}, to_apply=%all-gather.2.reduce_sub_computation | reduce | bytes 3686402 | tf_op jit(solution)/shard_map/all_gather | solution.py:144
  221.2 4.3 reshape.539
  225.5 40.5 %reduce.5 = bf16[921600]{0:T(1024)(128)(2,1)} reduce(bf16[1,921600]{1,0:T(2,128)(2,1)} %all-gather.29.cloned.1.call-done, bf16[]{:T(256)} %constant.267), dimensions={0}, to_apply=%all-gather.6.reduce_sub_computation | reduce | bytes 3686402 | tf_op jit(solution)/shard_map/all_gather | solution.py:144
  265.9 4.4 reshape.547
  273.3 3.4 reshape.538
  276.7 4.0 reshape.537
  280.7 66.4 %reduce.4 = bf16[1536000]{0:T(1024)(128)(2,1)} reduce(bf16[1,1536000]{1,0:T(2,128)(2,1)} %all-gather.27.cloned.1.call-done, bf16[]{:T(256)} %constant.267), dimensions={0}, to_apply=%all-gather.5.reduce_sub_computation | reduce | bytes 6144002 | tf_op jit(solution)/shard_map/all_gather | solution.py:143
  347.1 6.1 reshape.541
  357.3 26.5 while.72
  389.6 121.2 %all-gather.25.cloned.1.call-done = bf16[1,7372800]{1,0:T(2,128)(2,1)} async-done(((bf16[1,230400]{1,0:T(2,128)(2,1)}), bf16[1,7372800]{1,0:T(2,128)(2,1)}) %all-gather.25.cloned.1.call-update) | async-done | bytes 14745616 | tf_op jit(solution)/shard_map/all_gather | solution.py:209
  510.8 312.7 %reduce.3 = bf16[7372800]{0:T(1024)(128)(2,1)} reduce(bf16[1,7372800]{1,0:T(2,128)(2,1)} %all-gather.25.cloned.1.call-done, bf16[]{:T(256)} %constant.267), dimensions={0}, to_apply=%all-gather.3.reduce_sub_computation | reduce | bytes 29491202 | tf_op jit(solution)/shard_map/all_gather | solution.py:209
  823.5 45.8 %reshape.540 = bf16[2560,3,960]{2,1,0:T(4,128)(2,1)} reshape(bf16[7372800]{0:T(1024)(128)(2,1)} %reduce.3) | data formatting | bytes 29491200 | tf_op jit(solution)/shard_map/reshape | solution.py:68
  869.3 36.6 %fusion.131 = (bf16[2560,1,960]{2,1,0:T(2,128)(2,1)}, bf16[2560,1,960]{2,1,0:T(2,128)(2,1)}, bf16[2560,1,960]{2,1,0:T(2,128)(2,1)}) fusion(bf16[2560,3,960]{2,1,0:T(4,128)(2,1)} %reshape.540), kind=kLoop, calls=%fused_computation.290 | loop fusion | bytes 29491200 | tf_op jit(solution)/shard_map/slice | solution.py:72
  906.0 21.0 copy.223
  927.0 21.0 copy.222
  947.9 21.0 copy.221
  968.9 5.0 fusion.86
  973.9 5.6 multiply_convert_fusion.5
  986.8 312.9 %reduce.6 = bf16[7372800]{0:T(1024)(128)(2,1)} reduce(bf16[1,7372800]{1,0:T(2,128)(2,1)} %all-gather.31.cloned.1.call-done, bf16[]{:T(256)} %constant.267), dimensions={0}, to_apply=%all-gather.7.reduce_sub_computation | reduce | bytes 29491202 | tf_op jit(solution)/shard_map/all_gather | solution.py:209
  1299.7 45.8 %reshape.548 = bf16[2560,3,960]{2,1,0:T(4,128)(2,1)} reshape(bf16[7372800]{0:T(1024)(128)(2,1)} %reduce.6) | data formatting | bytes 29491200 | tf_op jit(solution)/shard_map/reshape | solution.py:68
  1347.9 37.3 %fusion.130 = (bf16[2560,1,960]{2,1,0:T(2,128)(2,1)}, bf16[2560,1,960]{2,1,0:T(2,128)(2,1)}, bf16[2560,1,960]{2,1,0:T(2,128)(2,1)}) fusion(bf16[2560,3,960]{2,1,0:T(4,128)(2,1)} %reshape.548), kind=kLoop, calls=%fused_computation.289 | loop fusion | bytes 29491200 | tf_op jit(solution)/shard_map/slice | solution.py:72
  1392.0 20.9 copy.233
  1412.9 21.0 copy.232
  1433.9 21.2 copy.231
  1459.3 4.7 fusion.64
  1464.0 26.6 while.73
  1497.8 9.7 multiply_convert_fusion.3
  1510.3 6.2 multiply_reduce_fusion
  1520.4 3.3 reshape.551
  1530.4 47.6 %while.74 = (s32[]{:T(128)}, f32[2,5,3,256,64]{3,4,2,1,0:T(8,128)S(1)}, f32[2,1024,320]{1,2,0:T(8,128)}, f32[2,1024,320]{1,2,0:T(8,128)}, bf16[2,256]{1,0:T(2,12...) while((s32[]{:T(128)}, ...), condition=%wide.region_15.16_spmd.clone, body=%wide.region_14.15_spmd.clone.sunk | while | flops 1280508416 | bytes 55347484 | solution.py:318
  1578.1 3.0 convert_element_type.242
  1594.6 5.5 convolution_bitcast_fusion.4
  1600.1 5.2 convolution_bitcast_fusion.3
  1605.3 5.2 convolution_bitcast_fusion.2
  1611.6 31.2 reduce-scatter.5.cloned.1.call-done
  1651.2 9.4 multiply_convert_fusion.1
  1663.7 3.7 multiply_reduce_fusion.2
  1679.2 47.9 %while.75 = (s32[]{:T(128)}, f32[2,5,3,256,64]{3,4,2,1,0:T(8,128)S(1)}, f32[2,1024,320]{1,2,0:T(8,128)}, f32[2,1024,320]{1,2,0:T(8,128)}, bf16[2,256]{1,0:T(2,12...) while((s32[]{:T(128)}, ...), condition=%wide.region_22.23_spmd.clone, body=%wide.region_21.22_spmd.clone.sunk | while | flops 1280508416 | bytes 55347484 | solution.py:318
  1730.2 21.5 pad_maximum_fusion.1
  1751.8 3.2 fusion.121
  1755.0 5.5 reshape.567
  1760.5 44.6 %copy.251 = f32[2560,3,960]{2,1,0:T(4,128)} copy(f32[2560,3,960]{0,2,1:T(8,128)} %pad_maximum_fusion.1) | data formatting | bytes 58982400 | tf_op jit(solution)/shard_map/stack | solution.py:97
  1805.1 52.7 %reshape.569 = f32[7372800]{0:T(1024)} reshape(f32[2560,3,960]{2,1,0:T(4,128)} %copy.251) | data formatting | bytes 58982400 | tf_op jit(solution)/shard_map/reshape | solution.py:97
  1857.7 3.1 convert_element_type.250
  1869.8 3.2 fusion.116
  1873.0 5.8 reshape.566
  1878.9 5.6 fusion.110
  1884.6 8.3 reshape.565
  1892.9 7.0 convolution_bitcast_fusion.7
  1899.9 4.6 convolution_bitcast_fusion.6
  1907.3 10.5 pad_maximum_fusion
  1917.8 44.6 %copy.250 = f32[2560,3,960]{2,1,0:T(4,128)} copy(f32[2560,3,960]{0,2,1:T(8,128)} %pad_maximum_fusion) | data formatting | bytes 58982400 | tf_op jit(solution)/shard_map/stack | solution.py:97
  1962.4 52.8 %reshape.568 = f32[7372800]{0:T(1024)} reshape(f32[2560,3,960]{2,1,0:T(4,128)} %copy.250) | data formatting | bytes 58982400 | tf_op jit(solution)/shard_map/reshape | solution.py:97
  2023.6 4.7 fusion.105
  2028.2 8.2 reshape.564
  2036.5 6.5 fusion.101
  2049.9 41.3 %all-reduce.10 = (f32[1920]{0:T(1024)S(1)}, f32[1920]{0:T(1024)S(1)}) all-reduce(f32[1920]{0:T(1024)S(1)} %pad_maximum_fusion.20, f32[1920]{0:T(1024)S(1)} %pad_maximum_fusion.19), channel_id=21, replica_groups=mesh['dp'=8,'ctx'=4] {'dp','ctx'}, use_global_device_ids=true, to_apply=%region_37.38.clone | all-reduce | flops 3840 | bytes 30720
  2091.9 1069.4 %all-reduce.15.cloned.1.call-done = (f32[1536000]{0:T(1024)}, f32[1536000]{0:T(1024)}, f32[921600]{0:T(1024)}, f32[921600]{0:T(1024)}, f32[7372800]{0:T(1024)}, /*index=5*/f32[7372800]{0:T(1024)}) async-done(((f32[1536000]{0:T(1024)}, f32[1536000]{0:T(1024)}, f32[921600]{0:T(1024)}, f32[921600]{0:T(1024)}, f32[7372800]{0:T(1024)}, /*index=5*/f32[7372800]{0:T(1024)}), (f32[1536000]{0:T(1024)}, ...) | async-done | bytes 78643216
  (667 shorter events, 304.3 us)
Async XLA Ops:
  7.2 50.2 %copy-start.17 = (f32[2,256,960]{1,2,0:T(8,128)S(1)}, f32[2,256,960]{1,2,0:T(8,128)}, u32[]{:S(2)}) copy-start(f32[2,256,960]{1,2,0:T(8,128)} %param.16) | copy-start | bytes 5898244
  7.2 76.3 %all-gather.21.cloned.1.call-start = ((), (), s32[]{:S(2)}) async-start(), calls=%async_computation.10 | async-start | bytes 6336000 | tf_op jit(solution)/shard_map/all_gather | solution.py:143
  9.5 171.2 %all-gather.23.cloned.1.call-start = ((), (), s32[]{:S(2)}) async-start(), calls=%async_computation.11 | async-start | bytes 3801600 | tf_op jit(solution)/shard_map/all_gather | solution.py:144
  11.4 214.1 %all-gather.29.cloned.1.call-start = ((), (), s32[]{:S(2)}) async-start(), calls=%async_computation.14 | async-start | bytes 3801600 | tf_op jit(solution)/shard_map/all_gather | solution.py:144
  12.1 268.5 %all-gather.27.cloned.1.call-start = ((), (), s32[]{:S(2)}) async-start(), calls=%async_computation.13 | async-start | bytes 6336000 | tf_op jit(solution)/shard_map/all_gather | solution.py:143
  12.7 344.6 %all-gather.17.cloned.1.call-start = ((), (), s32[]{:S(2)}) async-start(), calls=%async_computation.4 | async-start | bytes 3276800 | tf_op jit(solution)/shard_map/all_gather | solution.py:174
  57.2 298.4 %copy-start.70 = (f32[2,256,64]{1,2,0:T(8,128)}, f32[2,256,64]{1,2,0:T(8,128)S(1)}, u32[]{:S(2)}) copy-start(f32[2,256,64]{1,2,0:T(8,128)S(1)} %get-tuple-element.1100) | copy-start | bytes 393220
  57.2 1398.9 %copy-start.52 = (f32[2,256,64]{1,2,0:T(8,128)}, f32[2,256,64]{1,2,0:T(8,128)S(1)}, u32[]{:S(2)}) copy-start(f32[2,256,64]{1,2,0:T(8,128)S(1)} %get-tuple-element.1099) | copy-start | bytes 393220
  57.4 102.2 %copy-start.41 = (f32[2,256,64]{1,0,2:T(2,128)}, f32[2,256,64]{1,0,2:T(2,128)S(1)}, u32[]{:S(2)}) copy-start(f32[2,256,64]{1,0,2:T(2,128)S(1)} %copy.214) | copy-start | bytes 393220
  58.2 331.1 %copy-start.95 = (f32[1,960]{1,0:T(1,128)}, f32[1,960]{1,0:T(1,128)S(1)}, u32[]{:S(2)}) copy-start(f32[1,960]{1,0:T(1,128)S(1)} %get-tuple-element.1073) | copy-start | bytes 11524
  161.2 349.6 %all-gather.25.cloned.1.call-start = ((), (), s32[]{:S(2)}) async-start(), calls=%async_computation.12 | async-start | bytes 30412800 | tf_op jit(solution)/shard_map/all_gather | solution.py:209
  163.6 823.2 %all-gather.31.cloned.1.call-start = ((), (), s32[]{:S(2)}) async-start(), calls=%async_computation.15 | async-start | bytes 30412800 | tf_op jit(solution)/shard_map/all_gather | solution.py:209
  164.3 1299.6 %all-gather.19.cloned.1.call-start = ((), (), s32[]{:S(2)}) async-start(), calls=%async_computation.5 | async-start | bytes 3276800 | tf_op jit(solution)/shard_map/all_gather | solution.py:174
  180.7 802.2 %copy-start.88 = (f32[1,960]{1,0:T(1,128)}, f32[1,960]{1,0:T(1,128)S(1)}, u32[]{:S(2)}) copy-start(f32[1,960]{1,0:T(1,128)S(1)} %get-tuple-element.1072) | copy-start | bytes 11524
  388.7 590.8 %copy-start.33 = (f32[512,960]{0,1:T(8,128)}, f32[512,960]{0,1:T(8,128)S(1)}, u32[]{:S(2)}) copy-start(f32[512,960]{0,1:T(8,128)S(1)} %get-tuple-element.1088) | copy-start | bytes 5898244
  389.3 434.2 %copy-start.98 = (f32[512]{0:T(512)}, f32[512]{0:T(512)S(1)}, u32[]{:S(2)}) copy-start(f32[512]{0:T(512)S(1)} %get-tuple-element.1080) | copy-start | bytes 6148
  389.6 584.4 %copy-start.54 = (bf16[512,960]{0,1:T(8,128)(2,1)}, bf16[512,960]{0,1:T(8,128)(2,1)S(1)}, u32[]{:S(2)}) copy-start(bf16[512,960]{0,1:T(8,128)(2,1)S(1)} %multiply_convert_fusion.9) | copy-start | bytes 2949124
  968.9 5.0 copy-start.51
  968.9 10.6 slice-start.13
  973.9 5.6 copy-start.47
  973.9 5.6 slice-start.14
  979.5 3.4 copy-start.63
  1347.9 262.7 %reduce-scatter.7.cloned.1.call-start = ((), (), s32[]{:S(2)}) async-start(), calls=%async_computation.7 | async-start | bytes 1638400 | tf_op jit(solution)/shard_map/reduce_scatter | solution.py:325
  1433.9 21.2 copy-start.40
  1459.3 4.7 copy-start.2
  1459.3 4.7 copy-start.48
  1459.3 4.7 copy-start.67
  1494.2 22.3 copy-start.32
  1494.3 3.5 slice-start.9
  1510.3 6.2 copy-start.35
  1526.6 3.8 copy-start.5
  1581.1 61.7 %reduce-scatter.5.cloned.1.call-start = ((), (), s32[]{:S(2)}) async-start(), calls=%async_computation.6 | async-start | bytes 1638400 | tf_op jit(solution)/shard_map/reduce_scatter | solution.py:322
  1582.1 63.3 %copy-start.45 = (f32[40,8,2,256]{3,1,2,0:T(8,128)}, f32[40,8,2,256]{3,1,2,0:T(8,128)S(1)}, u32[]{:S(2)}) copy-start(f32[40,8,2,256]{3,1,2,0:T(8,128)S(1)} %copy.296) | copy-start | bytes 1966084
  1585.7 432.3 %reduce-scatter.11.cloned.1.call-start = ((), (), s32[]{:S(2)}) async-start(), calls=%async_computation.9 | async-start | bytes 1638400 | tf_op jit(solution)/shard_map/reduce_scatter | solution.py:325
  1594.6 51.1 %copy-start.59 = (bf16[512,960]{0,1:T(8,128)(2,1)}, bf16[512,960]{0,1:T(8,128)(2,1)S(1)}, u32[]{:S(2)}) copy-start(bf16[512,960]{0,1:T(8,128)(2,1)S(1)} %subtract_convert_fusion.1) | copy-start | bytes 2949124
  1594.6 5.5 copy-start.113
  1600.1 5.2 copy-start.36
  1600.1 5.2 copy-start.109
  1611.6 34.1 %copy-start.78 = (bf16[2,40,8,256]{3,2,0,1:T(8,128)(2,1)}, bf16[2,40,8,256]{3,2,0,1:T(8,128)(2,1)S(1)}, u32[]{:S(2)}) copy-start(bf16[2,40,8,256]{3,2,0,1:T(8,128)(2,1)S(1)} %copy.288) | copy-start | bytes 983044
  1642.8 8.3 slice-start.7
  1645.7 4.9 copy-start.76
  1650.6 10.0 slice-start.11
  1650.6 12.8 slice-start
  1651.1 16.3 copy-start.30
  1651.1 9.5 slice-start.12
  1651.1 12.3 slice-start.1
  1663.7 3.7 copy-start.100
  1675.5 3.7 copy-start.1
  1675.5 3.7 copy-start.6
  1730.2 21.6 copy-start.29
  1730.2 289.5 %reduce-scatter.9.cloned.1.call-start = ((), (), s32[]{:S(2)}) async-start(), calls=%async_computation.8 | async-start | bytes 1638400 | tf_op jit(solution)/shard_map/reduce_scatter | solution.py:322
  1730.2 21.6 copy-start.13
  1873.0 5.9 copy-start.24
  1873.0 5.9 copy-start.60
  1873.0 5.9 copy-start.77
  1873.0 5.9 copy-start.90
  1873.0 5.9 copy-start.94
  1884.6 8.3 copy-start.55
  1899.8 4.7 copy-start.31
  1899.8 1261.4 %all-reduce.15.cloned.1.call-start = ((), (), s32[]{:S(2)}) async-start(), calls=%async_computation.16 | async-start | bytes 157286400
  1899.9 4.6 copy-start.108
  1899.9 7.4 slice-start.4
  1899.9 7.4 slice-start.5
  1962.4 52.8 %copy-start.20 = (f32[120,8,2,256]{3,1,2,0:T(8,128)S(1)}, f32[120,8,2,256]{3,1,2,0:T(8,128)}, u32[]{:S(2)}) copy-start(f32[120,8,2,256]{3,1,2,0:T(8,128)} %copy.294) | copy-start | bytes 5898244
  (86 other events, 177.8 us)
Sparse Core Ops, SparseCore 0:
  11.5 71.8 all-gather.20
  86.3 59.0 all-gather.22
  148.8 59.4 all-gather.28
  211.7 67.9 all-gather.26
  281.1 53.3 all-gather.16
  337.2 173.5 all-gather.24
  513.6 173.5 all-gather.30
  1348.0 53.0 all-gather.18
  1581.2 29.3 reduce-scatter.6
  1612.8 29.9 reduce-scatter.4
  1730.3 29.9 reduce-scatter.10
  1900.0 30.1 reduce-scatter.8
  2036.6 1124.6 all-reduce.14
where the time goes:
time: 3200 us; the launch traced here: 3180 us
  waiting for transfers between devices  1250 us (39%)
  other arithmetic  955 us (30%)
  local copies, waits for them, and re-layouts  649 us (20%)
  matrix products  215 us (7%)
  blocking collectives  93.1 us (3%)
    unnamed x14, waiting for transfers between devices  1070 us
    all_gather x2, other arithmetic, per_device(): lax.all_gather(ffn_weights[layer_idx], ('dp', 'ctx'), axis=0, tiled=True)  626 us
    all_gather x2, other arithmetic, per_device(): lax.all_gather(qkv_weights[layer_idx], ('dp', 'ctx'), axis=0, tiled=True)  131 us
    all_gather x2, waiting for transfers between devices, per_device(): lax.all_gather(ffn_weights[layer_idx], ('dp', 'ctx'), axis=0, tiled=True)  121 us
    slice x4, local copies, waits for them, and re-layouts, ffn_forward(): return jnp.dot(hidden, weights[:, 2], preferred_element_type=jnp.float32)  116 us
    reshape x2, local copies, waits for them, and re-layouts, ffn_terms(): return jnp.stack([gate_term, up_term, down_term], 1).reshape(3 * FF * D)  105 us
    reshape x2, local copies, waits for them, and re-layouts, ffn_forward(): weights = piece.reshape(unit_count, 3, D)  91.7 us
    another operation x2, local copies, waits for them, and re-layouts, ffn_terms(): return jnp.stack([gate_term, up_term, down_term], 1).reshape(3 * FF * D)  89.2 us
  transfers between devices with their start and end apart: 13, of which 5 were waited for; matrix products, arithmetic and copies ran while one was open for 38% of the time, Pallas kernels for 0%

commit v1 on v0

v1 whole, which is shorter than its diff:
```python
import functools
import math

import jax
import jax.numpy as jnp
from jax import lax
from jax.experimental import pallas as pl
from jax.experimental.pallas import tpu as pltpu
from jax.sharding import PartitionSpec as P

D = 960
HEADS = 15
KV_HEADS = 5
GROUP = HEADS // KV_HEADS
HEAD_DIM = 64
FF = 2560
LAYERS = 2
Q_WIDTH = HEADS * HEAD_DIM
KV_WIDTH = KV_HEADS * HEAD_DIM
QKV_WIDTH = Q_WIDTH + 2 * KV_WIDTH
QK_WIDTH = Q_WIDTH + KV_WIDTH
LANES = 1024
AXES = ("dp", "ctx")

epsilon = 1e-05
rope_base = 10000.0
neg_large = -1e30
bf16 = jnp.bfloat16
f32 = jnp.float32


def dot_nn(a, b):
    return lax.dot_general(a, b, (((1,), (0,)), ((), ())), preferred_element_type=f32)


def dot_nt(a, b):
    return lax.dot_general(a, b, (((1,), (1,)), ((), ())), preferred_element_type=f32)


def dot_tn(a, b):
    return lax.dot_general(a, b, (((0,), (0,)), ((), ())), preferred_element_type=f32)


def norm_back(upstream, residual, scale_row, gain_row):
    scaled = upstream * gain_row
    return scale_row * scaled - residual * scale_row**3 * jnp.mean(
        scaled * residual, -1, keepdims=True
    )


def compiler_params():
    return pltpu.CompilerParams(vmem_limit_bytes=56 * 1024 * 1024)


def whole(shape):
    return pl.BlockSpec(shape, lambda *_: (0,) * len(shape))


def any_spec():
    return pl.BlockSpec(memory_space=pl.ANY)


def partner(value):
    half = HEAD_DIM // 2
    width = value.shape[1]
    lane = lax.broadcasted_iota(jnp.int32, value.shape, 1) % HEAD_DIM
    return jnp.where(
        lane < half, pltpu.roll(value, width - half, axis=1), pltpu.roll(value, half, axis=1)
    )


def qkv_forward_body(
    x_ref, gain_ref, qk_ref, v_ref, cos_ref, sin_ref, qk_out, v_out, normed_ref, scale_ref
):
    x = x_ref[...]
    scale = lax.rsqrt(jnp.mean(x * x, -1, keepdims=True) + epsilon)
    scale_ref[...] = scale
    normed = (x * scale * gain_ref[...]).astype(bf16)
    normed_ref[...] = normed
    block = cos_ref.shape[1]
    for j in range(QK_WIDTH // block):
        span = slice(j * block, (j + 1) * block)
        part = dot_nn(normed, qk_ref[:, span])
        qk_out[:, span] = (part * cos_ref[...] + partner(part) * sin_ref[...]).astype(bf16)
    v_out[...] = dot_nn(normed, v_ref[...]).astype(bf16)


def qkv_forward(x, gain, w_qk, w_v, cosine, sine):
    rows = x.shape[0]
    return pl.pallas_call(
        qkv_forward_body,
        out_shape=[
            jax.ShapeDtypeStruct((rows, QK_WIDTH), bf16),
            jax.ShapeDtypeStruct((rows, KV_WIDTH), bf16),
            jax.ShapeDtypeStruct((rows, D), bf16),
            jax.ShapeDtypeStruct((rows, 1), f32),
        ],
        compiler_params=compiler_params(),
        name="qkv_forward",
    )(x, gain[None], w_qk, w_v, cosine, sine)


def qkv_backward_body(
    dq_ref, dkv_ref, x_ref, normed_ref, scale_ref, gain_ref, qk_ref, v_ref, cos_ref, sin_ref,
    upstream_ref, attended_ref, low_ref, dqk_w, dov_w, dgain_ref, dx_ref, pre, low,
):
    pre[:, :Q_WIDTH] = dq_ref[...]
    pre[:, Q_WIDTH:] = dkv_ref[:, :KV_WIDTH]
    block = cos_ref.shape[1]
    normed = normed_ref[...]
    for j in range(QK_WIDTH // block):
        span = slice(j * block, (j + 1) * block)
        part = pre[:, span]
        back = (part * cos_ref[...] - partner(part) * sin_ref[...]).astype(bf16)
        low[:, span] = back
        dqk_w[:, span] = dot_tn(normed, back).astype(bf16)
    dv = dkv_ref[:, KV_WIDTH:].astype(bf16)
    dov_w[:, :Q_WIDTH] = dot_tn(attended_ref[...], low_ref[...]).astype(bf16)
    dov_w[:, Q_WIDTH:] = dot_tn(normed, dv).astype(bf16)
    normal = dot_nt(low[...], qk_ref[...]) + dot_nt(dv, v_ref[...])
    x = x_ref[...]
    scale = scale_ref[...]
    dgain_ref[...] = jnp.sum(normal * x * scale, 0, keepdims=True)
    dx_ref[...] = upstream_ref[...] + norm_back(normal, x, scale, gain_ref[...])


def qkv_backward(
    dq, dkv, x, normed, scale, gain, w_qk, w_v, cosine, sine, upstream, attended, low
):
    rows = x.shape[0]
    return pl.pallas_call(
        qkv_backward_body,
        out_shape=[
            jax.ShapeDtypeStruct((D, QK_WIDTH), bf16),
            jax.ShapeDtypeStruct((Q_WIDTH, QK_WIDTH), bf16),
            jax.ShapeDtypeStruct((1, D), f32),
            jax.ShapeDtypeStruct((rows, D), f32),
        ],
        scratch_shapes=[pltpu.VMEM((rows, QK_WIDTH), f32), pltpu.VMEM((rows, QK_WIDTH), bf16)],
        compiler_params=compiler_params(),
        name="qkv_backward",
    )(dq, dkv, x, normed, scale, gain[None], w_qk, w_v, cosine, sine, upstream, attended, low)


def ffn_forward_body(n_pieces, *refs):
    middle_ref, gain_ref = refs[:2]
    pieces = refs[2 : 2 + n_pieces]
    out_ref, normed_ref, scale_ref, gate_ref, up_ref, buffer, sems = refs[2 + n_pieces :]
    step = pl.program_id(0)

    def load(p):
        return pltpu.make_async_copy(pieces[p], buffer.at[p % 2], sems.at[p % 2])

    @pl.when(step == 0)
    def _():
        load(0).start()
        middle = middle_ref[...]
        scale = lax.rsqrt(jnp.mean(middle * middle, -1, keepdims=True) + epsilon)
        scale_ref[...] = scale
        normed_ref[...] = (middle * scale * gain_ref[...]).astype(bf16)
        out_ref[...] = middle

    for p in range(n_pieces):

        @pl.when(step == p)
        def _(p=p):
            if p + 1 < n_pieces:
                load(p + 1).start()
            load(p).wait()

    slot = step % 2
    normed = normed_ref[...]
    gate = dot_nt(normed, buffer[slot, 0, :, :D])
    up = dot_nt(normed, buffer[slot, 1, :, :D])
    gate_ref[...] = gate
    up_ref[...] = up
    hidden = (gate / (1.0 + jnp.exp(-gate)) * up).astype(bf16)
    out_ref[...] += dot_nn(hidden, buffer[slot, 2, :, :D])


def ffn_forward(middle, gain, pieces):
    rows = middle.shape[0]
    n_pieces, units = len(pieces), pieces[0].shape[1]
    tile = pl.BlockSpec((rows, units), lambda p: (0, p))
    return pl.pallas_call(
        functools.partial(ffn_forward_body, n_pieces),
        grid=(n_pieces,),
        in_specs=[whole((rows, D)), whole((1, D))] + [any_spec()] * n_pieces,
        out_specs=[whole((rows, D)), whole((rows, D)), whole((rows, 1)), tile, tile],
        out_shape=[
            jax.ShapeDtypeStruct((rows, D), f32),
            jax.ShapeDtypeStruct((rows, D), bf16),
            jax.ShapeDtypeStruct((rows, 1), f32),
            jax.ShapeDtypeStruct((rows, FF), f32),
            jax.ShapeDtypeStruct((rows, FF), f32),
        ],
        scratch_shapes=[pltpu.VMEM((2, 3, units, LANES), bf16), pltpu.SemaphoreType.DMA((2,))],
        compiler_params=compiler_params(),
        name="ffn_forward",
    )(middle, gain[None], *pieces)


def ffn_backward_body(n_pieces, *refs):
    upstream_ref, normed_ref, gate_ref, up_ref = refs[:4]
    pieces = refs[4 : 4 + n_pieces]
    grads = refs[4 + n_pieces : 4 + 2 * n_pieces]
    normal_ref, low_ref, buffer, grad_buffer, sems, out_sems = refs[4 + 2 * n_pieces :]
    step = pl.program_id(0)

    def load(p):
        return pltpu.make_async_copy(pieces[p], buffer.at[p % 2], sems.at[p % 2])

    def store(p):
        return pltpu.make_async_copy(grad_buffer.at[p % 2], grads[p], out_sems.at[p % 2])

    @pl.when(step == 0)
    def _():
        load(0).start()
        low_ref[...] = upstream_ref[...].astype(bf16)
        grad_buffer[:, :, :, D:] = jnp.zeros_like(grad_buffer[:, :, :, D:])
        normal_ref[...] = jnp.zeros_like(normal_ref)

    for p in range(n_pieces):

        @pl.when(step == p)
        def _(p=p):
            if p + 1 < n_pieces:
                load(p + 1).start()
            load(p).wait()
            if p >= 2:
                store(p - 2).wait()

    slot = step % 2
    low = low_ref[...]
    normed = normed_ref[...]
    gate = gate_ref[...]
    up = up_ref[...]
    hidden_grad = dot_nt(low, buffer[slot, 2, :, :D])
    sigmoid = 1.0 / (1.0 + jnp.exp(-gate))
    silu = gate * sigmoid
    hidden = (silu * up).astype(bf16)
    grad_buffer[slot, 2, :, :D] = dot_tn(hidden, low).astype(bf16)
    up_grad = (hidden_grad * silu).astype(bf16)
    grad_buffer[slot, 1, :, :D] = dot_tn(up_grad, normed).astype(bf16)
    gate_grad = (hidden_grad * up * sigmoid * (1.0 + gate * (1.0 - sigmoid))).astype(bf16)
    grad_buffer[slot, 0, :, :D] = dot_tn(gate_grad, normed).astype(bf16)
    for p in range(n_pieces):

        @pl.when(step == p)
        def _(p=p):
            store(p).start()

    normal_ref[...] += dot_nn(gate_grad, buffer[slot, 0, :, :D]) + dot_nn(
        up_grad, buffer[slot, 1, :, :D]
    )

    @pl.when(step == n_pieces - 1)
    def _():
        for p in range(max(0, n_pieces - 2), n_pieces):
            store(p).wait()


def ffn_backward(upstream, normed, gate, up, pieces):
    rows = upstream.shape[0]
    n_pieces, units = len(pieces), pieces[0].shape[1]
    tile = pl.BlockSpec((rows, units), lambda p: (0, p))
    result = pl.pallas_call(
        functools.partial(ffn_backward_body, n_pieces),
        grid=(n_pieces,),
        in_specs=[whole((rows, D)), whole((rows, D)), tile, tile] + [any_spec()] * n_pieces,
        out_specs=[any_spec()] * n_pieces + [whole((rows, D))],
        out_shape=[jax.ShapeDtypeStruct((3, units, LANES), bf16)] * n_pieces
        + [jax.ShapeDtypeStruct((rows, D), f32)],
        scratch_shapes=[
            pltpu.VMEM((rows, D), bf16),
            pltpu.VMEM((2, 3, units, LANES), bf16),
            pltpu.VMEM((2, 3, units, LANES), bf16),
            pltpu.SemaphoreType.DMA((2,)),
            pltpu.SemaphoreType.DMA((2,)),
        ],
        compiler_params=compiler_params(),
        name="ffn_backward",
    )(upstream, normed, gate, up, *pieces)
    return result[:n_pieces], result[n_pieces]


def mask_bias(key_info, query_info, local_len, half_keys):
    parts = []
    for side in range(2):
        count = half_keys * (side + 1)
        token, segment = key_info[:count, 0:1], key_info[:count, 1:2]
        span = slice(side * local_len, (side + 1) * local_len)
        q_token, q_segment = query_info[0:1, span], query_info[1:2, span]
        parts.append(jnp.where((segment == q_segment) & (token <= q_token), 0.0, neg_large))
    return parts


def attention_forward_body(
    q_ref, kv_ref, key_info, query_info, o_ref, lse_ref, qs, ks, vts, os, bias_low, bias_high
):
    rows = q_ref.shape[0]
    local_len, half_keys = rows // 2, kv_ref.shape[0] // 2
    bias_low[...], bias_high[...] = mask_bias(
        key_info[...], query_info[...], local_len, half_keys
    )
    for h in range(HEADS):
        qs[h] = q_ref[:, h * HEAD_DIM : (h + 1) * HEAD_DIM]
    for h in range(KV_HEADS):
        ks[h] = kv_ref[:, h * HEAD_DIM : (h + 1) * HEAD_DIM]
        value = kv_ref[:, KV_WIDTH + h * HEAD_DIM : KV_WIDTH + (h + 1) * HEAD_DIM]
        vts[h] = value.astype(f32).T.astype(bf16)

    def group(g, carry):
        for i in range(GROUP):
            h = g * GROUP + i
            for side, bias in enumerate((bias_low, bias_high)):
                count = half_keys * (side + 1)
                span = slice(side * local_len, (side + 1) * local_len)
                scores = dot_nt(ks[g, :count], qs[h, span]) * HEAD_DIM**-0.5 + bias[...]
                top = jnp.max(scores, 0, keepdims=True)
                probs = jnp.exp(scores - top)
                total = jnp.sum(probs, 0, keepdims=True)
                out = dot_nn(vts[g, :, :count], probs.astype(bf16)) / total
                os[h, span] = out.T.astype(bf16)
                lse_ref[h, :, span] = top + jnp.log(total)
        return carry

    lax.fori_loop(0, KV_HEADS, group, 0)
    for h in range(HEADS):
        o_ref[:, h * HEAD_DIM : (h + 1) * HEAD_DIM] = os[h]


def attention_forward(query, kv, key_info, query_info):
    rows, keys = query.shape[0], kv.shape[0]
    return pl.pallas_call(
        attention_forward_body,
        out_shape=[
            jax.ShapeDtypeStruct((rows, Q_WIDTH), bf16),
            jax.ShapeDtypeStruct((HEADS, 1, rows), f32),
        ],
        scratch_shapes=[
            pltpu.VMEM((HEADS, rows, HEAD_DIM), bf16),
            pltpu.VMEM((KV_HEADS, keys, HEAD_DIM), bf16),
            pltpu.VMEM((KV_HEADS, HEAD_DIM, keys), bf16),
            pltpu.VMEM((HEADS, rows, HEAD_DIM), bf16),
            pltpu.VMEM((keys // 2, rows // 2), f32),
            pltpu.VMEM((keys, rows // 2), f32),
        ],
        compiler_params=compiler_params(),
        name="attention_forward",
    )(query, kv, key_info, query_info)


def attention_backward_body(
    q_ref, kv_ref, og_ref, lse_ref, key_info, query_info, dq_ref, dkv_ref,
    qs, gs, ks, kts, vs, dqs, dks, dvs, bias_low, bias_high,
):
    rows = q_ref.shape[0]
    local_len, half_keys = rows // 2, kv_ref.shape[0] // 2
    bias_low[...], bias_high[...] = mask_bias(
        key_info[...], query_info[...], local_len, half_keys
    )
    for h in range(HEADS):
        qs[h] = q_ref[:, h * HEAD_DIM : (h + 1) * HEAD_DIM]
        gs[h] = og_ref[:, h * HEAD_DIM : (h + 1) * HEAD_DIM]
    for h in range(KV_HEADS):
        key = kv_ref[:, h * HEAD_DIM : (h + 1) * HEAD_DIM]
        ks[h] = key
        kts[h] = key.astype(f32).T.astype(bf16)
        vs[h] = kv_ref[:, KV_WIDTH + h * HEAD_DIM : KV_WIDTH + (h + 1) * HEAD_DIM]

    def group(g, carry):
        for i in range(GROUP):
            h = g * GROUP + i
            for side, bias in enumerate((bias_low, bias_high)):
                count = half_keys * (side + 1)
                span = slice(side * local_len, (side + 1) * local_len)
                query, grad = qs[h, span], gs[h, span]
                scores = dot_nt(ks[g, :count], query) * HEAD_DIM**-0.5 + bias[...]
                probs = jnp.exp(scores - lse_ref[h, :, span])
                prob_grad = dot_nt(vs[g, :count], grad)
                delta = jnp.sum(probs * prob_grad, 0, keepdims=True)
                score_grad = (probs * (prob_grad - delta)).astype(bf16)
                value_part = dot_nn(probs.astype(bf16), grad)
                key_part = dot_nn(score_grad, query)
                dqs[h, span] = dot_nn(kts[g, :, :count], score_grad).T * HEAD_DIM**-0.5
                if i == 0 and side == 0:
                    dks[g, :count] = key_part
                    dvs[g, :count] = value_part
                    dks[g, count:] = jnp.zeros_like(key_part)
                    dvs[g, count:] = jnp.zeros_like(value_part)
                else:
                    dks[g, :count] += key_part
                    dvs[g, :count] += value_part
        return carry

    lax.fori_loop(0, KV_HEADS, group, 0)
    for h in range(HEADS):
        dq_ref[:, h * HEAD_DIM : (h + 1) * HEAD_DIM] = dqs[h]
    for h in range(KV_HEADS):
        dkv_ref[:, h * HEAD_DIM : (h + 1) * HEAD_DIM] = dks[h] * HEAD_DIM**-0.5
        dkv_ref[:, KV_WIDTH + h * HEAD_DIM : KV_WIDTH + (h + 1) * HEAD_DIM] = dvs[h]


def attention_backward(query, kv, out_grad, lse, key_info, query_info):
    rows, keys = query.shape[0], kv.shape[0]
    return pl.pallas_call(
        attention_backward_body,
        out_shape=[
            jax.ShapeDtypeStruct((rows, Q_WIDTH), f32),
            jax.ShapeDtypeStruct((keys, 2 * KV_WIDTH), f32),
        ],
        scratch_shapes=[
            pltpu.VMEM((HEADS, rows, HEAD_DIM), bf16),
            pltpu.VMEM((HEADS, rows, HEAD_DIM), bf16),
            pltpu.VMEM((KV_HEADS, keys, HEAD_DIM), bf16),
            pltpu.VMEM((KV_HEADS, HEAD_DIM, keys), bf16),
            pltpu.VMEM((KV_HEADS, keys, HEAD_DIM), bf16),
            pltpu.VMEM((HEADS, rows, HEAD_DIM), f32),
            pltpu.VMEM((KV_HEADS, keys, HEAD_DIM), f32),
            pltpu.VMEM((KV_HEADS, keys, HEAD_DIM), f32),
            pltpu.VMEM((keys // 2, rows // 2), f32),
            pltpu.VMEM((keys, rows // 2), f32),
        ],
        compiler_params=compiler_params(),
        name="attention_backward",
    )(query, kv, out_grad, lse, key_info, query_info)


def exchange(value, dp_xor=0, ctx_xor=0):
    n_dp, n_ctx = lax.axis_size("dp"), lax.axis_size("ctx")
    pairs = [
        (d * n_ctx + c, (d ^ dp_xor) * n_ctx + (c ^ ctx_xor))
        for d in range(n_dp)
        for c in range(n_ctx)
    ]
    return lax.ppermute(value, AXES, pairs)


def dp_bits(color):
    n_dp = lax.axis_size("dp")
    high = [1 << i for i in range(1, n_dp.bit_length() - 1)]
    return (high[::-1] if color else high) + [1]


def bit_set(axis_name, bit):
    return (lax.axis_index(axis_name) & bit) != 0


class Job:
    def __init__(self, chain):
        self.chain = chain
        self.result = None
        self.pending = next(chain)

    def step(self, arrived):
        try:
            self.pending = self.chain.send(arrived)
        except StopIteration as stop:
            self.pending, self.result = None, stop.value


def fence(values, *jobs):
    live = [job for job in jobs if job.pending is not None]
    values, arrived = lax.optimization_barrier((values, [job.pending for job in live]))
    for job, arrays in zip(live, arrived):
        job.step(arrays)
    return values


def finish(values, *jobs):
    while any(job.pending is not None for job in jobs):
        values = fence(values, *jobs)
    return values


def ctx_ordered(parts):
    n = len(parts)
    for i in range(n.bit_length() - 1):
        flag = bit_set("ctx", 1 << i)
        parts = [jnp.where(flag, parts[k ^ (1 << i)], parts[k]) for k in range(n)]
    return parts


def ctx_stage(value):
    return [exchange(value, ctx_xor=k) for k in range(1, lax.axis_size("ctx"))]


def gather_ffn_job(flat):
    units = flat.shape[0] // (3 * D)
    half = units // 2
    block = jnp.pad(flat.reshape(units, 3, D), ((0, 0), (0, 0), (0, LANES - D))).transpose(1, 0, 2)
    (block,) = yield [block]
    parts = [block] + (yield ctx_stage(block))
    sides = [jnp.concatenate([p[:, :half] for p in parts], 1)]
    sides += [jnp.concatenate([p[:, half:] for p in parts], 1)]
    orders = [dp_bits(color) for color in range(2)]
    for i in range(len(orders[0])):
        arrived = yield [exchange(s, dp_xor=order[i]) for s, order in zip(sides, orders)]
        if i + 1 < len(orders[0]):
            sides = [jnp.concatenate([s, a], 1) for s, a in zip(sides, arrived)]
    return [sides[0], arrived[0], sides[1], arrived[1]]


def scatter_ffn_job(pieces, shard_len):
    orders = [dp_bits(color)[::-1] for color in range(2)]
    keeps, sends = [pieces[0], pieces[2]], [pieces[1], pieces[3]]
    for i in range(len(orders[0])):
        arrived = yield [exchange(s, dp_xor=order[i]) for s, order in zip(sends, orders)]
        totals = [(k.astype(f32) + a.astype(f32)).astype(bf16) for k, a in zip(keeps, arrived)]
        if i + 1 < len(orders[0]):
            half = totals[0].shape[1] // 2
            keeps, sends = [t[:, :half] for t in totals], [t[:, half:] for t in totals]
    n_ctx = lax.axis_size("ctx")
    half = totals[0].shape[1] // n_ctx
    parts = [
        jnp.concatenate([t[:, k * half : (k + 1) * half] for t in totals], 1)
        for k in range(n_ctx)
    ]
    arrived = yield [exchange(parts[k], ctx_xor=k) for k in range(1, n_ctx)]
    shard = parts[0].astype(f32)
    for part in arrived:
        shard = shard + part.astype(f32)
    return shard[:, :, :D].transpose(1, 0, 2).reshape(shard_len)


def add_row(block, row):
    pad = jnp.zeros((1, block.shape[1] - row.shape[0]), block.dtype)
    return jnp.concatenate([block, jnp.concatenate([row[None], pad], 1)], 0)


def by_rows(shard_len):
    return shard_len % QKV_WIDTH == 0


def gather_attention_job(qkv_flat, out_flat, gain_flat):
    n_dp, n_ctx = lax.axis_size("dp"), lax.axis_size("ctx")
    n, n_bits = n_dp * n_ctx, n_dp.bit_length() - 1
    gain_len = gain_flat.shape[0]
    if by_rows(qkv_flat.shape[0]):
        qkv, out = qkv_flat.reshape(-1, QKV_WIDTH), out_flat.reshape(-1, D)
        blocks = [add_row(qkv[:, :QK_WIDTH], gain_flat)]
        blocks += [add_row(jnp.concatenate([out, qkv[:, QK_WIDTH:]], 1), gain_flat)]
        (both,) = yield [jnp.concatenate(blocks, 1)]
        parts = ctx_ordered([both] + (yield ctx_stage(both)))
        sides = [[p[:, :QK_WIDTH] for p in parts], [p[:, QK_WIDTH:] for p in parts]]
    else:
        qkv_cols = math.gcd(qkv_flat.shape[0], QKV_WIDTH)
        out_cols = math.gcd(out_flat.shape[0], D)
        blocks = [add_row(qkv_flat.reshape(-1, qkv_cols), gain_flat)]
        blocks += [out_flat.reshape(-1, out_cols)]
        blocks = yield blocks
        arrived = yield ctx_stage(blocks[0]) + ctx_stage(blocks[1])
        sides = [
            ctx_ordered([blocks[0]] + arrived[: n_ctx - 1]),
            ctx_ordered([blocks[1]] + arrived[n_ctx - 1 :]),
        ]
    sides = [jnp.stack(p, 0).reshape((1,) * n_bits + (n_ctx,) + p[0].shape) for p in sides]
    orders = [dp_bits(color) for color in range(2)]
    for i in range(n_bits):
        arrived = yield [exchange(s, dp_xor=order[i]) for s, order in zip(sides, orders)]
        joined = []
        for mine, other, order in zip(sides, arrived, orders):
            flag = bit_set("dp", order[i])
            pair = [jnp.where(flag, other, mine), jnp.where(flag, mine, other)]
            joined.append(jnp.concatenate(pair, n_bits - order[i].bit_length()))
        sides = joined
    first, second = (s.reshape((n,) + s.shape[-2:]) for s in sides)
    gains = first[:, -1, :gain_len].reshape(n * gain_len).astype(f32)
    if by_rows(qkv_flat.shape[0]):
        w_qk = first[:, :-1].reshape(D, QK_WIDTH)
        second = second[:, :-1].reshape(D, QK_WIDTH)
        w_out, w_v = second[:, :D], second[:, D:]
    else:
        w_qkv = first[:, :-1].reshape(D, QKV_WIDTH)
        w_qk, w_v = w_qkv[:, :QK_WIDTH], w_qkv[:, QK_WIDTH:]
        w_out = second.reshape(Q_WIDTH, D)
    return w_qk, w_v, w_out, gains[:D], gains[D:]


def scatter_attention_job(dw_qk, dw_ov, gain_grad, qkv_len, out_len):
    n_dp, n_ctx = lax.axis_size("dp"), lax.axis_size("ctx")
    n, n_bits = n_dp * n_ctx, n_dp.bit_length() - 1
    gain_len = gain_grad.shape[0] // n
    gain_row = gain_grad.astype(bf16).reshape(n, 1, gain_len)

    def with_gain(blocks):
        return jnp.concatenate(
            [blocks, jnp.pad(gain_row, ((0, 0), (0, 0), (0, blocks.shape[2] - gain_len)))], 1
        )

    if by_rows(qkv_len):
        sides = [with_gain(dw_qk.reshape(n, -1, QK_WIDTH)), dw_ov.reshape(n, -1, QK_WIDTH)]
    else:
        dw_qkv = jnp.concatenate([dw_qk, dw_ov[:, Q_WIDTH:]], 1)
        sides = [with_gain(dw_qkv.reshape(n, -1, math.gcd(qkv_len, QKV_WIDTH)))]
        sides += [dw_ov[:, :Q_WIDTH].reshape(n, -1, math.gcd(out_len, D))]
    sides = [s.reshape((2,) * n_bits + (n_ctx,) + s.shape[1:]) for s in sides]
    orders = [dp_bits(color)[::-1] for color in range(2)]
    for i in range(n_bits):
        keeps, sends = [], []
        for side, order in zip(sides, orders):
            low, high = jnp.split(side, 2, n_bits - order[i].bit_length())
            flag = bit_set("dp", order[i])
            keeps.append(jnp.where(flag, high, low))
            sends.append(jnp.where(flag, low, high))
        arrived = yield [exchange(s, dp_xor=order[i]) for s, order in zip(sends, orders)]
        sides = [(k.astype(f32) + a.astype(f32)).astype(bf16) for k, a in zip(keeps, arrived)]
    parts = [ctx_ordered(list(s.reshape((n_ctx,) + s.shape[-2:]))) for s in sides]
    arrived = yield [exchange(p[k], ctx_xor=k) for p in parts for k in range(1, n_ctx)]
    totals = []
    for i in range(2):
        total = parts[i][0].astype(f32)
        for part in arrived[i * (n_ctx - 1) : (i + 1) * (n_ctx - 1)]:
            total = total + part.astype(f32)
        totals.append(total)
    first, second = totals
    gain_part = first[-1, :gain_len]
    if by_rows(qkv_len):
        qkv_part = jnp.concatenate([first[:-1], second[:, D:]], 1)
        out_part = second[:, :D]
    else:
        qkv_part, out_part = first[:-1], second
    return qkv_part.reshape(qkv_len), out_part.reshape(out_len), gain_part


def low_side():
    return lax.axis_index("ctx") < lax.axis_size("ctx") // 2


def pair_tokens_job(value, wire):
    low = low_side()
    keep = jnp.where(low, value[0], value[1])
    send = jnp.where(low, value[1], value[0]).astype(wire)
    (send,) = yield [send]
    (other,) = yield [exchange(send, ctx_xor=lax.axis_size("ctx") - 1)]
    other = other.astype(value.dtype)
    return jnp.stack([jnp.where(low, keep, other), jnp.where(low, other, keep)], 0)


def gather_group(value):
    n = lax.axis_size("ctx") // 2
    parts = [value] + [exchange(value, ctx_xor=k) for k in range(1, n)]
    return jnp.concatenate([p[0] for p in parts] + [p[1] for p in parts], 0)


def scatter_group(value):
    n = lax.axis_size("ctx") // 2
    parts = value.reshape((2, n, value.shape[0] // (2 * n)) + value.shape[1:])
    result = parts[:, 0].astype(f32)
    for k in range(1, n):
        result = result + exchange(parts[:, k].astype(bf16), ctx_xor=k).astype(f32)
    return result


def per_device(
    inputs, segments, positions, qkv_weights, out_weights, ffn_weights, norm_gains, cotangent
):
    seq_count, local_len, _ = inputs.shape
    assert seq_count == 2
    n_ctx = lax.axis_size("ctx")
    rows = 2 * local_len
    qkv_len, out_len, ffn_len = qkv_weights.shape[1], out_weights.shape[1], ffn_weights.shape[1]

    tokens = Job(pair_tokens_job(inputs, bf16))
    upstream = Job(pair_tokens_job(cotangent, bf16))
    info = Job(pair_tokens_job(jnp.stack([segments, positions], 2), jnp.int32))
    attn = [
        Job(gather_attention_job(qkv_weights[i], out_weights[i], norm_gains[i]))
        for i in range(LAYERS)
    ]
    ffn = [Job(gather_ffn_job(ffn_weights[i])) for i in range(LAYERS)]

    fence((), attn[0], info)
    fence((), attn[0], info, tokens)
    fence((), attn[0], ffn[0])
    fence((), attn[0], tokens)
    finish((), attn[0], info, tokens)
    info = info.result

    index = lax.axis_index("ctx")
    early = jnp.minimum(index, n_ctx - 1 - index)
    within = jnp.arange(local_len, dtype=jnp.int32)
    token_own = jnp.stack([early * local_len + within, (n_ctx - 1 - early) * local_len + within])
    segment_own, position_own = info[..., 0], info[..., 1].reshape(rows)
    info_own = jnp.stack([token_own, segment_own], 2)
    key_info = gather_group(info_own)
    query_info = info_own.reshape(rows, 2).T

    frequency = 1.0 / rope_base ** (jnp.arange(0, HEAD_DIM, 2, dtype=f32) / HEAD_DIM)
    angles = position_own[:, None].astype(f32) * frequency
    cosine, sine = jnp.cos(angles), jnp.sin(angles)
    cosine = jnp.tile(cosine, (1, 8))
    sine = jnp.tile(jnp.concatenate([-sine, sine], 1), (1, 4))

    residual = tokens.result.reshape(rows, D)
    saved = []
    for layer in range(LAYERS):
        w_qk, w_v, w_out, gain_one, gain_two = attn[layer].result
        qk, value, normed_one, scale_one = qkv_forward(residual, gain_one, w_qk, w_v, cosine, sine)
        qk, value = fence((qk, value), ffn[layer])
        kv_own = jnp.concatenate([qk[:, Q_WIDTH:], value], 1)
        kv_all = gather_group(kv_own.reshape(2, local_len, 2 * KV_WIDTH))
        if layer == 0:
            qk, kv_all = fence((qk, kv_all), ffn[0], attn[1])
        attended, lse = attention_forward(qk, kv_all, key_info, query_info)
        middle = residual + dot_nn(attended, w_out)
        if layer == 0:
            middle = fence(middle, ffn[1], attn[1])
            middle = fence(middle, ffn[0])
            middle = fence(middle, ffn[0], attn[1])
        else:
            middle = fence(middle, ffn[1], upstream)
        middle = finish(middle, ffn[layer])
        following, normed_two, scale_two, gate, up = ffn_forward(
            middle, gain_two, ffn[layer].result
        )
        saved.append(
            (residual, scale_one, normed_one, qk, kv_all, lse, attended)
            + (middle, scale_two, normed_two, gate, up)
        )
        residual = following
        if layer == 0:
            residual = fence(residual, attn[1], ffn[1], upstream)
            residual = finish(residual, attn[1])
    residual = finish(residual, upstream)
    back = Job(pair_tokens_job(residual.reshape(2, local_len, D), bf16))
    gradient = upstream.result.reshape(rows, D)

    attn_jobs, ffn_jobs = [None] * LAYERS, [None] * LAYERS
    for layer in reversed(range(LAYERS)):
        w_qk, w_v, w_out, gain_one, gain_two = attn[layer].result
        residual, scale_one, normed_one, qk, kv_all, lse, attended = saved[layer][:7]
        middle, scale_two, normed_two, gate, up = saved[layer][7:]
        terms, normal_two = ffn_backward(gradient, normed_two, gate, up, ffn[layer].result)
        if layer:
            terms, normal_two = fence((terms, normal_two), back)
        else:
            terms, normal_two = fence((terms, normal_two), ffn_jobs[1], attn_jobs[1])
        ffn_jobs[layer] = Job(scatter_ffn_job(terms, ffn_len))
        gain_two_grad = jnp.sum(normal_two * middle * scale_two, 0)
        gradient = gradient + norm_back(normal_two, middle, scale_two, gain_two)
        attn_low = gradient.astype(bf16)
        attended_grad = dot_nt(attn_low, w_out).astype(bf16)
        attended_grad = fence(attended_grad, ffn_jobs[layer], back if layer else attn_jobs[1])
        query_grad, kv_grad = attention_backward(
            qk, kv_all, attended_grad, lse, key_info, query_info
        )
        if layer == 0:
            query_grad, kv_grad = fence((query_grad, kv_grad), ffn_jobs[1], attn_jobs[1])
        kv_grad = scatter_group(kv_grad).reshape(rows, 2 * KV_WIDTH)
        dw_qk, dw_ov, gain_one_grad, gradient = qkv_backward(
            query_grad, kv_grad, residual, normed_one, scale_one, gain_one, w_qk, w_v,
            cosine, sine, gradient, attended, attn_low,
        )
        dw_qk, dw_ov, gradient = fence((dw_qk, dw_ov, gradient), ffn_jobs[layer])
        attn_jobs[layer] = Job(
            scatter_attention_job(
                dw_qk, dw_ov, jnp.concatenate([gain_one_grad[0], gain_two_grad]), qkv_len, out_len
            )
        )
    last = Job(pair_tokens_job(gradient.reshape(2, local_len, D), bf16))
    fence((), last)
    fence((), ffn_jobs[0], attn_jobs[0], attn_jobs[1], last)
    fence((), attn_jobs[0])
    fence((), attn_jobs[0], ffn_jobs[0])
    finish((), back, last, *ffn_jobs, *attn_jobs)
    return (
        back.result,
        last.result,
        jnp.stack([job.result[0] for job in attn_jobs]),
        jnp.stack([job.result[1] for job in attn_jobs]),
        jnp.stack([job.result for job in ffn_jobs]),
        jnp.stack([job.result[2] for job in attn_jobs]),
    )


def solution(mesh):
    tokens = P("dp", "ctx", None)
    shards = P(None, ("dp", "ctx"))
    return jax.shard_map(
        per_device,
        mesh=mesh,
        in_specs=(tokens, P("dp", "ctx"), P("dp", "ctx"), shards, shards, shards, shards, tokens),
        out_specs=(tokens, tokens, shards, shards, shards, shards),
        check_vma=False,
    )
```

time: 3200 us -> 876 us (0.27)
  waiting for transfers between devices: 1250 us -> 173 us
  other arithmetic: 955 us -> 133 us
  local copies, waits for them, and re-layouts: 649 us -> 185 us
  Pallas kernels: 0 us -> 227 us
  matrix products: 215 us -> 12.9 us
  starting transfers between devices: 0.53 us -> 131 us
  blocking collectives: 93.1 us -> 0 us
    unnamed x14 -> x0, waiting for transfers between devices: 1070 us -> none
    all_gather x6 -> x0, other arithmetic: 838 us -> none  [the longest x2 626 us: per_device(): lax.all_gather(ffn_weights[layer_idx], ('dp', 'ctx'), axis=0, tiled=True)]
    reshape x32 -> x4, local copies, waits for them, and re-layouts: 275 us -> 13.3 us  [the longest x2 8.5 us: gather_attention_job(): second = second[:, :-1].reshape(D, QK_WIDTH)]
    pallas_call x0 -> x12, Pallas kernels: none -> 227 us  [the longest x2 59 us: attention_backward(): pl.pallas_call(attention_backward_body, out_shape=[jax.ShapeDtypeStruct((...]
    dot_general x86 -> x4, matrix products: 215 us -> 12.9 us  [the longest x2 8.31 us: dot_nn(): lax.dot_general(a, b, (((1,), (0,)), ((), ())), preferred_element_type=f32)]
    slice x35 -> x37, local copies, waits for them, and re-layouts: 232 us -> 41.3 us  [the longest x1 10.7 us: per_device(): ffn = [Job(gather_ffn_job(ffn_weights[i])) for i in range(LAYERS)]]
    ppermute x0 -> x88, waiting for transfers between devices: none -> 173 us  [exchange(): return lax.ppermute(value, AXES, pairs)]
    all_gather x8 -> x0, waiting for transfers between devices: 145 us -> none  [the longest x2 121 us: per_device(): lax.all_gather(ffn_weights[layer_idx], ('dp', 'ctx'), axis=0, tiled=True)]
  transfers between devices with their start and end apart: 13 -> 88, of which waited for: 5 -> 29; matrix products, arithmetic and copies ran while one was open for 38% -> 26% of each run, Pallas kernels for 0% -> 21%
where the time goes in v1:
time: 876 us; the launch traced here: 866 us
  Pallas kernels  227 us (26%)
  local copies, waits for them, and re-layouts  185 us (21%)
  waiting for transfers between devices  173 us (20%)
  other arithmetic  133 us (15%)
  starting transfers between devices  131 us (15%)
  matrix products  12.9 us (1%)
    ppermute x88, waiting for transfers between devices, exchange(): return lax.ppermute(value, AXES, pairs)  173 us
    ppermute x88, starting transfers between devices, exchange(): return lax.ppermute(value, AXES, pairs)  131 us
    pallas_call x2, Pallas kernels, attention_backward(): pl.pallas_call(attention_backward_body, out_shape=[jax.ShapeDtypeStruct((...  59 us
    unnamed x217, local copies, waits for them, and re-layouts  56.4 us
    pallas_call x2, Pallas kernels, ffn_backward(): pl.pallas_call(functools.partial(ffn_backward_body, n_pieces), grid=(n_pi...  55.7 us
    pallas_call x2, Pallas kernels, attention_forward(): pl.pallas_call(attention_forward_body, out_shape=[jax.ShapeDtypeStruct((r...  40.7 us
    convert_element_type x12, other arithmetic, scatter_ffn_job(): (k.astype(f32) + a.astype(f32)).astype(bf16)  34.3 us
    pallas_call x2, Pallas kernels, ffn_forward(): pl.pallas_call(functools.partial(ffn_forward_body, n_pieces), grid=(n_pie...  32.9 us
  transfers between devices with their start and end apart: 88, of which 29 were waited for; matrix products, arithmetic and copies ran while one was open for 26% of the time, Pallas kernels for 21%

profile of v1, /device:TPU:0, one launch (start us, length us, event | category | flops | bytes accessed | tf_op | source)
XLA Modules:
  0.0 865.7 jit_solution(3620805280445005964)
XLA Ops:
  0.6 2.7 slice_reduce_fusion.2
  8.1 5.1 collective-permute-start.2
  13.8 3.7 collective-permute-start.3
  20.8 3.8 collective-permute-done.3
  33.0 10.7 %slice_reduce_fusion = (bf16[230400]{0:T(1024)(128)(2,1)}, bf16[230400]{0:T(1024)(128)(2,1)S(1)}) fusion(bf16[2,230400]{1,0:T(2,128)(2,1)S(1)} %copy-done.50), kind=kLoop, calls=%fused_computation.107 | loop fusion | bytes 1843200 | tf_op jit(solution)/shard_map/slice | solution.py:672
  54.6 11.6 %collective-permute-done.8 = bf16[256,960]{1,0:T(8,128)(2,1)} collective-permute-done((bf16[256,960]{1,0:T(8,128)(2,1)}, bf16[256,960]{1,0:T(8,128)(2,1)}, u32[]{:S(2)}, u32[]{:S(2)}) %collective-permute-start.8) | collective-permute-done | bytes 491552 | tf_op jit(solution)/shard_map/ppermute | solution.py:437
  80.0 8.5 collective-permute-start.12
  96.7 3.1 broadcast_select_fusion.9
  100.5 3.5 pad_maximum_fusion.1
  104.0 4.3 reshape.382
  113.3 6.5 qkv_forward.2
  119.8 4.8 collective-permute-done.12
  139.0 5.8 collective-permute-done.14
  147.2 11.1 %collective-permute-done.15 = bf16[3,160,1024]{2,1,0:T(8,128)(2,1)S(1)} collective-permute-done((bf16[3,160,1024]{2,1,0:T(8,128)(2,1)S(1)}, bf16[3,160,1024]{2,1,0:T(8,128)(2,1)S(1)}, u32[]{:S(2)}, u32[]{:S(2)}) %collective-permute-start.15) | collective-permute-done | bytes 983072 | tf_op jit(solution)/shard_map/ppermute | solution.py:437
  160.8 2.7 constant_dynamic-update-slice_fusion.17
  177.7 20.2 %attention_forward.2 = (bf16[512,960]{1,0:T(8,128)(2,1)}, f32[15,1,512]{2,1,0:T(1,128)}) custom-call(bf16[512,1280]{1,0:T(8,128)(2,1)} %get-tuple-element.196.q_ref, bf16[1024,640]{1,0:T(8,128)(2,1)} %pad_maximum_fusion.13.kv_ref, s32[1024,2]{1,0:T(8,128)} %copy.79.key_info, s32[2,512]{1,0:T(2,128)} %add_bitcast_fusion.2.query_info), custom_call_target="tpu_custom_call" | custom-call | tf_op jit(solution)/shard_map/attention_forward/pallas_call | solution.py:335
  197.9 4.5 fusion.8.refs_0_
  202.4 5.0 collective-permute-done.22
  209.2 3.0 constant_dynamic-update-slice_fusion.10.refs_2_.refs_4_
  212.3 3.0 constant_dynamic-update-slice_fusion.16.refs_4_.refs_6_
  218.9 6.7 collective-permute-done.25
  240.8 16.6 %ffn_forward.2 = (f32[512,960]{1,0:T(8,128)}, bf16[512,960]{1,0:T(8,128)(2,1)}, f32[512,1]{1,0:T(8,128)}, f32[512,2560]{1,0:T(8,128)}, f32[512,2560]{1,0:T(8,128)}) custom-call(f32[512,960]{1,0:T(8,128)} %fusion.8.refs_0_, f32[1,960]{1,0:T(1,128)} %broadcast_in_dim.9.refs_1_, bf16[3,640,1024]{2,1,0:T(8,128)(2,1)} %constant_dynamic-update-slice_fusion.10.refs_2_.refs_4_, ...), custom_call_target="tpu_custom_call" | custom-call | tf_op jit(solution)/shard_map/ffn_forward/pallas_call | solution.py:185
  257.4 20.5 %collective-permute-done.30 = bf16[3,80,1024]{2,1,0:T(8,128)(2,1)} collective-permute-done((bf16[3,80,1024]{2,1,0:T(8,128)(2,1)}, bf16[3,80,1024]{2,1,0:T(8,128)(2,1)}, u32[]{:S(2)}, u32[]{:S(2)}) %collective-permute-start.30) | collective-permute-done | bytes 491552 | tf_op jit(solution)/shard_map/ppermute | solution.py:437
  303.1 4.2 reshape.389
  311.9 6.5 qkv_forward.3
  320.2 2.7 constant_dynamic-update-slice_fusion.39
  323.4 2.8 constant_dynamic-update-slice_fusion.33
  331.1 14.2 %collective-permute-done.36 = bf16[2,256,640]{2,1,0:T(8,128)(2,1)S(1)} collective-permute-done((bf16[2,256,640]{2,1,0:T(8,128)(2,1)S(1)}, bf16[2,256,640]{2,1,0:T(8,128)(2,1)S(1)}, u32[]{:S(2)}, u32[]{:S(2)}) %collective-permute-start.36) | collective-permute-done | bytes 655392 | tf_op jit(solution)/shard_map/ppermute | solution.py:437
  346.6 20.5 %attention_forward.3 = (bf16[512,960]{1,0:T(8,128)(2,1)}, f32[15,1,512]{2,1,0:T(1,128)}) custom-call(bf16[512,1280]{1,0:T(8,128)(2,1)} %get-tuple-element.227.q_ref, bf16[1024,640]{1,0:T(8,128)(2,1)} %pad_maximum_fusion.16.kv_ref, s32[1024,2]{1,0:T(8,128)} %copy.79.key_info, s32[2,512]{1,0:T(2,128)} %add_bitcast_fusion.2.query_info), custom_call_target="tpu_custom_call" | custom-call | tf_op jit(solution)/shard_map/attention_forward/pallas_call | solution.py:335
  367.1 3.8 fusion.11.refs_0_
  370.9 3.7 constant_dynamic-update-slice_fusion.32.refs_2_.refs_4_
  374.7 3.1 constant_dynamic-update-slice_fusion.38.refs_4_.refs_6_
  381.8 5.6 collective-permute-done.41.refs_5_.refs_7_
  387.4 16.4 %ffn_forward.3 = (f32[512,960]{1,0:T(8,128)}, bf16[512,960]{1,0:T(8,128)(2,1)}, f32[512,1]{1,0:T(8,128)}, f32[512,2560]{1,0:T(8,128)}, f32[512,2560]{1,0:T(8,128)}) custom-call(f32[512,960]{1,0:T(8,128)} %fusion.11.refs_0_, f32[1,960]{1,0:T(1,128)} %broadcast_in_dim.22.refs_1_, bf16[3,640,1024]{2,1,0:T(8,128)(2,1)} %constant_dynamic-update-slice_fusion.32.refs_2_.refs_4_, ...), custom_call_target="tpu_custom_call" | custom-call | tf_op jit(solution)/shard_map/ffn_forward/pallas_call | solution.py:185
  406.3 27.7 %ffn_backward.2 = (bf16[3,640,1024]{2,1,0:T(8,128)(2,1)}, bf16[3,640,1024]{2,1,0:T(8,128)(2,1)}, bf16[3,640,1024]{2,1,0:T(8,128)(2,1)}, bf16[3,640,1024]{2,1,0:T(8,128)(2,1)}, f32[512,960]{1,0:T(8,128)}) custom-call(f32[512,960]{1,0:T(8,128)} %bitcast.212, bf16[512,960]{1,0:T(8,128)(2,1)} %get-tuple-element.242.refs_1_, ...), custom_call_target="tpu_custom_call" | custom-call | tf_op jit(solution)/shard_map/ffn_backward/pallas_call | solution.py:267
  434.6 11.7 %collective-permute-start.44 = (bf16[256,960]{1,0:T(8,128)(2,1)}, bf16[256,960]{1,0:T(8,128)(2,1)S(1)}, u32[]{:S(2)}, u32[]{:S(2)}) collective-permute-start(bf16[256,960]{1,0:T(8,128)(2,1)} %select_convert_fusion.1), channel_id=1, source_target_pairs={{0,3},{1,2},{2,1},{3,0},{4,7},{5,6},{6,5},{7,4},{8,11},{9,10},{10,... | collective-permute-start | bytes 1474568 | tf_op jit(solution)/shard_map/ppermute | solution.py:437
  453.7 5.1 collective-permute-done.44
  459.6 4.1 add_convert_fusion.3
  468.4 4.1 add_convert_fusion.2
  478.6 29.2 %attention_backward.2 = (f32[512,960]{1,0:T(8,128)}, f32[1024,640]{1,0:T(8,128)}) custom-call(bf16[512,1280]{1,0:T(8,128)(2,1)} %get-tuple-element.227.q_ref, bf16[1024,640]{1,0:T(8,128)(2,1)} %pad_maximum_fusion.16.kv_ref, bf16[512,960]{1,0:T(8,128)(2,1)} %fusion.17.og_ref, f32[15,1,512]{2,1,0:T(1,128)} %get-tuple-element.256.lse_ref, ...), custom_call_target="tpu_custom_call" | custom-call | tf_op jit(solution)/shard_map/attention_backward/pallas_call | solution.py:407
  511.4 13.6 %collective-permute-done.45 = bf16[2,256,640]{2,1,0:T(8,128)(2,1)S(1)} collective-permute-done((bf16[2,256,640]{2,1,0:T(8,128)(2,1)S(1)}, bf16[2,256,640]{2,1,0:T(8,128)(2,1)S(1)}, u32[]{:S(2)}, u32[]{:S(2)}) %collective-permute-start.45) | collective-permute-done | bytes 655392 | tf_op jit(solution)/shard_map/ppermute | solution.py:437
  527.5 13.1 %qkv_backward.2 = (bf16[960,1280]{1,0:T(8,128)(2,1)}, bf16[960,1280]{1,0:T(8,128)(2,1)}, f32[1,960]{1,0:T(1,128)}, f32[512,960]{1,0:T(8,128)}) custom-call(f32[512,960]{1,0:T(8,128)} %get-tuple-element.257.dq_ref, f32[512,640]{1,0:T(8,128)} %bitcast.223, f32[512,960]{1,0:T(8,128)} %get-tuple-element.219.x_ref, ...), custom_call_target="tpu_custom_call" | custom-call | tf_op jit(solution)/shard_map/qkv_backward/pallas_call | solution.py:131
  541.5 3.7 add_convert_fusion.7
  547.5 2.7 concatenate.247
  553.0 4.6 reshape_reshape.6
  567.0 28.0 %ffn_backward.3 = (bf16[3,640,1024]{2,1,0:T(8,128)(2,1)}, bf16[3,640,1024]{2,1,0:T(8,128)(2,1)}, bf16[3,640,1024]{2,1,0:T(8,128)(2,1)}, bf16[3,640,1024]{2,1,0:T(8,128)(2,1)}, f32[512,960]{1,0:T(8,128)}) custom-call(f32[512,960]{1,0:T(8,128)} %get-tuple-element.268.refs_0_, bf16[512,960]{1,0:T(8,128)(2,1)} %get-tuple-element.270.refs_1_, ...), custom_call_target="tpu_custom_call" | custom-call | tf_op jit(solution)/shard_map/ffn_backward/pallas_call | solution.py:267
  595.1 2.7 add_convert_fusion.14
  618.7 9.5 %collective-permute-done.55 = bf16[2,1,1,4,30,1280]{5,3,4,2,1,0:T(4,128)(2,1)S(1)} collective-permute-done((bf16[2,1,1,4,30,1280]{5,3,4,2,1,0:T(4,128)(2,1)S(1)}, bf16[2,1,1,4,30,1280]{5,3,4,2,1,0:T(4,128)(2,1)S(1)}, u32[]{:S(2)}, u32[]{:S(2)}) %collective-permute-start.55) | collective-permute-done | bytes 614432 | tf_op jit(solution)/shard_map/ppermute | solution.py:437
  634.2 4.1 add_convert_fusion.1
  642.6 4.1 add_convert_fusion
  649.3 29.8 %attention_backward.3 = (f32[512,960]{1,0:T(8,128)}, f32[1024,640]{1,0:T(8,128)}) custom-call(bf16[512,1280]{1,0:T(8,128)(2,1)} %get-tuple-element.196.q_ref, bf16[1024,640]{1,0:T(8,128)(2,1)} %pad_maximum_fusion.13.kv_ref, bf16[512,960]{1,0:T(8,128)(2,1)} %fusion.14.og_ref, f32[15,1,512]{2,1,0:T(1,128)} %get-tuple-element.289.lse_ref, ...), custom_call_target="tpu_custom_call" | custom-call | tf_op jit(solution)/shard_map/attention_backward/pallas_call | solution.py:407
  689.5 10.9 %collective-permute-done.61 = bf16[2,256,640]{2,1,0:T(8,128)(2,1)S(1)} collective-permute-done((bf16[2,256,640]{2,1,0:T(8,128)(2,1)S(1)}, bf16[2,256,640]{2,1,0:T(8,128)(2,1)S(1)}, u32[]{:S(2)}, u32[]{:S(2)}) %collective-permute-start.61) | collective-permute-done | bytes 655392 | tf_op jit(solution)/shard_map/ppermute | solution.py:437
  700.4 4.0 collective-permute-start.73
  705.5 13.0 %qkv_backward.3 = (bf16[960,1280]{1,0:T(8,128)(2,1)}, bf16[960,1280]{1,0:T(8,128)(2,1)}, f32[1,960]{1,0:T(1,128)}, f32[512,960]{1,0:T(8,128)}) custom-call(f32[512,960]{1,0:T(8,128)} %get-tuple-element.296.dq_ref, f32[512,640]{1,0:T(8,128)} %bitcast.222, f32[512,960]{1,0:T(8,128)} %bitcast.214, bf16[512,960]{1,0:T(8,128)(2,1)} %get-tuple-element.298.normed_ref, ...), custom_call_target="tpu_custom_call" | custom-call | tf_op jit(solution)/shard_map/qkv_backward/pallas_call | solution.py:131
  725.6 4.4 add_convert_fusion.4
  729.9 2.7 concatenate.256
  732.7 4.3 reshape_reshape.7
  756.8 2.8 copy.132
  763.2 3.8 stack_reshape.23
  769.1 4.7 collective-permute-done.65
  786.0 5.1 collective-permute-start.79
  801.4 5.7 collective-permute-done.76
  817.3 15.3 %collective-permute-done.80 = bf16[3,80,1024]{2,1,0:T(8,128)(2,1)} collective-permute-done((bf16[3,80,1024]{2,1,0:T(8,128)(2,1)}, bf16[3,80,1024]{2,1,0:T(8,128)(2,1)}, u32[]{:S(2)}, u32[]{:S(2)}) %collective-permute-start.80) | collective-permute-done | bytes 491552 | tf_op jit(solution)/shard_map/ppermute | solution.py:437
  837.2 9.4 %collective-permute-start.82 = (bf16[31,1280]{1,0:T(8,128)(2,1)}, bf16[31,1280]{1,0:T(8,128)(2,1)}, u32[]{:S(2)}, u32[]{:S(2)}) collective-permute-start(bf16[31,1280]{1,0:T(8,128)(2,1)} %get-tuple-element.510), channel_id=1, source_target_pairs={{0,1},{1,0},{2,3},{3,2},{4,5},{5,4},{6,7},{7,6},{8,9},{9,8},{10,11... | collective-permute-start | bytes 238088 | tf_op jit(solution)/shard_map/ppermute | solution.py:437
  (599 shorter events, 328.1 us)
Async XLA Ops:
  8.1 16.5 %collective-permute-start.2 = (bf16[31,2560]{1,0:T(8,128)(2,1)S(1)}, bf16[31,2560]{1,0:T(8,128)(2,1)S(1)}, u32[]{:S(2)}, u32[]{:S(2)}) collective-permute-start(bf16[31,2560]{1,0:T(8,128)(2,1)S(1)} %fusion.49), channel_id=1, source_target_pairs={{0,3},{1,2},{2,1},{3,0},{4,7},{5,6},{6,5},{7,4},{8,11},{9,10},{10,... | collective-permute-start | bytes 476168 | tf_op jit(solution)/shard_map/ppermute | solution.py:437
  29.2 16.2 %collective-permute-start.4 = (bf16[1,1,1,4,31,1280]{5,4,3,2,1,0:T(8,128)(2,1)}, bf16[1,1,1,4,31,1280]{5,4,3,2,1,0:T(8,128)(2,1)}, u32[]{:S(2)}, u32[]{:S(2)}) collective-permute-start(bf16[1,1,1,4,31,1280]{5,4,3,2,1,0:T(8,128)(2,1)} %maximum_bitcast_fusion), channel_id=1, source_target_pairs={{0,8},{1,9},{2,10},{3,11},{4,12},{5,13},{6,14},{7,15},{8,0},{9,1},... | collective-permute-start | bytes 952328 | tf_op jit(solution)/shard_map/ppermute | solution.py:437
  48.7 17.6 %collective-permute-start.7 = (bf16[2,1,1,4,31,1280]{5,3,4,2,1,0:T(4,128)(2,1)}, bf16[2,1,1,4,31,1280]{5,3,4,2,1,0:T(4,128)(2,1)}, u32[]{:S(2)}, u32[]{:S(2)}) collective-permute-start(bf16[2,1,1,4,31,1280]{5,3,4,2,1,0:T(4,128)(2,1)} %copy.65), channel_id=1, source_target_pairs={{0,8},{1,9},{2,10},{3,11},{4,12},{5,13},{6,14},{7,15},{8,0},{9,1},... | collective-permute-start | bytes 1904648 | tf_op jit(solution)/shard_map/ppermute | solution.py:437
  72.6 21.0 %collective-permute-start.10 = (bf16[2,2,1,4,31,1280]{5,3,4,2,1,0:T(4,128)(2,1)}, bf16[2,2,1,4,31,1280]{5,3,4,2,1,0:T(4,128)(2,1)}, u32[]{:S(2)}, u32[]{:S(2)}) collective-permute-start(bf16[2,2,1,4,31,1280]{5,3,4,2,1,0:T(4,128)(2,1)} %copy.71), channel_id=1, source_target_pairs={{0,4},{1,5},{2,6},{3,7},{4,0},{5,1},{6,2},{7,3},{8,12},{9,13},{10,... | collective-permute-start | bytes 3809288 | tf_op jit(solution)/shard_map/ppermute | solution.py:437
  74.8 18.8 %collective-permute-start.9 = (bf16[2,2,1,4,31,1280]{5,3,4,2,1,0:T(4,128)(2,1)}, bf16[2,2,1,4,31,1280]{5,3,4,2,1,0:T(4,128)(2,1)}, u32[]{:S(2)}, u32[]{:S(2)}) collective-permute-start(bf16[2,2,1,4,31,1280]{5,3,4,2,1,0:T(4,128)(2,1)} %copy.68), channel_id=1, source_target_pairs={{0,4},{1,5},{2,6},{3,7},{4,0},{5,1},{6,2},{7,3},{8,12},{9,13},{10,... | collective-permute-start | bytes 3809288 | tf_op jit(solution)/shard_map/ppermute | solution.py:437
  77.7 42.0 %collective-permute-start.13 = (bf16[3,80,1024]{2,1,0:T(8,128)(2,1)}, bf16[3,80,1024]{2,1,0:T(8,128)(2,1)}, u32[]{:S(2)}, u32[]{:S(2)}) collective-permute-start(bf16[3,80,1024]{2,1,0:T(8,128)(2,1)} %pad_bitcast_fusion.1), channel_id=1, source_target_pairs={{0,3},{1,2},{2,1},{3,0},{4,7},{5,6},{6,5},{7,4},{8,11},{9,10},{10,... | collective-permute-start | bytes 1474568 | tf_op jit(solution)/shard_map/ppermute | solution.py:437
  80.0 44.6 %collective-permute-start.12 = (bf16[3,80,1024]{2,1,0:T(8,128)(2,1)}, bf16[3,80,1024]{2,1,0:T(8,128)(2,1)}, u32[]{:S(2)}, u32[]{:S(2)}) collective-permute-start(bf16[3,80,1024]{2,1,0:T(8,128)(2,1)} %pad_bitcast_fusion.1), channel_id=1, source_target_pairs={{0,2},{1,3},{2,0},{3,1},{4,6},{5,7},{6,4},{7,5},{8,10},{9,11},{10,... | collective-permute-start | bytes 1474568 | tf_op jit(solution)/shard_map/ppermute | solution.py:437
  88.5 36.1 %collective-permute-start.11 = (bf16[3,80,1024]{2,1,0:T(8,128)(2,1)}, bf16[3,80,1024]{2,1,0:T(8,128)(2,1)}, u32[]{:S(2)}, u32[]{:S(2)}) collective-permute-start(bf16[3,80,1024]{2,1,0:T(8,128)(2,1)} %pad_bitcast_fusion.1), channel_id=1, source_target_pairs={{0,1},{1,0},{2,3},{3,2},{4,5},{5,4},{6,7},{7,6},{8,9},{9,8},{10,11... | collective-permute-start | bytes 1474568 | tf_op jit(solution)/shard_map/ppermute | solution.py:437
  127.9 17.0 %collective-permute-start.14 = (bf16[2,256,640]{2,1,0:T(8,128)(2,1)}, bf16[2,256,640]{2,1,0:T(8,128)(2,1)}, u32[]{:S(2)}, u32[]{:S(2)}) collective-permute-start(bf16[2,256,640]{2,1,0:T(8,128)(2,1)} %bitcast.27), channel_id=1, source_target_pairs={{0,1},{1,0},{2,3},{3,2},{4,5},{5,4},{6,7},{7,6},{8,9},{9,8},{10,11... | collective-permute-start | bytes 1966088 | tf_op jit(solution)/shard_map/ppermute | solution.py:437
  134.5 23.7 %collective-permute-start.15 = (bf16[3,160,1024]{2,1,0:T(8,128)(2,1)S(1)}, bf16[3,160,1024]{2,1,0:T(8,128)(2,1)S(1)}, u32[]{:S(2)}, u32[]{:S(2)}) collective-permute-start(bf16[3,160,1024]{2,1,0:T(8,128)(2,1)S(1)} %pad_maximum_fusion.17), channel_id=1, source_target_pairs={{0,8},{1,9},{2,10},{3,11},{4,12},{5,13},{6,14},{7,15},{8,0},{9,1},... | collective-permute-start | bytes 2949128 | tf_op jit(solution)/shard_map/ppermute | solution.py:437
  137.1 23.7 %collective-permute-start.16 = (bf16[3,160,1024]{2,1,0:T(8,128)(2,1)}, bf16[3,160,1024]{2,1,0:T(8,128)(2,1)}, u32[]{:S(2)}, u32[]{:S(2)}) collective-permute-start(bf16[3,160,1024]{2,1,0:T(8,128)(2,1)} %pad_maximum_fusion.18), channel_id=1, source_target_pairs={{0,16},{1,17},{2,18},{3,19},{4,20},{5,21},{6,22},{7,23},{8,24},{9,... | collective-permute-start | bytes 2949128 | tf_op jit(solution)/shard_map/ppermute | solution.py:437
  163.6 43.9 %collective-permute-start.22 = (bf16[3,320,1024]{2,1,0:T(8,128)(2,1)}, bf16[3,320,1024]{2,1,0:T(8,128)(2,1)}, u32[]{:S(2)}, u32[]{:S(2)}) collective-permute-start(bf16[3,320,1024]{2,1,0:T(8,128)(2,1)} %get-tuple-element.431), channel_id=1, source_target_pairs={{0,8},{1,9},{2,10},{3,11},{4,12},{5,13},{6,14},{7,15},{8,0},{9,1},... | collective-permute-start | bytes 5898248 | tf_op jit(solution)/shard_map/ppermute | solution.py:437
  165.6 43.6 %collective-permute-start.21 = (bf16[3,320,1024]{2,1,0:T(8,128)(2,1)}, bf16[3,320,1024]{2,1,0:T(8,128)(2,1)}, u32[]{:S(2)}, u32[]{:S(2)}) collective-permute-start(bf16[3,320,1024]{2,1,0:T(8,128)(2,1)} %get-tuple-element.433), channel_id=1, source_target_pairs={{0,16},{1,17},{2,18},{3,19},{4,20},{5,21},{6,22},{7,23},{8,24},{9,... | collective-permute-start | bytes 5898248 | tf_op jit(solution)/shard_map/ppermute | solution.py:437
  173.4 29.1 %collective-permute-start.20 = (bf16[31,2560]{1,0:T(8,128)(2,1)S(1)}, bf16[31,2560]{1,0:T(8,128)(2,1)S(1)}, u32[]{:S(2)}, u32[]{:S(2)}) collective-permute-start(bf16[31,2560]{1,0:T(8,128)(2,1)S(1)} %fusion.47), channel_id=1, source_target_pairs={{0,3},{1,2},{2,1},{3,0},{4,7},{5,6},{6,5},{7,4},{8,11},{9,10},{10,... | collective-permute-start | bytes 476168 | tf_op jit(solution)/shard_map/ppermute | solution.py:437
  175.6 26.8 %collective-permute-start.19 = (bf16[31,2560]{1,0:T(8,128)(2,1)S(1)}, bf16[31,2560]{1,0:T(8,128)(2,1)S(1)}, u32[]{:S(2)}, u32[]{:S(2)}) collective-permute-start(bf16[31,2560]{1,0:T(8,128)(2,1)S(1)} %fusion.47), channel_id=1, source_target_pairs={{0,2},{1,3},{2,0},{3,1},{4,6},{5,7},{6,4},{7,5},{8,10},{9,11},{10,... | collective-permute-start | bytes 476168 | tf_op jit(solution)/shard_map/ppermute | solution.py:437
  176.6 25.9 %collective-permute-start.18 = (bf16[31,2560]{1,0:T(8,128)(2,1)S(1)}, bf16[31,2560]{1,0:T(8,128)(2,1)S(1)}, u32[]{:S(2)}, u32[]{:S(2)}) collective-permute-start(bf16[31,2560]{1,0:T(8,128)(2,1)S(1)} %fusion.47), channel_id=1, source_target_pairs={{0,1},{1,0},{2,3},{3,2},{4,5},{5,4},{6,7},{7,6},{8,9},{9,8},{10,11... | collective-permute-start | bytes 476168 | tf_op jit(solution)/shard_map/ppermute | solution.py:437
  230.5 47.4 %collective-permute-start.28 = (bf16[2,1,1,4,31,1280]{5,3,4,2,1,0:T(4,128)(2,1)}, bf16[2,1,1,4,31,1280]{5,3,4,2,1,0:T(4,128)(2,1)}, u32[]{:S(2)}, u32[]{:S(2)}) collective-permute-start(bf16[2,1,1,4,31,1280]{5,3,4,2,1,0:T(4,128)(2,1)} %copy.83), channel_id=1, source_target_pairs={{0,8},{1,9},{2,10},{3,11},{4,12},{5,13},{6,14},{7,15},{8,0},{9,1},... | collective-permute-start | bytes 1904648 | tf_op jit(solution)/shard_map/ppermute | solution.py:437
  232.4 45.4 %collective-permute-start.27 = (bf16[1,2,1,4,31,1280]{5,3,4,2,1,0:T(4,128)(2,1)}, bf16[1,2,1,4,31,1280]{5,3,4,2,1,0:T(4,128)(2,1)}, u32[]{:S(2)}, u32[]{:S(2)}) collective-permute-start(bf16[1,2,1,4,31,1280]{5,3,4,2,1,0:T(4,128)(2,1)} %copy.82), channel_id=1, source_target_pairs={{0,16},{1,17},{2,18},{3,19},{4,20},{5,21},{6,22},{7,23},{8,24},{9,... | collective-permute-start | bytes 1904648 | tf_op jit(solution)/shard_map/ppermute | solution.py:437
  233.7 23.7 %collective-permute-start.31 = (bf16[3,80,1024]{2,1,0:T(8,128)(2,1)}, bf16[3,80,1024]{2,1,0:T(8,128)(2,1)}, u32[]{:S(2)}, u32[]{:S(2)}) collective-permute-start(bf16[3,80,1024]{2,1,0:T(8,128)(2,1)} %pad_bitcast_fusion), channel_id=1, source_target_pairs={{0,3},{1,2},{2,1},{3,0},{4,7},{5,6},{6,5},{7,4},{8,11},{9,10},{10,... | collective-permute-start | bytes 1474568 | tf_op jit(solution)/shard_map/ppermute | solution.py:437
  236.0 41.9 %collective-permute-start.30 = (bf16[3,80,1024]{2,1,0:T(8,128)(2,1)}, bf16[3,80,1024]{2,1,0:T(8,128)(2,1)}, u32[]{:S(2)}, u32[]{:S(2)}) collective-permute-start(bf16[3,80,1024]{2,1,0:T(8,128)(2,1)} %pad_bitcast_fusion), channel_id=1, source_target_pairs={{0,2},{1,3},{2,0},{3,1},{4,6},{5,7},{6,4},{7,5},{8,10},{9,11},{10,... | collective-permute-start | bytes 1474568 | tf_op jit(solution)/shard_map/ppermute | solution.py:437
  236.6 41.3 %collective-permute-start.29 = (bf16[3,80,1024]{2,1,0:T(8,128)(2,1)}, bf16[3,80,1024]{2,1,0:T(8,128)(2,1)}, u32[]{:S(2)}, u32[]{:S(2)}) collective-permute-start(bf16[3,80,1024]{2,1,0:T(8,128)(2,1)} %pad_bitcast_fusion), channel_id=1, source_target_pairs={{0,1},{1,0},{2,3},{3,2},{4,5},{5,4},{6,7},{7,6},{8,9},{9,8},{10,11... | collective-permute-start | bytes 1474568 | tf_op jit(solution)/shard_map/ppermute | solution.py:437
  293.9 24.5 %collective-permute-start.34 = (bf16[3,160,1024]{2,1,0:T(8,128)(2,1)}, bf16[3,160,1024]{2,1,0:T(8,128)(2,1)}, u32[]{:S(2)}, u32[]{:S(2)}) collective-permute-start(bf16[3,160,1024]{2,1,0:T(8,128)(2,1)} %pad_maximum_fusion.19), channel_id=1, source_target_pairs={{0,8},{1,9},{2,10},{3,11},{4,12},{5,13},{6,14},{7,15},{8,0},{9,1},... | collective-permute-start | bytes 2949128 | tf_op jit(solution)/shard_map/ppermute | solution.py:437
  296.5 23.7 %collective-permute-start.35 = (bf16[3,160,1024]{2,1,0:T(8,128)(2,1)}, bf16[3,160,1024]{2,1,0:T(8,128)(2,1)}, u32[]{:S(2)}, u32[]{:S(2)}) collective-permute-start(bf16[3,160,1024]{2,1,0:T(8,128)(2,1)} %pad_maximum_fusion.20), channel_id=1, source_target_pairs={{0,16},{1,17},{2,18},{3,19},{4,20},{5,21},{6,22},{7,23},{8,24},{9,... | collective-permute-start | bytes 2949128 | tf_op jit(solution)/shard_map/ppermute | solution.py:437
  322.9 48.0 %collective-permute-start.38 = (bf16[3,320,1024]{2,1,0:T(8,128)(2,1)}, bf16[3,320,1024]{2,1,0:T(8,128)(2,1)S(1)}, u32[]{:S(2)}, u32[]{:S(2)}) collective-permute-start(bf16[3,320,1024]{2,1,0:T(8,128)(2,1)} %get-tuple-element.427), channel_id=1, source_target_pairs={{0,8},{1,9},{2,10},{3,11},{4,12},{5,13},{6,14},{7,15},{8,0},{9,1},... | collective-permute-start | bytes 5898248 | tf_op jit(solution)/shard_map/ppermute | solution.py:437
  326.2 44.7 %collective-permute-start.37 = (bf16[3,320,1024]{2,1,0:T(8,128)(2,1)}, bf16[3,320,1024]{2,1,0:T(8,128)(2,1)}, u32[]{:S(2)}, u32[]{:S(2)}) collective-permute-start(bf16[3,320,1024]{2,1,0:T(8,128)(2,1)} %get-tuple-element.429), channel_id=1, source_target_pairs={{0,16},{1,17},{2,18},{3,19},{4,20},{5,21},{6,22},{7,23},{8,24},{9,... | collective-permute-start | bytes 5898248 | tf_op jit(solution)/shard_map/ppermute | solution.py:437
  328.4 16.9 %collective-permute-start.36 = (bf16[2,256,640]{2,1,0:T(8,128)(2,1)S(1)}, bf16[2,256,640]{2,1,0:T(8,128)(2,1)S(1)}, u32[]{:S(2)}, u32[]{:S(2)}) collective-permute-start(bf16[2,256,640]{2,1,0:T(8,128)(2,1)S(1)} %bitcast.230), channel_id=1, source_target_pairs={{0,1},{1,0},{2,3},{3,2},{4,5},{5,4},{6,7},{7,6},{8,9},{9,8},{10,11... | collective-permute-start | bytes 1966088 | tf_op jit(solution)/shard_map/ppermute | solution.py:437
  328.5 42.4 %collective-permute-start.39 = (bf16[256,960]{1,0:T(8,128)(2,1)S(1)}, bf16[256,960]{1,0:T(8,128)(2,1)S(1)}, u32[]{:S(2)}, u32[]{:S(2)}) collective-permute-start(bf16[256,960]{1,0:T(8,128)(2,1)S(1)} %copy-done.86), channel_id=1, source_target_pairs={{0,3},{1,2},{2,1},{3,0},{4,7},{5,6},{6,5},{7,4},{8,11},{9,10},{10,... | collective-permute-start | bytes 1474568 | tf_op jit(solution)/shard_map/ppermute | solution.py:437
  433.9 24.9 %collective-permute-start.42 = (bf16[3,640,1024]{2,1,0:T(8,128)(2,1)}, bf16[3,640,1024]{2,1,0:T(8,128)(2,1)}, u32[]{:S(2)}, u32[]{:S(2)}) collective-permute-start(bf16[3,640,1024]{2,1,0:T(8,128)(2,1)} %get-tuple-element.251), channel_id=1, source_target_pairs={{0,4},{1,5},{2,6},{3,7},{4,0},{5,1},{6,2},{7,3},{8,12},{9,13},{10,... | collective-permute-start | bytes 11796488 | tf_op jit(solution)/shard_map/ppermute | solution.py:437
  434.1 25.5 %collective-permute-start.43 = (bf16[3,640,1024]{2,1,0:T(8,128)(2,1)}, bf16[3,640,1024]{2,1,0:T(8,128)(2,1)}, u32[]{:S(2)}, u32[]{:S(2)}) collective-permute-start(bf16[3,640,1024]{2,1,0:T(8,128)(2,1)} %get-tuple-element.252), channel_id=1, source_target_pairs={{0,4},{1,5},{2,6},{3,7},{4,0},{5,1},{6,2},{7,3},{8,12},{9,13},{10,... | collective-permute-start | bytes 11796488 | tf_op jit(solution)/shard_map/ppermute | solution.py:437
  434.6 24.2 %collective-permute-start.44 = (bf16[256,960]{1,0:T(8,128)(2,1)}, bf16[256,960]{1,0:T(8,128)(2,1)S(1)}, u32[]{:S(2)}, u32[]{:S(2)}) collective-permute-start(bf16[256,960]{1,0:T(8,128)(2,1)} %select_convert_fusion.1), channel_id=1, source_target_pairs={{0,3},{1,2},{2,1},{3,0},{4,7},{5,6},{6,5},{7,4},{8,11},{9,10},{10,... | collective-permute-start | bytes 1474568 | tf_op jit(solution)/shard_map/ppermute | solution.py:437
  475.8 65.6 %collective-permute-start.47 = (bf16[3,320,1024]{2,1,0:T(8,128)(2,1)}, bf16[3,320,1024]{2,1,0:T(8,128)(2,1)S(1)}, u32[]{:S(2)}, u32[]{:S(2)}) collective-permute-start(bf16[3,320,1024]{2,1,0:T(8,128)(2,1)} %slice.625), channel_id=1, source_target_pairs={{0,8},{1,9},{2,10},{3,11},{4,12},{5,13},{6,14},{7,15},{8,0},{9,1},... | collective-permute-start | bytes 5898248 | tf_op jit(solution)/shard_map/ppermute | solution.py:437
  477.3 64.1 %collective-permute-start.46 = (bf16[3,320,1024]{2,1,0:T(8,128)(2,1)}, bf16[3,320,1024]{2,1,0:T(8,128)(2,1)}, u32[]{:S(2)}, u32[]{:S(2)}) collective-permute-start(bf16[3,320,1024]{2,1,0:T(8,128)(2,1)} %slice.624), channel_id=1, source_target_pairs={{0,16},{1,17},{2,18},{3,19},{4,20},{5,21},{6,22},{7,23},{8,24},{9,... | collective-permute-start | bytes 5898248 | tf_op jit(solution)/shard_map/ppermute | solution.py:437
  509.2 15.8 %collective-permute-start.45 = (bf16[2,256,640]{2,1,0:T(8,128)(2,1)S(1)}, bf16[2,256,640]{2,1,0:T(8,128)(2,1)S(1)}, u32[]{:S(2)}, u32[]{:S(2)}) collective-permute-start(bf16[2,256,640]{2,1,0:T(8,128)(2,1)S(1)} %fusion.32), channel_id=1, source_target_pairs={{0,1},{1,0},{2,3},{3,2},{4,5},{5,4},{6,7},{7,6},{8,9},{9,8},{10,11... | collective-permute-start | bytes 1966088 | tf_op jit(solution)/shard_map/ppermute | solution.py:437
  553.0 42.1 %collective-permute-start.50 = (bf16[2,2,1,4,31,1280]{5,3,4,2,1,0:T(4,128)(2,1)}, bf16[2,2,1,4,31,1280]{5,3,4,2,1,0:T(4,128)(2,1)}, u32[]{:S(2)}, u32[]{:S(2)}) collective-permute-start(bf16[2,2,1,4,31,1280]{5,3,4,2,1,0:T(4,128)(2,1)} %copy.107), channel_id=1, source_target_pairs={{0,4},{1,5},{2,6},{3,7},{4,0},{5,1},{6,2},{7,3},{8,12},{9,13},{10,... | collective-permute-start | bytes 3809288 | tf_op jit(solution)/shard_map/ppermute | solution.py:437
  561.7 33.4 %collective-permute-start.51 = (bf16[2,2,1,4,30,1280]{5,3,4,2,1,0:T(4,128)(2,1)}, bf16[2,2,1,4,30,1280]{5,3,4,2,1,0:T(4,128)(2,1)}, u32[]{:S(2)}, u32[]{:S(2)}) collective-permute-start(bf16[2,2,1,4,30,1280]{5,3,4,2,1,0:T(4,128)(2,1)} %copy.108), channel_id=1, source_target_pairs={{0,4},{1,5},{2,6},{3,7},{4,0},{5,1},{6,2},{7,3},{8,12},{9,13},{10,... | collective-permute-start | bytes 3686408 | tf_op jit(solution)/shard_map/ppermute | solution.py:437
  565.4 29.6 %collective-permute-start.49 = (bf16[3,160,1024]{2,1,0:T(8,128)(2,1)}, bf16[3,160,1024]{2,1,0:T(8,128)(2,1)}, u32[]{:S(2)}, u32[]{:S(2)}) collective-permute-start(bf16[3,160,1024]{2,1,0:T(8,128)(2,1)} %slice.629), channel_id=1, source_target_pairs={{0,16},{1,17},{2,18},{3,19},{4,20},{5,21},{6,22},{7,23},{8,24},{9,... | collective-permute-start | bytes 2949128 | tf_op jit(solution)/shard_map/ppermute | solution.py:437
  566.1 28.9 %collective-permute-start.48 = (bf16[3,160,1024]{2,1,0:T(8,128)(2,1)}, bf16[3,160,1024]{2,1,0:T(8,128)(2,1)}, u32[]{:S(2)}, u32[]{:S(2)}) collective-permute-start(bf16[3,160,1024]{2,1,0:T(8,128)(2,1)} %slice.627), channel_id=1, source_target_pairs={{0,8},{1,9},{2,10},{3,11},{4,12},{5,13},{6,14},{7,15},{8,0},{9,1},... | collective-permute-start | bytes 2949128 | tf_op jit(solution)/shard_map/ppermute | solution.py:437
  599.5 31.3 %collective-permute-start.52 = (bf16[3,640,1024]{2,1,0:T(8,128)(2,1)}, bf16[3,640,1024]{2,1,0:T(8,128)(2,1)}, u32[]{:S(2)}, u32[]{:S(2)}) collective-permute-start(bf16[3,640,1024]{2,1,0:T(8,128)(2,1)} %get-tuple-element.284), channel_id=1, source_target_pairs={{0,4},{1,5},{2,6},{3,7},{4,0},{5,1},{6,2},{7,3},{8,12},{9,13},{10,... | collective-permute-start | bytes 11796488 | tf_op jit(solution)/shard_map/ppermute | solution.py:437
  599.6 31.2 %collective-permute-start.53 = (bf16[3,640,1024]{2,1,0:T(8,128)(2,1)}, bf16[3,640,1024]{2,1,0:T(8,128)(2,1)}, u32[]{:S(2)}, u32[]{:S(2)}) collective-permute-start(bf16[3,640,1024]{2,1,0:T(8,128)(2,1)} %get-tuple-element.285), channel_id=1, source_target_pairs={{0,4},{1,5},{2,6},{3,7},{4,0},{5,1},{6,2},{7,3},{8,12},{9,13},{10,... | collective-permute-start | bytes 11796488 | tf_op jit(solution)/shard_map/ppermute | solution.py:437
  604.5 74.6 %collective-permute-start.56 = (bf16[3,80,1024]{2,1,0:T(8,128)(2,1)}, bf16[3,80,1024]{2,1,0:T(8,128)(2,1)}, u32[]{:S(2)}, u32[]{:S(2)}) collective-permute-start(bf16[3,80,1024]{2,1,0:T(8,128)(2,1)} %pad_maximum_fusion.29), channel_id=1, source_target_pairs={{0,1},{1,0},{2,3},{3,2},{4,5},{5,4},{6,7},{7,6},{8,9},{9,8},{10,11... | collective-permute-start | bytes 1474568 | tf_op jit(solution)/shard_map/ppermute | solution.py:437
  608.9 21.2 %collective-permute-start.54 = (bf16[1,2,1,4,31,1280]{5,3,4,2,1,0:T(4,128)(2,1)S(1)}, bf16[1,2,1,4,31,1280]{5,3,4,2,1,0:T(4,128)(2,1)S(1)}, u32[]{:S(2)}, u32[]{:S(2)}) collective-permute-start(bf16[1,2,1,4,31,1280]{5,3,4,2,1,0:T(4,128)(2,1)S(1)} %copy.111), channel_id=1, source_target_pairs={{0,16},{1,17},{2,18},{3,19},{4,20},{5,21},{6,22},{7,23},{8,24},{9,... | collective-permute-start | bytes 1904648 | tf_op jit(solution)/shard_map/ppermute | solution.py:437
  628.2 51.4 %collective-permute-start.57 = (bf16[3,80,1024]{2,1,0:T(8,128)(2,1)S(1)}, bf16[3,80,1024]{2,1,0:T(8,128)(2,1)S(1)}, u32[]{:S(2)}, u32[]{:S(2)}) collective-permute-start(bf16[3,80,1024]{2,1,0:T(8,128)(2,1)S(1)} %pad_maximum_fusion.30), channel_id=1, source_target_pairs={{0,2},{1,3},{2,0},{3,1},{4,6},{5,7},{6,4},{7,5},{8,10},{9,11},{10,... | collective-permute-start | bytes 1474568 | tf_op jit(solution)/shard_map/ppermute | solution.py:437
  630.1 50.7 %collective-permute-start.58 = (bf16[3,80,1024]{2,1,0:T(8,128)(2,1)S(1)}, bf16[3,80,1024]{2,1,0:T(8,128)(2,1)S(1)}, u32[]{:S(2)}, u32[]{:S(2)}) collective-permute-start(bf16[3,80,1024]{2,1,0:T(8,128)(2,1)S(1)} %pad_maximum_fusion.31), channel_id=1, source_target_pairs={{0,3},{1,2},{2,1},{3,0},{4,7},{5,6},{6,5},{7,4},{8,11},{9,10},{10,... | collective-permute-start | bytes 1474568 | tf_op jit(solution)/shard_map/ppermute | solution.py:437
  631.3 49.5 %collective-permute-start.60 = (bf16[1,1,1,4,30,1280]{5,4,3,2,1,0:T(8,128)(2,1)S(1)}, bf16[1,1,1,4,30,1280]{5,4,3,2,1,0:T(8,128)(2,1)S(1)}, u32[]{:S(2)}, u32[]{:S(2)}) collective-permute-start(bf16[1,1,1,4,30,1280]{5,4,3,2,1,0:T(8,128)(2,1)S(1)} %broadcast_select_fusion.27), channel_id=1, source_target_pairs={{0,16},{1,17},{2,18},{3,19},{4,20},{5,21},{6,22},{7,23},{8,24},{9,... | collective-permute-start | bytes 921608 | tf_op jit(solution)/shard_map/ppermute | solution.py:437
  632.7 48.1 %collective-permute-start.59 = (bf16[1,1,1,4,31,1280]{5,4,3,2,1,0:T(8,128)(2,1)S(1)}, bf16[1,1,1,4,31,1280]{5,4,3,2,1,0:T(8,128)(2,1)S(1)}, u32[]{:S(2)}, u32[]{:S(2)}) collective-permute-start(bf16[1,1,1,4,31,1280]{5,4,3,2,1,0:T(8,128)(2,1)S(1)} %broadcast_select_fusion.33), channel_id=1, source_target_pairs={{0,8},{1,9},{2,10},{3,11},{4,12},{5,13},{6,14},{7,15},{8,0},{9,1},... | collective-permute-start | bytes 952328 | tf_op jit(solution)/shard_map/ppermute | solution.py:437
  679.0 42.8 %collective-permute-start.63 = (bf16[3,320,1024]{2,1,0:T(8,128)(2,1)}, bf16[3,320,1024]{2,1,0:T(8,128)(2,1)}, u32[]{:S(2)}, u32[]{:S(2)}) collective-permute-start(bf16[3,320,1024]{2,1,0:T(8,128)(2,1)} %slice.641), channel_id=1, source_target_pairs={{0,8},{1,9},{2,10},{3,11},{4,12},{5,13},{6,14},{7,15},{8,0},{9,1},... | collective-permute-start | bytes 5898248 | tf_op jit(solution)/shard_map/ppermute | solution.py:437
  679.6 43.4 %collective-permute-start.62 = (bf16[3,320,1024]{2,1,0:T(8,128)(2,1)}, bf16[3,320,1024]{2,1,0:T(8,128)(2,1)S(1)}, u32[]{:S(2)}, u32[]{:S(2)}) collective-permute-start(bf16[3,320,1024]{2,1,0:T(8,128)(2,1)} %slice.640), channel_id=1, source_target_pairs={{0,16},{1,17},{2,18},{3,19},{4,20},{5,21},{6,22},{7,23},{8,24},{9,... | collective-permute-start | bytes 5898248 | tf_op jit(solution)/shard_map/ppermute | solution.py:437
  683.2 17.1 %collective-permute-start.61 = (bf16[2,256,640]{2,1,0:T(8,128)(2,1)S(1)}, bf16[2,256,640]{2,1,0:T(8,128)(2,1)S(1)}, u32[]{:S(2)}, u32[]{:S(2)}) collective-permute-start(bf16[2,256,640]{2,1,0:T(8,128)(2,1)S(1)} %fusion.33), channel_id=1, source_target_pairs={{0,1},{1,0},{2,3},{3,2},{4,5},{5,4},{6,7},{7,6},{8,9},{9,8},{10,11... | collective-permute-start | bytes 1966088 | tf_op jit(solution)/shard_map/ppermute | solution.py:437
  686.0 64.0 %collective-permute-start.70 = (bf16[31,1280]{1,0:T(8,128)(2,1)}, bf16[31,1280]{1,0:T(8,128)(2,1)}, u32[]{:S(2)}, u32[]{:S(2)}) collective-permute-start(bf16[31,1280]{1,0:T(8,128)(2,1)} %get-tuple-element.515), channel_id=1, source_target_pairs={{0,3},{1,2},{2,1},{3,0},{4,7},{5,6},{6,5},{7,4},{8,11},{9,10},{10,... | collective-permute-start | bytes 238088 | tf_op jit(solution)/shard_map/ppermute | solution.py:437
  688.3 62.5 %collective-permute-start.69 = (bf16[31,1280]{1,0:T(8,128)(2,1)}, bf16[31,1280]{1,0:T(8,128)(2,1)}, u32[]{:S(2)}, u32[]{:S(2)}) collective-permute-start(bf16[31,1280]{1,0:T(8,128)(2,1)} %get-tuple-element.516), channel_id=1, source_target_pairs={{0,2},{1,3},{2,0},{3,1},{4,6},{5,7},{6,4},{7,5},{8,10},{9,11},{10,... | collective-permute-start | bytes 238088 | tf_op jit(solution)/shard_map/ppermute | solution.py:437
  700.4 43.2 %collective-permute-start.73 = (bf16[30,1280]{1,0:T(8,128)(2,1)}, bf16[30,1280]{1,0:T(8,128)(2,1)}, u32[]{:S(2)}, u32[]{:S(2)}) collective-permute-start(bf16[30,1280]{1,0:T(8,128)(2,1)} %get-tuple-element.512), channel_id=1, source_target_pairs={{0,3},{1,2},{2,1},{3,0},{4,7},{5,6},{6,5},{7,4},{8,11},{9,10},{10,... | collective-permute-start | bytes 230408 | tf_op jit(solution)/shard_map/ppermute | solution.py:437
  721.9 21.7 %collective-permute-start.72 = (bf16[30,1280]{1,0:T(8,128)(2,1)}, bf16[30,1280]{1,0:T(8,128)(2,1)}, u32[]{:S(2)}, u32[]{:S(2)}) collective-permute-start(bf16[30,1280]{1,0:T(8,128)(2,1)} %get-tuple-element.513), channel_id=1, source_target_pairs={{0,2},{1,3},{2,0},{3,1},{4,6},{5,7},{6,4},{7,5},{8,10},{9,11},{10,... | collective-permute-start | bytes 230408 | tf_op jit(solution)/shard_map/ppermute | solution.py:437
  723.0 25.8 %collective-permute-start.71 = (bf16[30,1280]{1,0:T(8,128)(2,1)}, bf16[30,1280]{1,0:T(8,128)(2,1)}, u32[]{:S(2)}, u32[]{:S(2)}) collective-permute-start(bf16[30,1280]{1,0:T(8,128)(2,1)} %get-tuple-element.514), channel_id=1, source_target_pairs={{0,1},{1,0},{2,3},{3,2},{4,5},{5,4},{6,7},{7,6},{8,9},{9,8},{10,11... | collective-permute-start | bytes 230408 | tf_op jit(solution)/shard_map/ppermute | solution.py:437
  743.6 30.7 %collective-permute-start.66 = (bf16[2,2,1,4,31,1280]{5,3,4,2,1,0:T(4,128)(2,1)}, bf16[2,2,1,4,31,1280]{5,3,4,2,1,0:T(4,128)(2,1)}, u32[]{:S(2)}, u32[]{:S(2)}) collective-permute-start(bf16[2,2,1,4,31,1280]{5,3,4,2,1,0:T(4,128)(2,1)} %copy.122), channel_id=1, source_target_pairs={{0,4},{1,5},{2,6},{3,7},{4,0},{5,1},{6,2},{7,3},{8,12},{9,13},{10,... | collective-permute-start | bytes 3809288 | tf_op jit(solution)/shard_map/ppermute | solution.py:437
  743.6 30.7 %collective-permute-start.67 = (bf16[2,2,1,4,30,1280]{5,3,4,2,1,0:T(4,128)(2,1)}, bf16[2,2,1,4,30,1280]{5,3,4,2,1,0:T(4,128)(2,1)}, u32[]{:S(2)}, u32[]{:S(2)}) collective-permute-start(bf16[2,2,1,4,30,1280]{5,3,4,2,1,0:T(4,128)(2,1)} %copy.123), channel_id=1, source_target_pairs={{0,4},{1,5},{2,6},{3,7},{4,0},{5,1},{6,2},{7,3},{8,12},{9,13},{10,... | collective-permute-start | bytes 3686408 | tf_op jit(solution)/shard_map/ppermute | solution.py:437
  750.0 23.8 %collective-permute-start.65 = (bf16[3,160,1024]{2,1,0:T(8,128)(2,1)}, bf16[3,160,1024]{2,1,0:T(8,128)(2,1)}, u32[]{:S(2)}, u32[]{:S(2)}) collective-permute-start(bf16[3,160,1024]{2,1,0:T(8,128)(2,1)} %slice.645), channel_id=1, source_target_pairs={{0,16},{1,17},{2,18},{3,19},{4,20},{5,21},{6,22},{7,23},{8,24},{9,... | collective-permute-start | bytes 2949128 | tf_op jit(solution)/shard_map/ppermute | solution.py:437
  750.8 23.5 %collective-permute-start.64 = (bf16[3,160,1024]{2,1,0:T(8,128)(2,1)}, bf16[3,160,1024]{2,1,0:T(8,128)(2,1)}, u32[]{:S(2)}, u32[]{:S(2)}) collective-permute-start(bf16[3,160,1024]{2,1,0:T(8,128)(2,1)} %slice.643), channel_id=1, source_target_pairs={{0,8},{1,9},{2,10},{3,11},{4,12},{5,13},{6,14},{7,15},{8,0},{9,1},... | collective-permute-start | bytes 2949128 | tf_op jit(solution)/shard_map/ppermute | solution.py:437
  786.0 31.3 %collective-permute-start.79 = (bf16[3,80,1024]{2,1,0:T(8,128)(2,1)}, bf16[3,80,1024]{2,1,0:T(8,128)(2,1)}, u32[]{:S(2)}, u32[]{:S(2)}) collective-permute-start(bf16[3,80,1024]{2,1,0:T(8,128)(2,1)} %pad_maximum_fusion.32), channel_id=1, source_target_pairs={{0,1},{1,0},{2,3},{3,2},{4,5},{5,4},{6,7},{7,6},{8,9},{9,8},{10,11... | collective-permute-start | bytes 1474568 | tf_op jit(solution)/shard_map/ppermute | solution.py:437
  796.6 36.0 %collective-permute-start.80 = (bf16[3,80,1024]{2,1,0:T(8,128)(2,1)}, bf16[3,80,1024]{2,1,0:T(8,128)(2,1)}, u32[]{:S(2)}, u32[]{:S(2)}) collective-permute-start(bf16[3,80,1024]{2,1,0:T(8,128)(2,1)} %pad_maximum_fusion.33), channel_id=1, source_target_pairs={{0,2},{1,3},{2,0},{3,1},{4,6},{5,7},{6,4},{7,5},{8,10},{9,11},{10,... | collective-permute-start | bytes 1474568 | tf_op jit(solution)/shard_map/ppermute | solution.py:437
  797.4 35.2 %collective-permute-start.81 = (bf16[3,80,1024]{2,1,0:T(8,128)(2,1)}, bf16[3,80,1024]{2,1,0:T(8,128)(2,1)}, u32[]{:S(2)}, u32[]{:S(2)}) collective-permute-start(bf16[3,80,1024]{2,1,0:T(8,128)(2,1)} %pad_maximum_fusion.34), channel_id=1, source_target_pairs={{0,3},{1,2},{2,1},{3,0},{4,7},{5,6},{6,5},{7,4},{8,11},{9,10},{10,... | collective-permute-start | bytes 1474568 | tf_op jit(solution)/shard_map/ppermute | solution.py:437
  809.1 23.5 %collective-permute-start.78 = (bf16[1,1,1,4,30,1280]{5,4,3,2,1,0:T(8,128)(2,1)}, bf16[1,1,1,4,30,1280]{5,4,3,2,1,0:T(8,128)(2,1)}, u32[]{:S(2)}, u32[]{:S(2)}) collective-permute-start(bf16[1,1,1,4,30,1280]{5,4,3,2,1,0:T(8,128)(2,1)} %broadcast_select_fusion.26), channel_id=1, source_target_pairs={{0,16},{1,17},{2,18},{3,19},{4,20},{5,21},{6,22},{7,23},{8,24},{9,... | collective-permute-start | bytes 921608 | tf_op jit(solution)/shard_map/ppermute | solution.py:437
  810.1 22.5 %collective-permute-start.77 = (bf16[1,1,1,4,31,1280]{5,4,3,2,1,0:T(8,128)(2,1)}, bf16[1,1,1,4,31,1280]{5,4,3,2,1,0:T(8,128)(2,1)}, u32[]{:S(2)}, u32[]{:S(2)}) collective-permute-start(bf16[1,1,1,4,31,1280]{5,4,3,2,1,0:T(8,128)(2,1)} %broadcast_select_fusion.32), channel_id=1, source_target_pairs={{0,8},{1,9},{2,10},{3,11},{4,12},{5,13},{6,14},{7,15},{8,0},{9,1},... | collective-permute-start | bytes 952328 | tf_op jit(solution)/shard_map/ppermute | solution.py:437
  835.7 24.6 %collective-permute-start.84 = (bf16[31,1280]{1,0:T(8,128)(2,1)}, bf16[31,1280]{1,0:T(8,128)(2,1)}, u32[]{:S(2)}, u32[]{:S(2)}) collective-permute-start(bf16[31,1280]{1,0:T(8,128)(2,1)} %get-tuple-element.509), channel_id=1, source_target_pairs={{0,3},{1,2},{2,1},{3,0},{4,7},{5,6},{6,5},{7,4},{8,11},{9,10},{10,... | collective-permute-start | bytes 238088 | tf_op jit(solution)/shard_map/ppermute | solution.py:437
  837.2 23.1 %collective-permute-start.82 = (bf16[31,1280]{1,0:T(8,128)(2,1)}, bf16[31,1280]{1,0:T(8,128)(2,1)}, u32[]{:S(2)}, u32[]{:S(2)}) collective-permute-start(bf16[31,1280]{1,0:T(8,128)(2,1)} %get-tuple-element.510), channel_id=1, source_target_pairs={{0,1},{1,0},{2,3},{3,2},{4,5},{5,4},{6,7},{7,6},{8,9},{9,8},{10,11... | collective-permute-start | bytes 238088 | tf_op jit(solution)/shard_map/ppermute | solution.py:437
  (124 other events, 1043.4 us)

commit v2 on v1

--- a/solution.py
+++ b/solution.py
@@ -427,6 +427,55 @@
     )(query, kv, out_grad, lse, key_info, query_info)
 
 
+def join_body(moves, n_in, n_out, *refs):
+    sources, targets = refs[:n_in], refs[n_in : n_in + n_out]
+    buffers, in_sems, out_sems = refs[n_in + n_out : -2], refs[-2], refs[-1]
+    loads, stores = [], []
+    for m, (i, start, size, o, place) in enumerate(moves):
+        run = pl.ds(place, size)
+        source = sources[i].at[:, pl.ds(start, size)]
+        loads.append(pltpu.make_async_copy(source, buffers[o].at[:, run], in_sems.at[m]))
+        stores.append(
+            pltpu.make_async_copy(buffers[o].at[:, run], targets[o].at[:, run], out_sems.at[m])
+        )
+    for load in loads:
+        load.start()
+    for load, store in zip(loads, stores):
+        load.wait()
+        store.start()
+    for store in stores:
+        store.wait()
+
+
+def join(groups):
+    sources, moves, shapes = [], [], []
+    for o, group in enumerate(groups):
+        place = 0
+        for array, start, size in group:
+            index = next((i for i, known in enumerate(sources) if known is array), None)
+            if index is None:
+                index = len(sources)
+                sources.append(array)
+            moves.append((index, start, size, o, place))
+            place += size
+        shapes.append((3, place, LANES))
+    if any(size % 16 for _, _, size, _, _ in moves):
+        return [
+            jnp.concatenate([array[:, start : start + size] for array, start, size in group], 1)
+            for group in groups
+        ]
+    return pl.pallas_call(
+        functools.partial(join_body, moves, len(sources), len(groups)),
+        in_specs=[any_spec()] * len(sources),
+        out_specs=[any_spec()] * len(groups),
+        out_shape=[jax.ShapeDtypeStruct(shape, bf16) for shape in shapes],
+        scratch_shapes=[pltpu.VMEM(shape, bf16) for shape in shapes]
+        + [pltpu.SemaphoreType.DMA((len(moves),))] * 2,
+        compiler_params=compiler_params(),
+        name="join",
+    )(*sources)
+
+
 def exchange(value, dp_xor=0, ctx_xor=0):
     n_dp, n_ctx = lax.axis_size("dp"), lax.axis_size("ctx")
     pairs = [
@@ -486,37 +535,46 @@
     return [exchange(value, ctx_xor=k) for k in range(1, lax.axis_size("ctx"))]
 
 
-def gather_ffn_job(flat):
-    units = flat.shape[0] // (3 * D)
-    half = units // 2
-    block = jnp.pad(flat.reshape(units, 3, D), ((0, 0), (0, 0), (0, LANES - D))).transpose(1, 0, 2)
+def ffn_block(flat):
+    block = flat.reshape(-1, 3, D)
+    return jnp.pad(block, ((0, 0), (0, 0), (0, LANES - D))).transpose(1, 0, 2)
+
+
+def gather_ffn_job(block):
+    half = block.shape[1] // 2
     (block,) = yield [block]
     parts = [block] + (yield ctx_stage(block))
-    sides = [jnp.concatenate([p[:, :half] for p in parts], 1)]
-    sides += [jnp.concatenate([p[:, half:] for p in parts], 1)]
+    sides = join([[(p, 0, half) for p in parts], [(p, half, half) for p in parts]])
     orders = [dp_bits(color) for color in range(2)]
     for i in range(len(orders[0])):
         arrived = yield [exchange(s, dp_xor=order[i]) for s, order in zip(sides, orders)]
         if i + 1 < len(orders[0]):
-            sides = [jnp.concatenate([s, a], 1) for s, a in zip(sides, arrived)]
+            size = sides[0].shape[1]
+            sides = join([[(s, 0, size), (a, 0, size)] for s, a in zip(sides, arrived)])
     return [sides[0], arrived[0], sides[1], arrived[1]]
 
 
 def scatter_ffn_job(pieces, shard_len):
     orders = [dp_bits(color)[::-1] for color in range(2)]
     keeps, sends = [pieces[0], pieces[2]], [pieces[1], pieces[3]]
+    n_ctx = lax.axis_size("ctx")
+
+    def part_sums(count):
+        size = keeps[0].shape[1] // count
+        runs = [slice(i * size, (i + 1) * size) for i in range(count)]
+        return [
+            [
+                (k[:, run].astype(f32) + a[:, run].astype(f32)).astype(bf16)
+                for k, a in zip(keeps, arrived)
+            ]
+            for run in runs
+        ]
+
     for i in range(len(orders[0])):
         arrived = yield [exchange(s, dp_xor=order[i]) for s, order in zip(sends, orders)]
-        totals = [(k.astype(f32) + a.astype(f32)).astype(bf16) for k, a in zip(keeps, arrived)]
         if i + 1 < len(orders[0]):
-            half = totals[0].shape[1] // 2
-            keeps, sends = [t[:, :half] for t in totals], [t[:, half:] for t in totals]
-    n_ctx = lax.axis_size("ctx")
-    half = totals[0].shape[1] // n_ctx
-    parts = [
-        jnp.concatenate([t[:, k * half : (k + 1) * half] for t in totals], 1)
-        for k in range(n_ctx)
-    ]
+            keeps, sends = part_sums(2)
+    parts = [jnp.concatenate(pair, 1) for pair in part_sums(n_ctx)]
     arrived = yield [exchange(parts[k], ctx_xor=k) for k in range(1, n_ctx)]
     shard = parts[0].astype(f32)
     for part in arrived:
@@ -524,9 +582,14 @@
     return shard[:, :, :D].transpose(1, 0, 2).reshape(shard_len)
 
 
+def padded(rows):
+    return -(-(rows + 1) // 16) * 16
+
+
 def add_row(block, row):
-    pad = jnp.zeros((1, block.shape[1] - row.shape[0]), block.dtype)
-    return jnp.concatenate([block, jnp.concatenate([row[None], pad], 1)], 0)
+    rows, cols = block.shape
+    extra = jnp.pad(row[None], ((0, padded(rows) - rows - 1), (0, cols - row.shape[0])))
+    return jnp.concatenate([block, extra], 0)
 
 
 def by_rows(shard_len):
@@ -537,6 +600,7 @@
     n_dp, n_ctx = lax.axis_size("dp"), lax.axis_size("ctx")
     n, n_bits = n_dp * n_ctx, n_dp.bit_length() - 1
     gain_len = gain_flat.shape[0]
+    rows = qkv_flat.shape[0] // math.gcd(qkv_flat.shape[0], QKV_WIDTH)
     if by_rows(qkv_flat.shape[0]):
         qkv, out = qkv_flat.reshape(-1, QKV_WIDTH), out_flat.reshape(-1, D)
         blocks = [add_row(qkv[:, :QK_WIDTH], gain_flat)]
@@ -566,13 +630,13 @@
             joined.append(jnp.concatenate(pair, n_bits - order[i].bit_length()))
         sides = joined
     first, second = (s.reshape((n,) + s.shape[-2:]) for s in sides)
-    gains = first[:, -1, :gain_len].reshape(n * gain_len).astype(f32)
+    gains = first[:, rows, :gain_len].reshape(n * gain_len).astype(f32)
     if by_rows(qkv_flat.shape[0]):
-        w_qk = first[:, :-1].reshape(D, QK_WIDTH)
-        second = second[:, :-1].reshape(D, QK_WIDTH)
+        w_qk = first[:, :rows].reshape(D, QK_WIDTH)
+        second = second[:, :rows].reshape(D, QK_WIDTH)
         w_out, w_v = second[:, :D], second[:, D:]
     else:
-        w_qkv = first[:, :-1].reshape(D, QKV_WIDTH)
+        w_qkv = first[:, :rows].reshape(D, QKV_WIDTH)
         w_qk, w_v = w_qkv[:, :QK_WIDTH], w_qkv[:, QK_WIDTH:]
         w_out = second.reshape(Q_WIDTH, D)
     return w_qk, w_v, w_out, gains[:D], gains[D:]
@@ -584,13 +648,17 @@
     gain_len = gain_grad.shape[0] // n
     gain_row = gain_grad.astype(bf16).reshape(n, 1, gain_len)
 
+    rows = qkv_len // math.gcd(qkv_len, QKV_WIDTH)
+
     def with_gain(blocks):
-        return jnp.concatenate(
-            [blocks, jnp.pad(gain_row, ((0, 0), (0, 0), (0, blocks.shape[2] - gain_len)))], 1
-        )
+        extra = ((0, 0), (0, padded(rows) - rows - 1), (0, blocks.shape[2] - gain_len))
+        return jnp.concatenate([blocks, jnp.pad(gain_row, extra)], 1)
+
+    def with_zeros(blocks):
+        return jnp.pad(blocks, ((0, 0), (0, padded(rows) - rows), (0, 0)))
 
     if by_rows(qkv_len):
-        sides = [with_gain(dw_qk.reshape(n, -1, QK_WIDTH)), dw_ov.reshape(n, -1, QK_WIDTH)]
+        sides = [with_gain(dw_qk.reshape(n, -1, QK_WIDTH)), with_zeros(dw_ov.reshape(n, -1, QK_WIDTH))]
     else:
         dw_qkv = jnp.concatenate([dw_qk, dw_ov[:, Q_WIDTH:]], 1)
         sides = [with_gain(dw_qkv.reshape(n, -1, math.gcd(qkv_len, QKV_WIDTH)))]
@@ -615,12 +683,12 @@
             total = total + part.astype(f32)
         totals.append(total)
     first, second = totals
-    gain_part = first[-1, :gain_len]
+    gain_part = first[rows, :gain_len]
     if by_rows(qkv_len):
-        qkv_part = jnp.concatenate([first[:-1], second[:, D:]], 1)
-        out_part = second[:, :D]
+        qkv_part = jnp.concatenate([first[:rows], second[:rows, D:]], 1)
+        out_part = second[:rows, :D]
     else:
-        qkv_part, out_part = first[:-1], second
+        qkv_part, out_part = first[:rows], second
     return qkv_part.reshape(qkv_len), out_part.reshape(out_len), gain_part
 
 
@@ -669,12 +737,13 @@
         Job(gather_attention_job(qkv_weights[i], out_weights[i], norm_gains[i]))
         for i in range(LAYERS)
     ]
-    ffn = [Job(gather_ffn_job(ffn_weights[i])) for i in range(LAYERS)]
 
     fence((), attn[0], info)
-    fence((), attn[0], info, tokens)
-    fence((), attn[0], ffn[0])
-    fence((), attn[0], tokens)
+    blocks = [ffn_block(ffn_weights[i]) for i in range(LAYERS)]
+    blocks = fence(blocks, attn[0], info, tokens)
+    ffn = [Job(gather_ffn_job(block)) for block in blocks]
+    fence((), attn[0])
+    fence((), attn[0], tokens, ffn[0])
     finish((), attn[0], info, tokens)
     info = info.result
 
@@ -703,6 +772,8 @@
         kv_all = gather_group(kv_own.reshape(2, local_len, 2 * KV_WIDTH))
         if layer == 0:
             qk, kv_all = fence((qk, kv_all), ffn[0], attn[1])
+        else:
+            qk, kv_all = fence((qk, kv_all), upstream)
         attended, lse = attention_forward(qk, kv_all, key_info, query_info)
         middle = residual + dot_nn(attended, w_out)
         if layer == 0:
@@ -721,7 +792,7 @@
         )
         residual = following
         if layer == 0:
-            residual = fence(residual, attn[1], ffn[1], upstream)
+            residual = fence(residual, attn[1], ffn[1])
             residual = finish(residual, attn[1])
     residual = finish(residual, upstream)
     back = Job(pair_tokens_job(residual.reshape(2, local_len, D), bf16))
@@ -734,26 +805,37 @@
         middle, scale_two, normed_two, gate, up = saved[layer][7:]
         terms, normal_two = ffn_backward(gradient, normed_two, gate, up, ffn[layer].result)
         if layer:
-            terms, normal_two = fence((terms, normal_two), back)
+            terms, normal_two = fence((terms, normal_two))
         else:
-            terms, normal_two = fence((terms, normal_two), ffn_jobs[1], attn_jobs[1])
+            terms, normal_two = fence((terms, normal_two), attn_jobs[1])
         ffn_jobs[layer] = Job(scatter_ffn_job(terms, ffn_len))
         gain_two_grad = jnp.sum(normal_two * middle * scale_two, 0)
         gradient = gradient + norm_back(normal_two, middle, scale_two, gain_two)
         attn_low = gradient.astype(bf16)
         attended_grad = dot_nt(attn_low, w_out).astype(bf16)
-        attended_grad = fence(attended_grad, ffn_jobs[layer], back if layer else attn_jobs[1])
+        if layer:
+            attended_grad = fence(attended_grad, ffn_jobs[1], back)
+        else:
+            attended_grad = fence(attended_grad, ffn_jobs[0], attn_jobs[1], ffn_jobs[1])
         query_grad, kv_grad = attention_backward(
             qk, kv_all, attended_grad, lse, key_info, query_info
         )
-        if layer == 0:
-            query_grad, kv_grad = fence((query_grad, kv_grad), ffn_jobs[1], attn_jobs[1])
-        kv_grad = scatter_group(kv_grad).reshape(rows, 2 * KV_WIDTH)
+        if layer:
+            query_grad, kv_grad = fence((query_grad, kv_grad), back)
+            kv_grad = scatter_group(kv_grad).reshape(rows, 2 * KV_WIDTH)
+            query_grad, kv_grad = fence((query_grad, kv_grad), ffn_jobs[1])
+        else:
+            query_grad, kv_grad = fence((query_grad, kv_grad))
+            kv_grad = scatter_group(kv_grad).reshape(rows, 2 * KV_WIDTH)
+            query_grad, kv_grad = fence((query_grad, kv_grad), ffn_jobs[0], attn_jobs[1])
         dw_qk, dw_ov, gain_one_grad, gradient = qkv_backward(
             query_grad, kv_grad, residual, normed_one, scale_one, gain_one, w_qk, w_v,
             cosine, sine, gradient, attended, attn_low,
         )
-        dw_qk, dw_ov, gradient = fence((dw_qk, dw_ov, gradient), ffn_jobs[layer])
+        if layer:
+            dw_qk, dw_ov, gradient = fence((dw_qk, dw_ov, gradient), ffn_jobs[1])
+        else:
+            dw_qk, dw_ov, gradient = fence((dw_qk, dw_ov, gradient))
         attn_jobs[layer] = Job(
             scatter_attention_job(
                 dw_qk, dw_ov, jnp.concatenate([gain_one_grad[0], gain_two_grad]), qkv_len, out_len
@@ -761,8 +843,8 @@
         )
     last = Job(pair_tokens_job(gradient.reshape(2, local_len, D), bf16))
     fence((), last)
-    fence((), ffn_jobs[0], attn_jobs[0], attn_jobs[1], last)
-    fence((), attn_jobs[0])
+    fence((), ffn_jobs[0], attn_jobs[0], attn_jobs[1])
+    fence((), attn_jobs[0], last)
     fence((), attn_jobs[0], ffn_jobs[0])
     finish((), back, last, *ffn_jobs, *attn_jobs)
     return (

time: 876 us -> 840 us (0.959)
  local copies, waits for them, and re-layouts: 185 us -> 106 us
  waiting for transfers between devices: 173 us -> 213 us
  starting transfers between devices: 131 us -> 107 us
  Pallas kernels: 227 us -> 246 us
  other arithmetic: 133 us -> 147 us
    unnamed x217 -> x165, local copies, waits for them, and re-layouts: 56.4 us -> 12.9 us
    ppermute x88, waiting for transfers between devices: 173 us -> 213 us  [exchange(): return lax.ppermute(value, AXES, pairs)]
    concatenate x18 -> x2, local copies, waits for them, and re-layouts: 29.8 us -> 5.45 us  [with_gain(): return jnp.concatenate([blocks, jnp.pad(gain_row, extra)], 1)]
    ppermute x88, starting transfers between devices: 131 us -> 107 us  [exchange(): return lax.ppermute(value, AXES, pairs)]
    pallas_call x0 -> x4, Pallas kernels: none -> 19.6 us  [join(): pl.pallas_call(functools.partial(join_body, moves, len(sources), len(grou...]
    select_n x8 -> x0, local copies, waits for them, and re-layouts: 10.2 us -> none  [scatter_attention_job(): sends.append(jnp.where(flag, low, high))]
    slice x20 -> x15, local copies, waits for them, and re-layouts: 26.5 us -> 17.4 us  [the longest x1 9.88 us: per_device(): blocks = [ffn_block(ffn_weights[i]) for i in range(LAYERS)]]
    reshape x4 -> x6, local copies, waits for them, and re-layouts: 13.3 us -> 21.9 us  [the longest x2 8.67 us: gather_attention_job(): second = second[:, :rows].reshape(D, QK_WIDTH)]
  transfers between devices with their start and end apart: 88 -> 88, of which waited for: 29 -> 34; matrix products, arithmetic and copies ran while one was open for 26% -> 25% of each run, Pallas kernels for 21% -> 20%
where the time goes in v2:
time: 840 us; the launch traced here: 834 us
  Pallas kernels  246 us (29%)
  waiting for transfers between devices  213 us (25%)
  other arithmetic  147 us (18%)
  starting transfers between devices  107 us (13%)
  local copies, waits for them, and re-layouts  106 us (13%)
  matrix products  12.9 us (2%)
    ppermute x88, waiting for transfers between devices, exchange(): return lax.ppermute(value, AXES, pairs)  213 us
    ppermute x88, starting transfers between devices, exchange(): return lax.ppermute(value, AXES, pairs)  107 us
    pallas_call x2, Pallas kernels, attention_backward(): pl.pallas_call(attention_backward_body, out_shape=[jax.ShapeDtypeStruct((...  58.4 us
    pallas_call x2, Pallas kernels, ffn_backward(): pl.pallas_call(functools.partial(ffn_backward_body, n_pieces), grid=(n_pi...  55.6 us
    pallas_call x2, Pallas kernels, attention_forward(): pl.pallas_call(attention_forward_body, out_shape=[jax.ShapeDtypeStruct((r...  40.4 us
    convert_element_type x12, other arithmetic, part_sums(): (k[:, run].astype(f32) + a[:, run].astype(f32)).astype(bf16)  37 us
    pallas_call x2, Pallas kernels, ffn_forward(): pl.pallas_call(functools.partial(ffn_forward_body, n_pieces), grid=(n_pie...  33 us
    pallas_call x2, Pallas kernels, qkv_backward(): pl.pallas_call(qkv_backward_body, out_shape=[jax.ShapeDtypeStruct((D, QK_...  26.1 us
  transfers between devices with their start and end apart: 88, of which 34 were waited for; matrix products, arithmetic and copies ran while one was open for 25% of the time, Pallas kernels for 20%

profile of v2, /device:TPU:0, one launch (start us, length us, event | category | flops | bytes accessed | tf_op | source)
XLA Modules:
  0.0 834.5 jit_solution(14975984504976813973)
XLA Ops:
  0.6 2.8 slice_reduce_fusion.2
  9.4 5.0 collective-permute-start.2
  15.0 3.8 collective-permute-start.3
  18.8 9.9 %slice_reduce_fusion = (bf16[230400]{0:T(1024)(128)(2,1)S(1)}, bf16[230400]{0:T(1024)(128)(2,1)S(1)}) fusion(bf16[2,230400]{1,0:T(2,128)(2,1)S(1)} %copy-done.44), kind=kLoop, calls=%fused_computation.111 | loop fusion | bytes 1843200 | tf_op jit(solution)/shard_map/slice | solution.py:742
  40.7 5.3 collective-permute-done.4
  53.6 12.7 %collective-permute-done.8 = bf16[256,960]{1,0:T(8,128)(2,1)} collective-permute-done((bf16[256,960]{1,0:T(8,128)(2,1)}, bf16[256,960]{1,0:T(8,128)(2,1)}, u32[]{:S(2)}, u32[]{:S(2)}) %collective-permute-start.8) | collective-permute-done | bytes 491552 | tf_op jit(solution)/shard_map/ppermute | solution.py:486
  76.1 9.7 %collective-permute-start.12 = (bf16[3,80,1024]{2,1,0:T(8,128)(2,1)}, bf16[3,80,1024]{2,1,0:T(8,128)(2,1)}, u32[]{:S(2)}, u32[]{:S(2)}) collective-permute-start(bf16[3,80,1024]{2,1,0:T(8,128)(2,1)} %pad_bitcast_fusion.1), channel_id=1, source_target_pairs={{0,2},{1,3},{2,0},{3,1},{4,6},{5,7},{6,4},{7,5},{8,10},{9,11},{10,... | collective-permute-start | bytes 1474568 | tf_op jit(solution)/shard_map/ppermute | solution.py:486
  91.9 3.0 broadcast_select_fusion.9
  95.6 3.5 pad_maximum_fusion.1
  99.1 4.4 reshape.394
  108.1 6.5 qkv_forward.2
  114.5 8.0 collective-permute-done.12
  131.6 13.6 %collective-permute-done.14 = bf16[2,256,640]{2,1,0:T(8,128)(2,1)} collective-permute-done((bf16[2,256,640]{2,1,0:T(8,128)(2,1)}, bf16[2,256,640]{2,1,0:T(8,128)(2,1)}, u32[]{:S(2)}, u32[]{:S(2)}) %collective-permute-start.14) | collective-permute-done | bytes 655392 | tf_op jit(solution)/shard_map/ppermute | solution.py:486
  147.6 4.6 collective-permute-done.15.refs_1_
  153.1 3.2 join.4
  167.0 20.4 %attention_forward.2 = (bf16[512,960]{1,0:T(8,128)(2,1)}, f32[15,1,512]{2,1,0:T(1,128)}) custom-call(bf16[512,1280]{1,0:T(8,128)(2,1)} %get-tuple-element.208.q_ref, bf16[1024,640]{1,0:T(8,128)(2,1)} %pad_maximum_fusion.13.kv_ref, s32[1024,2]{1,0:T(8,128)} %copy.70.key_info, s32[2,512]{1,0:T(2,128)} %add_bitcast_fusion.2.query_info), custom_call_target="tpu_custom_call" | custom-call | tf_op jit(solution)/shard_map/attention_forward/pallas_call | solution.py:335
  187.4 4.5 fusion.8.refs_0_
  191.9 8.4 %collective-permute-done.21.refs_1_ = bf16[3,320,1024]{2,1,0:T(8,128)(2,1)} collective-permute-done((bf16[3,320,1024]{2,1,0:T(8,128)(2,1)}, bf16[3,320,1024]{2,1,0:T(8,128)(2,1)}, u32[]{:S(2)}, u32[]{:S(2)}) %collective-permute-start.21) | collective-permute-done | bytes 1966112 | tf_op jit(solution)/shard_map/ppermute | solution.py:486
  200.5 6.6 join.5
  210.5 7.1 collective-permute-done.25
  227.9 16.4 %ffn_forward.2 = (f32[512,960]{1,0:T(8,128)}, bf16[512,960]{1,0:T(8,128)(2,1)}, f32[512,1]{1,0:T(8,128)}, f32[512,2560]{1,0:T(8,128)}, f32[512,2560]{1,0:T(8,128)}) custom-call(f32[512,960]{1,0:T(8,128)} %fusion.8.refs_0_, f32[1,960]{1,0:T(1,128)} %broadcast_in_dim.9.refs_1_, bf16[3,640,1024]{2,1,0:T(8,128)(2,1)} %get-tuple-element.221.refs_2_.refs_4_, ...), custom_call_target="tpu_custom_call" | custom-call | tf_op jit(solution)/shard_map/ffn_forward/pallas_call | solution.py:185
  244.3 23.8 %collective-permute-done.30 = bf16[3,80,1024]{2,1,0:T(8,128)(2,1)} collective-permute-done((bf16[3,80,1024]{2,1,0:T(8,128)(2,1)S(1)}, bf16[3,80,1024]{2,1,0:T(8,128)(2,1)}, u32[]{:S(2)}, u32[]{:S(2)}) %collective-permute-start.30) | collective-permute-done | bytes 491552 | tf_op jit(solution)/shard_map/ppermute | solution.py:486
  282.9 4.2 reshape.401
  291.9 6.5 qkv_forward.3
  302.0 3.2 join.6
  311.1 13.7 %collective-permute-done.36 = bf16[2,256,640]{2,1,0:T(8,128)(2,1)} collective-permute-done((bf16[2,256,640]{2,1,0:T(8,128)(2,1)}, bf16[2,256,640]{2,1,0:T(8,128)(2,1)}, u32[]{:S(2)}, u32[]{:S(2)}) %collective-permute-start.36) | collective-permute-done | bytes 655392 | tf_op jit(solution)/shard_map/ppermute | solution.py:486
  328.3 20.0 %attention_forward.3 = (bf16[512,960]{1,0:T(8,128)(2,1)}, f32[15,1,512]{2,1,0:T(1,128)}) custom-call(bf16[512,1280]{1,0:T(8,128)(2,1)} %get-tuple-element.246.q_ref, bf16[1024,640]{1,0:T(8,128)(2,1)} %pad_maximum_fusion.16.kv_ref, s32[1024,2]{1,0:T(8,128)} %copy.70.key_info, s32[2,512]{1,0:T(2,128)} %add_bitcast_fusion.2.query_info), custom_call_target="tpu_custom_call" | custom-call | tf_op jit(solution)/shard_map/attention_forward/pallas_call | solution.py:335
  348.3 3.8 fusion.11.refs_0_
  352.1 6.6 join.7
  361.7 4.1 collective-permute-done.40.refs_3_.refs_5_
  365.9 5.6 collective-permute-done.41.refs_5_.refs_7_
  371.5 16.6 %ffn_forward.3 = (f32[512,960]{1,0:T(8,128)}, bf16[512,960]{1,0:T(8,128)(2,1)}, f32[512,1]{1,0:T(8,128)}, f32[512,2560]{1,0:T(8,128)}, f32[512,2560]{1,0:T(8,128)}) custom-call(f32[512,960]{1,0:T(8,128)} %fusion.11.refs_0_, f32[1,960]{1,0:T(1,128)} %broadcast_in_dim.22.refs_1_, bf16[3,640,1024]{2,1,0:T(8,128)(2,1)} %get-tuple-element.257.refs_2_.refs_4_, ...), custom_call_target="tpu_custom_call" | custom-call | tf_op jit(solution)/shard_map/ffn_forward/pallas_call | solution.py:185
  388.1 27.9 %ffn_backward.2 = (bf16[3,640,1024]{2,1,0:T(8,128)(2,1)}, bf16[3,640,1024]{2,1,0:T(8,128)(2,1)}, bf16[3,640,1024]{2,1,0:T(8,128)(2,1)}, bf16[3,640,1024]{2,1,0:T(8,128)(2,1)}, f32[512,960]{1,0:T(8,128)}) custom-call(f32[512,960]{1,0:T(8,128)} %bitcast.216, bf16[512,960]{1,0:T(8,128)(2,1)} %get-tuple-element.265.refs_1_, ...), custom_call_target="tpu_custom_call" | custom-call | tf_op jit(solution)/shard_map/ffn_backward/pallas_call | solution.py:267
  426.0 2.9 collective-permute-done.43
  428.8 5.8 add_convert_fusion.4
  435.7 5.5 add_convert_fusion.5
  445.3 29.1 %attention_backward.2 = (f32[512,960]{1,0:T(8,128)}, f32[1024,640]{1,0:T(8,128)}) custom-call(bf16[512,1280]{1,0:T(8,128)(2,1)} %get-tuple-element.246.q_ref, bf16[1024,640]{1,0:T(8,128)(2,1)} %pad_maximum_fusion.16.kv_ref, bf16[512,960]{1,0:T(8,128)(2,1)} %fusion.17.og_ref, f32[15,1,512]{2,1,0:T(1,128)} %get-tuple-element.272.lse_ref, ...), custom_call_target="tpu_custom_call" | custom-call | tf_op jit(solution)/shard_map/attention_backward/pallas_call | solution.py:407
  475.9 15.9 %collective-permute-done.45 = bf16[2,256,640]{2,1,0:T(8,128)(2,1)S(1)} collective-permute-done((bf16[2,256,640]{2,1,0:T(8,128)(2,1)S(1)}, bf16[2,256,640]{2,1,0:T(8,128)(2,1)S(1)}, u32[]{:S(2)}, u32[]{:S(2)}) %collective-permute-start.45) | collective-permute-done | bytes 655392 | tf_op jit(solution)/shard_map/ppermute | solution.py:486
  500.5 13.1 %qkv_backward.2 = (bf16[960,1280]{1,0:T(8,128)(2,1)}, bf16[960,1280]{1,0:T(8,128)(2,1)}, f32[1,960]{1,0:T(1,128)}, f32[512,960]{1,0:T(8,128)}) custom-call(f32[512,960]{1,0:T(8,128)} %get-tuple-element.283.dq_ref, f32[512,640]{1,0:T(8,128)} %bitcast.226, f32[512,960]{1,0:T(8,128)} %get-tuple-element.236.x_ref, ...), custom_call_target="tpu_custom_call" | custom-call | tf_op jit(solution)/shard_map/qkv_backward/pallas_call | solution.py:131
  514.5 4.4 collective-permute-done.49
  522.3 2.7 concatenate.197
  526.8 4.2 reshape.406
  535.8 27.6 %ffn_backward.3 = (bf16[3,640,1024]{2,1,0:T(8,128)(2,1)}, bf16[3,640,1024]{2,1,0:T(8,128)(2,1)}, bf16[3,640,1024]{2,1,0:T(8,128)(2,1)}, bf16[3,640,1024]{2,1,0:T(8,128)(2,1)}, f32[512,960]{1,0:T(8,128)}) custom-call(f32[512,960]{1,0:T(8,128)} %get-tuple-element.292.refs_0_, bf16[512,960]{1,0:T(8,128)(2,1)} %get-tuple-element.294.refs_1_, ...), custom_call_target="tpu_custom_call" | custom-call | tf_op jit(solution)/shard_map/ffn_backward/pallas_call | solution.py:267
  568.1 2.7 collective-permute-start.58
  576.1 12.3 %collective-permute-done.56 = bf16[3,80,1024]{2,1,0:T(8,128)(2,1)S(1)} collective-permute-done((bf16[3,80,1024]{2,1,0:T(8,128)(2,1)S(1)}, bf16[3,80,1024]{2,1,0:T(8,128)(2,1)S(1)}, u32[]{:S(2)}, u32[]{:S(2)}) %collective-permute-start.56) | collective-permute-done | bytes 491552 | tf_op jit(solution)/shard_map/ppermute | solution.py:486
  589.4 13.6 %collective-permute-done.57 = bf16[3,80,1024]{2,1,0:T(8,128)(2,1)S(1)} collective-permute-done((bf16[3,80,1024]{2,1,0:T(8,128)(2,1)S(1)}, bf16[3,80,1024]{2,1,0:T(8,128)(2,1)S(1)}, u32[]{:S(2)}, u32[]{:S(2)}) %collective-permute-start.57) | collective-permute-done | bytes 491552 | tf_op jit(solution)/shard_map/ppermute | solution.py:486
  608.9 8.5 %collective-permute-done.54 = bf16[1,2,1,4,32,1280]{5,4,3,2,1,0:T(8,128)(2,1)S(1)} collective-permute-done((bf16[1,2,1,4,32,1280]{5,4,3,2,1,0:T(8,128)(2,1)S(1)}, bf16[1,2,1,4,32,1280]{5,4,3,2,1,0:T(8,128)(2,1)S(1)}, u32[]{:S(2)}, u32[]{:S(2)}) %collective-permute-start.54) | collective-permute-done | bytes 655392 | tf_op jit(solution)/shard_map/ppermute | solution.py:486
  617.7 4.0 add_convert_fusion
  622.7 4.1 add_convert_fusion.3
  629.5 29.3 %attention_backward.3 = (f32[512,960]{1,0:T(8,128)}, f32[1024,640]{1,0:T(8,128)}) custom-call(bf16[512,1280]{1,0:T(8,128)(2,1)} %get-tuple-element.208.q_ref, bf16[1024,640]{1,0:T(8,128)(2,1)} %pad_maximum_fusion.13.kv_ref, bf16[512,960]{1,0:T(8,128)(2,1)} %fusion.14.og_ref, f32[15,1,512]{2,1,0:T(1,128)} %get-tuple-element.313.lse_ref, ...), custom_call_target="tpu_custom_call" | custom-call | tf_op jit(solution)/shard_map/attention_backward/pallas_call | solution.py:407
  663.2 2.9 fusion.28
  666.2 7.9 collective-permute-done.59
  680.2 13.0 %qkv_backward.3 = (bf16[960,1280]{1,0:T(8,128)(2,1)}, bf16[960,1280]{1,0:T(8,128)(2,1)}, f32[1,960]{1,0:T(1,128)}, f32[512,960]{1,0:T(8,128)}) custom-call(f32[512,960]{1,0:T(8,128)} %get-tuple-element.322.dq_ref, f32[512,640]{1,0:T(8,128)} %bitcast.227, f32[512,960]{1,0:T(8,128)} %bitcast.218, bf16[512,960]{1,0:T(8,128)(2,1)} %get-tuple-element.324.normed_ref, ...), custom_call_target="tpu_custom_call" | custom-call | tf_op jit(solution)/shard_map/qkv_backward/pallas_call | solution.py:131
  694.1 2.7 concatenate.206
  703.7 4.4 reshape.410
  713.1 3.8 add_convert_fusion.13
  724.0 2.8 copy.94
  732.6 3.8 stack_reshape.23
  742.0 3.2 collective-permute-start.76
  765.4 3.2 collective-permute-start.81
  779.4 4.3 collective-permute-done.79
  783.7 16.2 %collective-permute-done.80 = bf16[3,80,1024]{2,1,0:T(8,128)(2,1)} collective-permute-done((bf16[3,80,1024]{2,1,0:T(8,128)(2,1)}, bf16[3,80,1024]{2,1,0:T(8,128)(2,1)}, u32[]{:S(2)}, u32[]{:S(2)}) %collective-permute-start.80) | collective-permute-done | bytes 491552 | tf_op jit(solution)/shard_map/ppermute | solution.py:486
  804.7 10.6 %collective-permute-start.82 = (bf16[32,1280]{1,0:T(8,128)(2,1)}, bf16[32,1280]{1,0:T(8,128)(2,1)}, u32[]{:S(2)}, u32[]{:S(2)}) collective-permute-start(bf16[32,1280]{1,0:T(8,128)(2,1)} %get-tuple-element.508), channel_id=1, source_target_pairs={{0,1},{1,0},{2,3},{3,2},{4,5},{5,4},{6,7},{7,6},{8,9},{9,8},{10,11... | collective-permute-start | bytes 245768 | tf_op jit(solution)/shard_map/ppermute | solution.py:486
  827.0 2.9 collective-permute-done.86
  (529 shorter events, 269.0 us)
Async XLA Ops:
  9.4 26.8 %collective-permute-start.2 = (bf16[32,2560]{1,0:T(8,128)(2,1)}, bf16[32,2560]{1,0:T(8,128)(2,1)}, u32[]{:S(2)}, u32[]{:S(2)}) collective-permute-start(bf16[32,2560]{1,0:T(8,128)(2,1)} %fusion.45), channel_id=1, source_target_pairs={{0,3},{1,2},{2,1},{3,0},{4,7},{5,6},{6,5},{7,4},{8,11},{9,10},{10,... | collective-permute-start | bytes 491528 | tf_op jit(solution)/shard_map/ppermute | solution.py:486
  14.4 21.8 %collective-permute-start.1 = (bf16[32,2560]{1,0:T(8,128)(2,1)}, bf16[32,2560]{1,0:T(8,128)(2,1)}, u32[]{:S(2)}, u32[]{:S(2)}) collective-permute-start(bf16[32,2560]{1,0:T(8,128)(2,1)} %fusion.45), channel_id=1, source_target_pairs={{0,2},{1,3},{2,0},{3,1},{4,6},{5,7},{6,4},{7,5},{8,10},{9,11},{10,... | collective-permute-start | bytes 491528 | tf_op jit(solution)/shard_map/ppermute | solution.py:486
  14.4 21.8 %collective-permute-start = (bf16[32,2560]{1,0:T(8,128)(2,1)}, bf16[32,2560]{1,0:T(8,128)(2,1)}, u32[]{:S(2)}, u32[]{:S(2)}) collective-permute-start(bf16[32,2560]{1,0:T(8,128)(2,1)} %fusion.45), channel_id=1, source_target_pairs={{0,1},{1,0},{2,3},{3,2},{4,5},{5,4},{6,7},{7,6},{8,9},{9,8},{10,11... | collective-permute-start | bytes 491528 | tf_op jit(solution)/shard_map/ppermute | solution.py:486
  15.0 21.2 %collective-permute-start.3 = (s32[256,2]{0,1:T(2,128)S(1)}, s32[256,2]{0,1:T(2,128)}, u32[]{:S(2)}, u32[]{:S(2)}) collective-permute-start(s32[256,2]{0,1:T(2,128)S(1)} %select_bitcast_fusion.12), channel_id=1, source_target_pairs={{0,3},{1,2},{2,1},{3,0},{4,7},{5,6},{6,5},{7,4},{8,11},{9,10},{10,... | collective-permute-start | bytes 6152 | tf_op jit(solution)/shard_map/ppermute | solution.py:486
  49.3 17.0 %collective-permute-start.6 = (bf16[1,2,1,4,32,1280]{5,4,3,2,1,0:T(8,128)(2,1)}, bf16[1,2,1,4,32,1280]{5,4,3,2,1,0:T(8,128)(2,1)}, u32[]{:S(2)}, u32[]{:S(2)}) collective-permute-start(bf16[1,2,1,4,32,1280]{5,4,3,2,1,0:T(8,128)(2,1)} %pad_maximum_fusion.23), channel_id=1, source_target_pairs={{0,16},{1,17},{2,18},{3,19},{4,20},{5,21},{6,22},{7,23},{8,24},{9,... | collective-permute-start | bytes 1966088 | tf_op jit(solution)/shard_map/ppermute | solution.py:486
  70.9 18.4 %collective-permute-start.9 = (bf16[2,2,1,4,32,1280]{5,4,3,2,1,0:T(8,128)(2,1)}, bf16[2,2,1,4,32,1280]{5,4,3,2,1,0:T(8,128)(2,1)}, u32[]{:S(2)}, u32[]{:S(2)}) collective-permute-start(bf16[2,2,1,4,32,1280]{5,4,3,2,1,0:T(8,128)(2,1)} %pad_maximum_fusion.11), channel_id=1, source_target_pairs={{0,4},{1,5},{2,6},{3,7},{4,0},{5,1},{6,2},{7,3},{8,12},{9,13},{10,... | collective-permute-start | bytes 3932168 | tf_op jit(solution)/shard_map/ppermute | solution.py:486
  72.1 17.2 %collective-permute-start.10 = (bf16[2,2,1,4,32,1280]{5,4,3,2,1,0:T(8,128)(2,1)}, bf16[2,2,1,4,32,1280]{5,4,3,2,1,0:T(8,128)(2,1)}, u32[]{:S(2)}, u32[]{:S(2)}) collective-permute-start(bf16[2,2,1,4,32,1280]{5,4,3,2,1,0:T(8,128)(2,1)} %pad_maximum_fusion.12), channel_id=1, source_target_pairs={{0,4},{1,5},{2,6},{3,7},{4,0},{5,1},{6,2},{7,3},{8,12},{9,13},{10,... | collective-permute-start | bytes 3932168 | tf_op jit(solution)/shard_map/ppermute | solution.py:486
  75.7 38.8 %collective-permute-start.13 = (bf16[3,80,1024]{2,1,0:T(8,128)(2,1)}, bf16[3,80,1024]{2,1,0:T(8,128)(2,1)}, u32[]{:S(2)}, u32[]{:S(2)}) collective-permute-start(bf16[3,80,1024]{2,1,0:T(8,128)(2,1)} %pad_bitcast_fusion.1), channel_id=1, source_target_pairs={{0,3},{1,2},{2,1},{3,0},{4,7},{5,6},{6,5},{7,4},{8,11},{9,10},{10,... | collective-permute-start | bytes 1474568 | tf_op jit(solution)/shard_map/ppermute | solution.py:486
  76.1 46.5 %collective-permute-start.12 = (bf16[3,80,1024]{2,1,0:T(8,128)(2,1)}, bf16[3,80,1024]{2,1,0:T(8,128)(2,1)}, u32[]{:S(2)}, u32[]{:S(2)}) collective-permute-start(bf16[3,80,1024]{2,1,0:T(8,128)(2,1)} %pad_bitcast_fusion.1), channel_id=1, source_target_pairs={{0,2},{1,3},{2,0},{3,1},{4,6},{5,7},{6,4},{7,5},{8,10},{9,11},{10,... | collective-permute-start | bytes 1474568 | tf_op jit(solution)/shard_map/ppermute | solution.py:486
  85.8 36.8 %collective-permute-start.11 = (bf16[3,80,1024]{2,1,0:T(8,128)(2,1)}, bf16[3,80,1024]{2,1,0:T(8,128)(2,1)}, u32[]{:S(2)}, u32[]{:S(2)}) collective-permute-start(bf16[3,80,1024]{2,1,0:T(8,128)(2,1)} %pad_bitcast_fusion.1), channel_id=1, source_target_pairs={{0,1},{1,0},{2,3},{3,2},{4,5},{5,4},{6,7},{7,6},{8,9},{9,8},{10,11... | collective-permute-start | bytes 1474568 | tf_op jit(solution)/shard_map/ppermute | solution.py:486
  128.2 17.0 %collective-permute-start.14 = (bf16[2,256,640]{2,1,0:T(8,128)(2,1)}, bf16[2,256,640]{2,1,0:T(8,128)(2,1)}, u32[]{:S(2)}, u32[]{:S(2)}) collective-permute-start(bf16[2,256,640]{2,1,0:T(8,128)(2,1)} %bitcast.28), channel_id=1, source_target_pairs={{0,1},{1,0},{2,3},{3,2},{4,5},{5,4},{6,7},{7,6},{8,9},{9,8},{10,11... | collective-permute-start | bytes 1966088 | tf_op jit(solution)/shard_map/ppermute | solution.py:486
  128.3 23.9 %collective-permute-start.15 = (bf16[3,160,1024]{2,1,0:T(8,128)(2,1)S(1)}, bf16[3,160,1024]{2,1,0:T(8,128)(2,1)}, u32[]{:S(2)}, u32[]{:S(2)}) collective-permute-start(bf16[3,160,1024]{2,1,0:T(8,128)(2,1)S(1)} %pad_maximum_fusion.17.refs_0_), channel_id=1, source_target_pairs={{0,8},{1,9},{2,10},{3,11},{4,12},{5,13},{6,14},{7,15},{8,0},{9,1},... | collective-permute-start | bytes 2949128 | tf_op jit(solution)/shard_map/ppermute | solution.py:486
  129.5 23.6 %collective-permute-start.16 = (bf16[3,160,1024]{2,1,0:T(8,128)(2,1)S(1)}, bf16[3,160,1024]{2,1,0:T(8,128)(2,1)}, u32[]{:S(2)}, u32[]{:S(2)}) collective-permute-start(bf16[3,160,1024]{2,1,0:T(8,128)(2,1)S(1)} %pad_maximum_fusion.18.refs_2_), channel_id=1, source_target_pairs={{0,16},{1,17},{2,18},{3,19},{4,20},{5,21},{6,22},{7,23},{8,24},{9,... | collective-permute-start | bytes 2949128 | tf_op jit(solution)/shard_map/ppermute | solution.py:486
  156.3 44.0 %collective-permute-start.21 = (bf16[3,320,1024]{2,1,0:T(8,128)(2,1)}, bf16[3,320,1024]{2,1,0:T(8,128)(2,1)}, u32[]{:S(2)}, u32[]{:S(2)}) collective-permute-start(bf16[3,320,1024]{2,1,0:T(8,128)(2,1)} %get-tuple-element.216.refs_0_), channel_id=1, source_target_pairs={{0,16},{1,17},{2,18},{3,19},{4,20},{5,21},{6,22},{7,23},{8,24},{9,... | collective-permute-start | bytes 5898248 | tf_op jit(solution)/shard_map/ppermute | solution.py:486
  156.9 43.6 %collective-permute-start.22 = (bf16[3,320,1024]{2,1,0:T(8,128)(2,1)}, bf16[3,320,1024]{2,1,0:T(8,128)(2,1)}, u32[]{:S(2)}, u32[]{:S(2)}) collective-permute-start(bf16[3,320,1024]{2,1,0:T(8,128)(2,1)} %get-tuple-element.217.refs_2_), channel_id=1, source_target_pairs={{0,8},{1,9},{2,10},{3,11},{4,12},{5,13},{6,14},{7,15},{8,0},{9,1},... | collective-permute-start | bytes 5898248 | tf_op jit(solution)/shard_map/ppermute | solution.py:486
  162.6 29.3 %collective-permute-start.20 = (bf16[32,2560]{1,0:T(8,128)(2,1)S(1)}, bf16[32,2560]{1,0:T(8,128)(2,1)S(1)}, u32[]{:S(2)}, u32[]{:S(2)}) collective-permute-start(bf16[32,2560]{1,0:T(8,128)(2,1)S(1)} %fusion.43), channel_id=1, source_target_pairs={{0,3},{1,2},{2,1},{3,0},{4,7},{5,6},{6,5},{7,4},{8,11},{9,10},{10,... | collective-permute-start | bytes 491528 | tf_op jit(solution)/shard_map/ppermute | solution.py:486
  163.3 28.6 %collective-permute-start.19 = (bf16[32,2560]{1,0:T(8,128)(2,1)S(1)}, bf16[32,2560]{1,0:T(8,128)(2,1)S(1)}, u32[]{:S(2)}, u32[]{:S(2)}) collective-permute-start(bf16[32,2560]{1,0:T(8,128)(2,1)S(1)} %fusion.43), channel_id=1, source_target_pairs={{0,2},{1,3},{2,0},{3,1},{4,6},{5,7},{6,4},{7,5},{8,10},{9,11},{10,... | collective-permute-start | bytes 491528 | tf_op jit(solution)/shard_map/ppermute | solution.py:486
  165.8 26.1 %collective-permute-start.18 = (bf16[32,2560]{1,0:T(8,128)(2,1)S(1)}, bf16[32,2560]{1,0:T(8,128)(2,1)S(1)}, u32[]{:S(2)}, u32[]{:S(2)}) collective-permute-start(bf16[32,2560]{1,0:T(8,128)(2,1)S(1)} %fusion.43), channel_id=1, source_target_pairs={{0,1},{1,0},{2,3},{3,2},{4,5},{5,4},{6,7},{7,6},{8,9},{9,8},{10,11... | collective-permute-start | bytes 491528 | tf_op jit(solution)/shard_map/ppermute | solution.py:486
  220.1 48.0 %collective-permute-start.27 = (bf16[1,2,1,4,32,1280]{5,4,3,2,1,0:T(8,128)(2,1)S(1)}, bf16[1,2,1,4,32,1280]{5,4,3,2,1,0:T(8,128)(2,1)}, u32[]{:S(2)}, u32[]{:S(2)}) collective-permute-start(bf16[1,2,1,4,32,1280]{5,4,3,2,1,0:T(8,128)(2,1)S(1)} %pad_maximum_fusion.25), channel_id=1, source_target_pairs={{0,16},{1,17},{2,18},{3,19},{4,20},{5,21},{6,22},{7,23},{8,24},{9,... | collective-permute-start | bytes 1966088 | tf_op jit(solution)/shard_map/ppermute | solution.py:486
  221.8 46.3 %collective-permute-start.28 = (bf16[2,1,1,4,32,1280]{5,4,3,2,1,0:T(8,128)(2,1)S(1)}, bf16[2,1,1,4,32,1280]{5,4,3,2,1,0:T(8,128)(2,1)}, u32[]{:S(2)}, u32[]{:S(2)}) collective-permute-start(bf16[2,1,1,4,32,1280]{5,4,3,2,1,0:T(8,128)(2,1)S(1)} %pad_maximum_fusion.26), channel_id=1, source_target_pairs={{0,8},{1,9},{2,10},{3,11},{4,12},{5,13},{6,14},{7,15},{8,0},{9,1},... | collective-permute-start | bytes 1966088 | tf_op jit(solution)/shard_map/ppermute | solution.py:486
  222.8 21.5 %collective-permute-start.31 = (bf16[3,80,1024]{2,1,0:T(8,128)(2,1)S(1)}, bf16[3,80,1024]{2,1,0:T(8,128)(2,1)}, u32[]{:S(2)}, u32[]{:S(2)}) collective-permute-start(bf16[3,80,1024]{2,1,0:T(8,128)(2,1)S(1)} %copy-done.54), channel_id=1, source_target_pairs={{0,3},{1,2},{2,1},{3,0},{4,7},{5,6},{6,5},{7,4},{8,11},{9,10},{10,... | collective-permute-start | bytes 1474568 | tf_op jit(solution)/shard_map/ppermute | solution.py:486
  223.2 44.9 %collective-permute-start.30 = (bf16[3,80,1024]{2,1,0:T(8,128)(2,1)S(1)}, bf16[3,80,1024]{2,1,0:T(8,128)(2,1)}, u32[]{:S(2)}, u32[]{:S(2)}) collective-permute-start(bf16[3,80,1024]{2,1,0:T(8,128)(2,1)S(1)} %copy-done.54), channel_id=1, source_target_pairs={{0,2},{1,3},{2,0},{3,1},{4,6},{5,7},{6,4},{7,5},{8,10},{9,11},{10,... | collective-permute-start | bytes 1474568 | tf_op jit(solution)/shard_map/ppermute | solution.py:486
  225.7 42.4 %collective-permute-start.29 = (bf16[3,80,1024]{2,1,0:T(8,128)(2,1)S(1)}, bf16[3,80,1024]{2,1,0:T(8,128)(2,1)}, u32[]{:S(2)}, u32[]{:S(2)}) collective-permute-start(bf16[3,80,1024]{2,1,0:T(8,128)(2,1)S(1)} %copy-done.54), channel_id=1, source_target_pairs={{0,1},{1,0},{2,3},{3,2},{4,5},{5,4},{6,7},{7,6},{8,9},{9,8},{10,11... | collective-permute-start | bytes 1474568 | tf_op jit(solution)/shard_map/ppermute | solution.py:486
  275.8 24.4 %collective-permute-start.34 = (bf16[3,160,1024]{2,1,0:T(8,128)(2,1)}, bf16[3,160,1024]{2,1,0:T(8,128)(2,1)}, u32[]{:S(2)}, u32[]{:S(2)}) collective-permute-start(bf16[3,160,1024]{2,1,0:T(8,128)(2,1)} %pad_maximum_fusion.19.refs_0_), channel_id=1, source_target_pairs={{0,8},{1,9},{2,10},{3,11},{4,12},{5,13},{6,14},{7,15},{8,0},{9,1},... | collective-permute-start | bytes 2949128 | tf_op jit(solution)/shard_map/ppermute | solution.py:486
  277.9 24.1 %collective-permute-start.35 = (bf16[3,160,1024]{2,1,0:T(8,128)(2,1)}, bf16[3,160,1024]{2,1,0:T(8,128)(2,1)}, u32[]{:S(2)}, u32[]{:S(2)}) collective-permute-start(bf16[3,160,1024]{2,1,0:T(8,128)(2,1)} %pad_maximum_fusion.20.refs_2_), channel_id=1, source_target_pairs={{0,16},{1,17},{2,18},{3,19},{4,20},{5,21},{6,22},{7,23},{8,24},{9,... | collective-permute-start | bytes 2949128 | tf_op jit(solution)/shard_map/ppermute | solution.py:486
  305.3 46.8 %collective-permute-start.37 = (bf16[3,320,1024]{2,1,0:T(8,128)(2,1)}, bf16[3,320,1024]{2,1,0:T(8,128)(2,1)}, u32[]{:S(2)}, u32[]{:S(2)}) collective-permute-start(bf16[3,320,1024]{2,1,0:T(8,128)(2,1)} %get-tuple-element.251.refs_0_), channel_id=1, source_target_pairs={{0,16},{1,17},{2,18},{3,19},{4,20},{5,21},{6,22},{7,23},{8,24},{9,... | collective-permute-start | bytes 5898248 | tf_op jit(solution)/shard_map/ppermute | solution.py:486
  305.8 46.3 %collective-permute-start.38 = (bf16[3,320,1024]{2,1,0:T(8,128)(2,1)}, bf16[3,320,1024]{2,1,0:T(8,128)(2,1)}, u32[]{:S(2)}, u32[]{:S(2)}) collective-permute-start(bf16[3,320,1024]{2,1,0:T(8,128)(2,1)} %get-tuple-element.252.refs_2_), channel_id=1, source_target_pairs={{0,8},{1,9},{2,10},{3,11},{4,12},{5,13},{6,14},{7,15},{8,0},{9,1},... | collective-permute-start | bytes 5898248 | tf_op jit(solution)/shard_map/ppermute | solution.py:486
  309.1 15.7 %collective-permute-start.36 = (bf16[2,256,640]{2,1,0:T(8,128)(2,1)}, bf16[2,256,640]{2,1,0:T(8,128)(2,1)}, u32[]{:S(2)}, u32[]{:S(2)}) collective-permute-start(bf16[2,256,640]{2,1,0:T(8,128)(2,1)} %bitcast.50), channel_id=1, source_target_pairs={{0,1},{1,0},{2,3},{3,2},{4,5},{5,4},{6,7},{7,6},{8,9},{9,8},{10,11... | collective-permute-start | bytes 1966088 | tf_op jit(solution)/shard_map/ppermute | solution.py:486
  327.1 25.0 %collective-permute-start.39 = (bf16[256,960]{1,0:T(8,128)(2,1)}, bf16[256,960]{1,0:T(8,128)(2,1)S(1)}, u32[]{:S(2)}, u32[]{:S(2)}) collective-permute-start(bf16[256,960]{1,0:T(8,128)(2,1)} %fusion.35), channel_id=1, source_target_pairs={{0,3},{1,2},{2,1},{3,0},{4,7},{5,6},{6,5},{7,4},{8,11},{9,10},{10,... | collective-permute-start | bytes 1474568 | tf_op jit(solution)/shard_map/ppermute | solution.py:486
  434.7 59.7 %collective-permute-start.47 = (bf16[3,320,1024]{2,1,0:T(8,128)(2,1)}, bf16[3,320,1024]{2,1,0:T(8,128)(2,1)S(1)}, u32[]{:S(2)}, u32[]{:S(2)}) collective-permute-start(bf16[3,320,1024]{2,1,0:T(8,128)(2,1)} %get-tuple-element.409), channel_id=1, source_target_pairs={{0,8},{1,9},{2,10},{3,11},{4,12},{5,13},{6,14},{7,15},{8,0},{9,1},... | collective-permute-start | bytes 5898248 | tf_op jit(solution)/shard_map/ppermute | solution.py:486
  441.2 53.2 %collective-permute-start.46 = (bf16[3,320,1024]{2,1,0:T(8,128)(2,1)}, bf16[3,320,1024]{2,1,0:T(8,128)(2,1)S(1)}, u32[]{:S(2)}, u32[]{:S(2)}) collective-permute-start(bf16[3,320,1024]{2,1,0:T(8,128)(2,1)} %get-tuple-element.411), channel_id=1, source_target_pairs={{0,16},{1,17},{2,18},{3,19},{4,20},{5,21},{6,22},{7,23},{8,24},{9,... | collective-permute-start | bytes 5898248 | tf_op jit(solution)/shard_map/ppermute | solution.py:486
  442.7 31.8 %collective-permute-start.44 = (bf16[256,960]{1,0:T(8,128)(2,1)}, bf16[256,960]{1,0:T(8,128)(2,1)}, u32[]{:S(2)}, u32[]{:S(2)}) collective-permute-start(bf16[256,960]{1,0:T(8,128)(2,1)} %select_convert_fusion.1), channel_id=1, source_target_pairs={{0,3},{1,2},{2,1},{3,0},{4,7},{5,6},{6,5},{7,4},{8,11},{9,10},{10,... | collective-permute-start | bytes 1474568 | tf_op jit(solution)/shard_map/ppermute | solution.py:486
  475.8 16.0 %collective-permute-start.45 = (bf16[2,256,640]{2,1,0:T(8,128)(2,1)S(1)}, bf16[2,256,640]{2,1,0:T(8,128)(2,1)S(1)}, u32[]{:S(2)}, u32[]{:S(2)}) collective-permute-start(bf16[2,256,640]{2,1,0:T(8,128)(2,1)S(1)} %fusion.32), channel_id=1, source_target_pairs={{0,1},{1,0},{2,3},{3,2},{4,5},{5,4},{6,7},{7,6},{8,9},{9,8},{10,11... | collective-permute-start | bytes 1966088 | tf_op jit(solution)/shard_map/ppermute | solution.py:486
  496.7 22.3 %collective-permute-start.49 = (bf16[3,160,1024]{2,1,0:T(8,128)(2,1)}, bf16[3,160,1024]{2,1,0:T(8,128)(2,1)S(1)}, u32[]{:S(2)}, u32[]{:S(2)}) collective-permute-start(bf16[3,160,1024]{2,1,0:T(8,128)(2,1)} %get-tuple-element.419), channel_id=1, source_target_pairs={{0,16},{1,17},{2,18},{3,19},{4,20},{5,21},{6,22},{7,23},{8,24},{9,... | collective-permute-start | bytes 2949128 | tf_op jit(solution)/shard_map/ppermute | solution.py:486
  499.4 22.0 %collective-permute-start.48 = (bf16[3,160,1024]{2,1,0:T(8,128)(2,1)}, bf16[3,160,1024]{2,1,0:T(8,128)(2,1)S(1)}, u32[]{:S(2)}, u32[]{:S(2)}) collective-permute-start(bf16[3,160,1024]{2,1,0:T(8,128)(2,1)} %get-tuple-element.417), channel_id=1, source_target_pairs={{0,8},{1,9},{2,10},{3,11},{4,12},{5,13},{6,14},{7,15},{8,0},{9,1},... | collective-permute-start | bytes 2949128 | tf_op jit(solution)/shard_map/ppermute | solution.py:486
  526.8 37.8 %collective-permute-start.50 = (bf16[2,2,1,4,32,1280]{5,4,3,2,1,0:T(8,128)(2,1)}, bf16[2,2,1,4,32,1280]{5,4,3,2,1,0:T(8,128)(2,1)}, u32[]{:S(2)}, u32[]{:S(2)}) collective-permute-start(bf16[2,2,1,4,32,1280]{5,4,3,2,1,0:T(8,128)(2,1)} %broadcast_select_fusion.3), channel_id=1, source_target_pairs={{0,4},{1,5},{2,6},{3,7},{4,0},{5,1},{6,2},{7,3},{8,12},{9,13},{10,... | collective-permute-start | bytes 3932168 | tf_op jit(solution)/shard_map/ppermute | solution.py:486
  534.9 29.6 %collective-permute-start.51 = (bf16[2,2,1,4,32,1280]{5,4,3,2,1,0:T(8,128)(2,1)}, bf16[2,2,1,4,32,1280]{5,4,3,2,1,0:T(8,128)(2,1)}, u32[]{:S(2)}, u32[]{:S(2)}) collective-permute-start(bf16[2,2,1,4,32,1280]{5,4,3,2,1,0:T(8,128)(2,1)} %broadcast_select_fusion.2), channel_id=1, source_target_pairs={{0,4},{1,5},{2,6},{3,7},{4,0},{5,1},{6,2},{7,3},{8,12},{9,13},{10,... | collective-permute-start | bytes 3932168 | tf_op jit(solution)/shard_map/ppermute | solution.py:486
  564.5 52.9 %collective-permute-start.52 = (bf16[3,640,1024]{2,1,0:T(8,128)(2,1)}, bf16[3,640,1024]{2,1,0:T(8,128)(2,1)S(1)}, u32[]{:S(2)}, u32[]{:S(2)}) collective-permute-start(bf16[3,640,1024]{2,1,0:T(8,128)(2,1)} %get-tuple-element.306), channel_id=1, source_target_pairs={{0,4},{1,5},{2,6},{3,7},{4,0},{5,1},{6,2},{7,3},{8,12},{9,13},{10,... | collective-permute-start | bytes 11796488 | tf_op jit(solution)/shard_map/ppermute | solution.py:486
  564.6 52.9 %collective-permute-start.53 = (bf16[3,640,1024]{2,1,0:T(8,128)(2,1)}, bf16[3,640,1024]{2,1,0:T(8,128)(2,1)S(1)}, u32[]{:S(2)}, u32[]{:S(2)}) collective-permute-start(bf16[3,640,1024]{2,1,0:T(8,128)(2,1)} %get-tuple-element.307), channel_id=1, source_target_pairs={{0,4},{1,5},{2,6},{3,7},{4,0},{5,1},{6,2},{7,3},{8,12},{9,13},{10,... | collective-permute-start | bytes 11796488 | tf_op jit(solution)/shard_map/ppermute | solution.py:486
  566.2 22.3 %collective-permute-start.56 = (bf16[3,80,1024]{2,1,0:T(8,128)(2,1)S(1)}, bf16[3,80,1024]{2,1,0:T(8,128)(2,1)S(1)}, u32[]{:S(2)}, u32[]{:S(2)}) collective-permute-start(bf16[3,80,1024]{2,1,0:T(8,128)(2,1)S(1)} %pad_maximum_fusion.29), channel_id=1, source_target_pairs={{0,1},{1,0},{2,3},{3,2},{4,5},{5,4},{6,7},{7,6},{8,9},{9,8},{10,11... | collective-permute-start | bytes 1474568 | tf_op jit(solution)/shard_map/ppermute | solution.py:486
  566.8 36.1 %collective-permute-start.57 = (bf16[3,80,1024]{2,1,0:T(8,128)(2,1)S(1)}, bf16[3,80,1024]{2,1,0:T(8,128)(2,1)S(1)}, u32[]{:S(2)}, u32[]{:S(2)}) collective-permute-start(bf16[3,80,1024]{2,1,0:T(8,128)(2,1)S(1)} %pad_maximum_fusion.30), channel_id=1, source_target_pairs={{0,2},{1,3},{2,0},{3,1},{4,6},{5,7},{6,4},{7,5},{8,10},{9,11},{10,... | collective-permute-start | bytes 1474568 | tf_op jit(solution)/shard_map/ppermute | solution.py:486
  568.1 40.8 %collective-permute-start.58 = (bf16[3,80,1024]{2,1,0:T(8,128)(2,1)S(1)}, bf16[3,80,1024]{2,1,0:T(8,128)(2,1)S(1)}, u32[]{:S(2)}, u32[]{:S(2)}) collective-permute-start(bf16[3,80,1024]{2,1,0:T(8,128)(2,1)S(1)} %pad_maximum_fusion.31), channel_id=1, source_target_pairs={{0,3},{1,2},{2,1},{3,0},{4,7},{5,6},{6,5},{7,4},{8,11},{9,10},{10,... | collective-permute-start | bytes 1474568 | tf_op jit(solution)/shard_map/ppermute | solution.py:486
  588.4 20.5 %collective-permute-start.55 = (bf16[2,1,1,4,32,1280]{5,4,3,2,1,0:T(8,128)(2,1)S(1)}, bf16[2,1,1,4,32,1280]{5,4,3,2,1,0:T(8,128)(2,1)S(1)}, u32[]{:S(2)}, u32[]{:S(2)}) collective-permute-start(bf16[2,1,1,4,32,1280]{5,4,3,2,1,0:T(8,128)(2,1)S(1)} %broadcast_select_fusion.13), channel_id=1, source_target_pairs={{0,8},{1,9},{2,10},{3,11},{4,12},{5,13},{6,14},{7,15},{8,0},{9,1},... | collective-permute-start | bytes 1966088 | tf_op jit(solution)/shard_map/ppermute | solution.py:486
  621.7 55.0 %collective-permute-start.61 = (bf16[3,320,1024]{2,1,0:T(8,128)(2,1)}, bf16[3,320,1024]{2,1,0:T(8,128)(2,1)S(1)}, u32[]{:S(2)}, u32[]{:S(2)}) collective-permute-start(bf16[3,320,1024]{2,1,0:T(8,128)(2,1)} %get-tuple-element.405), channel_id=1, source_target_pairs={{0,8},{1,9},{2,10},{3,11},{4,12},{5,13},{6,14},{7,15},{8,0},{9,1},... | collective-permute-start | bytes 5898248 | tf_op jit(solution)/shard_map/ppermute | solution.py:486
  626.8 50.0 %collective-permute-start.60 = (bf16[3,320,1024]{2,1,0:T(8,128)(2,1)}, bf16[3,320,1024]{2,1,0:T(8,128)(2,1)}, u32[]{:S(2)}, u32[]{:S(2)}) collective-permute-start(bf16[3,320,1024]{2,1,0:T(8,128)(2,1)} %get-tuple-element.406), channel_id=1, source_target_pairs={{0,16},{1,17},{2,18},{3,19},{4,20},{5,21},{6,22},{7,23},{8,24},{9,... | collective-permute-start | bytes 5898248 | tf_op jit(solution)/shard_map/ppermute | solution.py:486
  629.1 47.7 %collective-permute-start.63 = (bf16[1,1,1,4,32,1280]{5,4,3,2,1,0:T(8,128)(2,1)}, bf16[1,1,1,4,32,1280]{5,4,3,2,1,0:T(8,128)(2,1)}, u32[]{:S(2)}, u32[]{:S(2)}) collective-permute-start(bf16[1,1,1,4,32,1280]{5,4,3,2,1,0:T(8,128)(2,1)} %broadcast_select_fusion.27), channel_id=1, source_target_pairs={{0,16},{1,17},{2,18},{3,19},{4,20},{5,21},{6,22},{7,23},{8,24},{9,... | collective-permute-start | bytes 983048 | tf_op jit(solution)/shard_map/ppermute | solution.py:486
  662.1 14.6 %collective-permute-start.62 = (bf16[1,1,1,4,32,1280]{5,4,3,2,1,0:T(8,128)(2,1)}, bf16[1,1,1,4,32,1280]{5,4,3,2,1,0:T(8,128)(2,1)}, u32[]{:S(2)}, u32[]{:S(2)}) collective-permute-start(bf16[1,1,1,4,32,1280]{5,4,3,2,1,0:T(8,128)(2,1)} %broadcast_select_fusion.33), channel_id=1, source_target_pairs={{0,8},{1,9},{2,10},{3,11},{4,12},{5,13},{6,14},{7,15},{8,0},{9,1},... | collective-permute-start | bytes 983048 | tf_op jit(solution)/shard_map/ppermute | solution.py:486
  697.6 21.6 %collective-permute-start.70 = (bf16[32,1280]{1,0:T(8,128)(2,1)}, bf16[32,1280]{1,0:T(8,128)(2,1)S(1)}, u32[]{:S(2)}, u32[]{:S(2)}) collective-permute-start(bf16[32,1280]{1,0:T(8,128)(2,1)} %get-tuple-element.513), channel_id=1, source_target_pairs={{0,3},{1,2},{2,1},{3,0},{4,7},{5,6},{6,5},{7,4},{8,11},{9,10},{10,... | collective-permute-start | bytes 245768 | tf_op jit(solution)/shard_map/ppermute | solution.py:486
  697.6 23.1 %collective-permute-start.69 = (bf16[32,1280]{1,0:T(8,128)(2,1)}, bf16[32,1280]{1,0:T(8,128)(2,1)}, u32[]{:S(2)}, u32[]{:S(2)}) collective-permute-start(bf16[32,1280]{1,0:T(8,128)(2,1)} %get-tuple-element.514), channel_id=1, source_target_pairs={{0,2},{1,3},{2,0},{3,1},{4,6},{5,7},{6,4},{7,5},{8,10},{9,11},{10,... | collective-permute-start | bytes 245768 | tf_op jit(solution)/shard_map/ppermute | solution.py:486
  699.4 23.2 %collective-permute-start.68 = (bf16[32,1280]{1,0:T(8,128)(2,1)}, bf16[32,1280]{1,0:T(8,128)(2,1)}, u32[]{:S(2)}, u32[]{:S(2)}) collective-permute-start(bf16[32,1280]{1,0:T(8,128)(2,1)} %get-tuple-element.515), channel_id=1, source_target_pairs={{0,1},{1,0},{2,3},{3,2},{4,5},{5,4},{6,7},{7,6},{8,9},{9,8},{10,11... | collective-permute-start | bytes 245768 | tf_op jit(solution)/shard_map/ppermute | solution.py:486
  703.7 41.5 %collective-permute-start.66 = (bf16[2,2,1,4,32,1280]{5,4,3,2,1,0:T(8,128)(2,1)}, bf16[2,2,1,4,32,1280]{5,4,3,2,1,0:T(8,128)(2,1)}, u32[]{:S(2)}, u32[]{:S(2)}) collective-permute-start(bf16[2,2,1,4,32,1280]{5,4,3,2,1,0:T(8,128)(2,1)} %broadcast_select_fusion.1), channel_id=1, source_target_pairs={{0,4},{1,5},{2,6},{3,7},{4,0},{5,1},{6,2},{7,3},{8,12},{9,13},{10,... | collective-permute-start | bytes 3932168 | tf_op jit(solution)/shard_map/ppermute | solution.py:486
  712.1 33.1 %collective-permute-start.67 = (bf16[2,2,1,4,32,1280]{5,4,3,2,1,0:T(8,128)(2,1)}, bf16[2,2,1,4,32,1280]{5,4,3,2,1,0:T(8,128)(2,1)}, u32[]{:S(2)}, u32[]{:S(2)}) collective-permute-start(bf16[2,2,1,4,32,1280]{5,4,3,2,1,0:T(8,128)(2,1)} %broadcast_select_fusion), channel_id=1, source_target_pairs={{0,4},{1,5},{2,6},{3,7},{4,0},{5,1},{6,2},{7,3},{8,12},{9,13},{10,... | collective-permute-start | bytes 3932168 | tf_op jit(solution)/shard_map/ppermute | solution.py:486
  719.2 26.0 %collective-permute-start.65 = (bf16[3,160,1024]{2,1,0:T(8,128)(2,1)}, bf16[3,160,1024]{2,1,0:T(8,128)(2,1)}, u32[]{:S(2)}, u32[]{:S(2)}) collective-permute-start(bf16[3,160,1024]{2,1,0:T(8,128)(2,1)} %get-tuple-element.415), channel_id=1, source_target_pairs={{0,16},{1,17},{2,18},{3,19},{4,20},{5,21},{6,22},{7,23},{8,24},{9,... | collective-permute-start | bytes 2949128 | tf_op jit(solution)/shard_map/ppermute | solution.py:486
  720.7 24.4 %collective-permute-start.64 = (bf16[3,160,1024]{2,1,0:T(8,128)(2,1)}, bf16[3,160,1024]{2,1,0:T(8,128)(2,1)}, u32[]{:S(2)}, u32[]{:S(2)}) collective-permute-start(bf16[3,160,1024]{2,1,0:T(8,128)(2,1)} %get-tuple-element.413), channel_id=1, source_target_pairs={{0,8},{1,9},{2,10},{3,11},{4,12},{5,13},{6,14},{7,15},{8,0},{9,1},... | collective-permute-start | bytes 2949128 | tf_op jit(solution)/shard_map/ppermute | solution.py:486
  742.0 23.5 %collective-permute-start.76 = (bf16[256,960]{1,0:T(8,128)(2,1)}, bf16[256,960]{1,0:T(8,128)(2,1)}, u32[]{:S(2)}, u32[]{:S(2)}) collective-permute-start(bf16[256,960]{1,0:T(8,128)(2,1)} %select_convert_fusion), channel_id=1, source_target_pairs={{0,3},{1,2},{2,1},{3,0},{4,7},{5,6},{6,5},{7,4},{8,11},{9,10},{10,... | collective-permute-start | bytes 1474568 | tf_op jit(solution)/shard_map/ppermute | solution.py:486
  752.5 16.2 %collective-permute-start.75 = (bf16[2,1,1,4,32,1280]{5,4,3,2,1,0:T(8,128)(2,1)}, bf16[2,1,1,4,32,1280]{5,4,3,2,1,0:T(8,128)(2,1)}, u32[]{:S(2)}, u32[]{:S(2)}) collective-permute-start(bf16[2,1,1,4,32,1280]{5,4,3,2,1,0:T(8,128)(2,1)} %broadcast_select_fusion.12), channel_id=1, source_target_pairs={{0,8},{1,9},{2,10},{3,11},{4,12},{5,13},{6,14},{7,15},{8,0},{9,1},... | collective-permute-start | bytes 1966088 | tf_op jit(solution)/shard_map/ppermute | solution.py:486
  753.4 16.0 %collective-permute-start.74 = (bf16[1,2,1,4,32,1280]{5,4,3,2,1,0:T(8,128)(2,1)}, bf16[1,2,1,4,32,1280]{5,4,3,2,1,0:T(8,128)(2,1)}, u32[]{:S(2)}, u32[]{:S(2)}) collective-permute-start(bf16[1,2,1,4,32,1280]{5,4,3,2,1,0:T(8,128)(2,1)} %broadcast_select_fusion.18), channel_id=1, source_target_pairs={{0,16},{1,17},{2,18},{3,19},{4,20},{5,21},{6,22},{7,23},{8,24},{9,... | collective-permute-start | bytes 1966088 | tf_op jit(solution)/shard_map/ppermute | solution.py:486
  762.6 21.1 %collective-permute-start.79 = (bf16[3,80,1024]{2,1,0:T(8,128)(2,1)}, bf16[3,80,1024]{2,1,0:T(8,128)(2,1)}, u32[]{:S(2)}, u32[]{:S(2)}) collective-permute-start(bf16[3,80,1024]{2,1,0:T(8,128)(2,1)} %pad_maximum_fusion.32), channel_id=1, source_target_pairs={{0,1},{1,0},{2,3},{3,2},{4,5},{5,4},{6,7},{7,6},{8,9},{9,8},{10,11... | collective-permute-start | bytes 1474568 | tf_op jit(solution)/shard_map/ppermute | solution.py:486
  763.4 36.4 %collective-permute-start.80 = (bf16[3,80,1024]{2,1,0:T(8,128)(2,1)}, bf16[3,80,1024]{2,1,0:T(8,128)(2,1)}, u32[]{:S(2)}, u32[]{:S(2)}) collective-permute-start(bf16[3,80,1024]{2,1,0:T(8,128)(2,1)} %pad_maximum_fusion.33), channel_id=1, source_target_pairs={{0,2},{1,3},{2,0},{3,1},{4,6},{5,7},{6,4},{7,5},{8,10},{9,11},{10,... | collective-permute-start | bytes 1474568 | tf_op jit(solution)/shard_map/ppermute | solution.py:486
  765.4 34.4 %collective-permute-start.81 = (bf16[3,80,1024]{2,1,0:T(8,128)(2,1)}, bf16[3,80,1024]{2,1,0:T(8,128)(2,1)}, u32[]{:S(2)}, u32[]{:S(2)}) collective-permute-start(bf16[3,80,1024]{2,1,0:T(8,128)(2,1)} %pad_maximum_fusion.34), channel_id=1, source_target_pairs={{0,3},{1,2},{2,1},{3,0},{4,7},{5,6},{6,5},{7,4},{8,11},{9,10},{10,... | collective-permute-start | bytes 1474568 | tf_op jit(solution)/shard_map/ppermute | solution.py:486
  773.7 26.1 %collective-permute-start.78 = (bf16[1,1,1,4,32,1280]{5,4,3,2,1,0:T(8,128)(2,1)}, bf16[1,1,1,4,32,1280]{5,4,3,2,1,0:T(8,128)(2,1)}, u32[]{:S(2)}, u32[]{:S(2)}) collective-permute-start(bf16[1,1,1,4,32,1280]{5,4,3,2,1,0:T(8,128)(2,1)} %broadcast_select_fusion.26), channel_id=1, source_target_pairs={{0,16},{1,17},{2,18},{3,19},{4,20},{5,21},{6,22},{7,23},{8,24},{9,... | collective-permute-start | bytes 983048 | tf_op jit(solution)/shard_map/ppermute | solution.py:486
  774.6 25.3 %collective-permute-start.77 = (bf16[1,1,1,4,32,1280]{5,4,3,2,1,0:T(8,128)(2,1)}, bf16[1,1,1,4,32,1280]{5,4,3,2,1,0:T(8,128)(2,1)}, u32[]{:S(2)}, u32[]{:S(2)}) collective-permute-start(bf16[1,1,1,4,32,1280]{5,4,3,2,1,0:T(8,128)(2,1)} %broadcast_select_fusion.32), channel_id=1, source_target_pairs={{0,8},{1,9},{2,10},{3,11},{4,12},{5,13},{6,14},{7,15},{8,0},{9,1},... | collective-permute-start | bytes 983048 | tf_op jit(solution)/shard_map/ppermute | solution.py:486
  802.9 20.5 %collective-permute-start.84 = (bf16[32,1280]{1,0:T(8,128)(2,1)}, bf16[32,1280]{1,0:T(8,128)(2,1)}, u32[]{:S(2)}, u32[]{:S(2)}) collective-permute-start(bf16[32,1280]{1,0:T(8,128)(2,1)} %get-tuple-element.507), channel_id=1, source_target_pairs={{0,3},{1,2},{2,1},{3,0},{4,7},{5,6},{6,5},{7,4},{8,11},{9,10},{10,... | collective-permute-start | bytes 245768 | tf_op jit(solution)/shard_map/ppermute | solution.py:486
  804.7 22.3 %collective-permute-start.82 = (bf16[32,1280]{1,0:T(8,128)(2,1)}, bf16[32,1280]{1,0:T(8,128)(2,1)}, u32[]{:S(2)}, u32[]{:S(2)}) collective-permute-start(bf16[32,1280]{1,0:T(8,128)(2,1)} %get-tuple-element.508), channel_id=1, source_target_pairs={{0,1},{1,0},{2,3},{3,2},{4,5},{5,4},{6,7},{7,6},{8,9},{9,8},{10,11... | collective-permute-start | bytes 245768 | tf_op jit(solution)/shard_map/ppermute | solution.py:486
  (102 other events, 875.6 us)

commit v3 on v2

--- a/solution.py
+++ b/solution.py
@@ -541,10 +541,10 @@
 
 
 def gather_ffn_job(block):
-    half = block.shape[1] // 2
     (block,) = yield [block]
     parts = [block] + (yield ctx_stage(block))
-    sides = join([[(p, 0, half) for p in parts], [(p, half, half) for p in parts]])
+    units, half = block.shape[1], len(parts) // 2
+    sides = join([[(p, 0, units) for p in run] for run in (parts[:half], parts[half:])])
     orders = [dp_bits(color) for color in range(2)]
     for i in range(len(orders[0])):
         arrived = yield [exchange(s, dp_xor=order[i]) for s, order in zip(sides, orders)]
@@ -574,7 +574,8 @@
         arrived = yield [exchange(s, dp_xor=order[i]) for s, order in zip(sends, orders)]
         if i + 1 < len(orders[0]):
             keeps, sends = part_sums(2)
-    parts = [jnp.concatenate(pair, 1) for pair in part_sums(n_ctx)]
+    runs = part_sums(n_ctx // 2)
+    parts = [run[0] for run in runs] + [run[1] for run in runs]
     arrived = yield [exchange(parts[k], ctx_xor=k) for k in range(1, n_ctx)]
     shard = parts[0].astype(f32)
     for part in arrived:
@@ -807,7 +808,7 @@
         if layer:
             terms, normal_two = fence((terms, normal_two))
         else:
-            terms, normal_two = fence((terms, normal_two), attn_jobs[1])
+            terms, normal_two = fence((terms, normal_two), attn_jobs[1], ffn_jobs[1])
         ffn_jobs[layer] = Job(scatter_ffn_job(terms, ffn_len))
         gain_two_grad = jnp.sum(normal_two * middle * scale_two, 0)
         gradient = gradient + norm_back(normal_two, middle, scale_two, gain_two)
@@ -816,7 +817,7 @@
         if layer:
             attended_grad = fence(attended_grad, ffn_jobs[1], back)
         else:
-            attended_grad = fence(attended_grad, ffn_jobs[0], attn_jobs[1], ffn_jobs[1])
+            attended_grad = fence(attended_grad, ffn_jobs[0], attn_jobs[1])
         query_grad, kv_grad = attention_backward(
             qk, kv_all, attended_grad, lse, key_info, query_info
         )
@@ -825,9 +826,9 @@
             kv_grad = scatter_group(kv_grad).reshape(rows, 2 * KV_WIDTH)
             query_grad, kv_grad = fence((query_grad, kv_grad), ffn_jobs[1])
         else:
-            query_grad, kv_grad = fence((query_grad, kv_grad))
+            query_grad, kv_grad = fence((query_grad, kv_grad), ffn_jobs[0])
             kv_grad = scatter_group(kv_grad).reshape(rows, 2 * KV_WIDTH)
-            query_grad, kv_grad = fence((query_grad, kv_grad), ffn_jobs[0], attn_jobs[1])
+            query_grad, kv_grad = fence((query_grad, kv_grad), attn_jobs[1])
         dw_qk, dw_ov, gain_one_grad, gradient = qkv_backward(
             query_grad, kv_grad, residual, normed_one, scale_one, gain_one, w_qk, w_v,
             cosine, sine, gradient, attended, attn_low,

time: 840 us -> 828 us (0.986)
  waiting for transfers between devices: 213 us -> 187 us
  starting transfers between devices: 107 us -> 122 us
    ppermute x88, waiting for transfers between devices: 213 us -> 187 us  [exchange(): return lax.ppermute(value, AXES, pairs)]
    ppermute x88, starting transfers between devices: 107 us -> 122 us  [exchange(): return lax.ppermute(value, AXES, pairs)]
    pallas_call x4 -> x6, Pallas kernels: 19.6 us -> 24.3 us  [join(): pl.pallas_call(functools.partial(join_body, moves, len(sources), len(grou...]
  transfers between devices with their start and end apart: 88 -> 88, of which waited for: 34 -> 34; matrix products, arithmetic and copies ran while one was open for 25% -> 25% of each run, Pallas kernels for 20% -> 23%
where the time goes in v3:
time: 828 us; the launch traced here: 823 us
  Pallas kernels  251 us (30%)
  waiting for transfers between devices  187 us (23%)
  other arithmetic  149 us (18%)
  starting transfers between devices  122 us (15%)
  local copies, waits for them, and re-layouts  99.8 us (12%)
  matrix products  12.8 us (2%)
    ppermute x88, waiting for transfers between devices, exchange(): return lax.ppermute(value, AXES, pairs)  187 us
    ppermute x88, starting transfers between devices, exchange(): return lax.ppermute(value, AXES, pairs)  122 us
    pallas_call x2, Pallas kernels, attention_backward(): pl.pallas_call(attention_backward_body, out_shape=[jax.ShapeDtypeStruct((...  58.6 us
    pallas_call x2, Pallas kernels, ffn_backward(): pl.pallas_call(functools.partial(ffn_backward_body, n_pieces), grid=(n_pi...  55.2 us
    convert_element_type x12, other arithmetic, part_sums(): (k[:, run].astype(f32) + a[:, run].astype(f32)).astype(bf16)  43.1 us
    pallas_call x2, Pallas kernels, attention_forward(): pl.pallas_call(attention_forward_body, out_shape=[jax.ShapeDtypeStruct((r...  40.4 us
    pallas_call x2, Pallas kernels, ffn_forward(): pl.pallas_call(functools.partial(ffn_forward_body, n_pieces), grid=(n_pie...  33.1 us
    pallas_call x2, Pallas kernels, qkv_backward(): pl.pallas_call(qkv_backward_body, out_shape=[jax.ShapeDtypeStruct((D, QK_...  26.1 us
  transfers between devices with their start and end apart: 88, of which 34 were waited for; matrix products, arithmetic and copies ran while one was open for 25% of the time, Pallas kernels for 23%

profile of v3, /device:TPU:0, one launch (start us, length us, event | category | flops | bytes accessed | tf_op | source)
XLA Modules:
  0.0 823.0 jit_solution(421603140741384152)
XLA Ops:
  0.6 2.8 slice_reduce_fusion.2
  9.4 5.0 collective-permute-start.2
  15.0 3.8 collective-permute-start.3
  18.8 9.9 %slice_reduce_fusion = (bf16[230400]{0:T(1024)(128)(2,1)S(1)}, bf16[230400]{0:T(1024)(128)(2,1)S(1)}) fusion(bf16[2,230400]{1,0:T(2,128)(2,1)S(1)} %copy-done.46), kind=kLoop, calls=%fused_computation.117 | loop fusion | bytes 1843200 | tf_op jit(solution)/shard_map/slice | solution.py:743
  40.8 5.3 collective-permute-done.4
  52.1 12.4 %collective-permute-done.8 = bf16[256,960]{1,0:T(8,128)(2,1)S(1)} collective-permute-done((bf16[256,960]{1,0:T(8,128)(2,1)S(1)}, bf16[256,960]{1,0:T(8,128)(2,1)S(1)}, u32[]{:S(2)}, u32[]{:S(2)}) %collective-permute-start.8) | collective-permute-done | bytes 491552 | tf_op jit(solution)/shard_map/ppermute | solution.py:486
  72.2 10.1 %collective-permute-start.12 = (bf16[3,80,1024]{2,1,0:T(8,128)(2,1)}, bf16[3,80,1024]{2,1,0:T(8,128)(2,1)}, u32[]{:S(2)}, u32[]{:S(2)}) collective-permute-start(bf16[3,80,1024]{2,1,0:T(8,128)(2,1)} %pad_bitcast_fusion.1.refs_0_), channel_id=1, source_target_pairs={{0,2},{1,3},{2,0},{3,1},{4,6},{5,7},{6,4},{7,5},{8,10},{9,11},{10,... | collective-permute-start | bytes 1474568 | tf_op jit(solution)/shard_map/ppermute | solution.py:486
  88.0 3.0 broadcast_select_fusion.9
  91.7 3.5 pad_maximum_fusion.1
  95.2 4.4 reshape.394
  104.2 6.5 qkv_forward.2
  110.6 8.0 collective-permute-done.12.refs_2_
  127.2 11.8 %collective-permute-done.14 = bf16[2,256,640]{2,1,0:T(8,128)(2,1)} collective-permute-done((bf16[2,256,640]{2,1,0:T(8,128)(2,1)}, bf16[2,256,640]{2,1,0:T(8,128)(2,1)}, u32[]{:S(2)}, u32[]{:S(2)}) %collective-permute-start.14) | collective-permute-done | bytes 655392 | tf_op jit(solution)/shard_map/ppermute | solution.py:486
  141.4 7.0 collective-permute-done.15.refs_1_
  150.6 3.2 join.7
  164.8 20.4 %attention_forward.2 = (bf16[512,960]{1,0:T(8,128)(2,1)}, f32[15,1,512]{2,1,0:T(1,128)}) custom-call(bf16[512,1280]{1,0:T(8,128)(2,1)} %get-tuple-element.216.q_ref, bf16[1024,640]{1,0:T(8,128)(2,1)} %pad_maximum_fusion.13.kv_ref, s32[1024,2]{1,0:T(8,128)} %copy.70.key_info, s32[2,512]{1,0:T(2,128)} %add_bitcast_fusion.2.query_info), custom_call_target="tpu_custom_call" | custom-call | tf_op jit(solution)/shard_map/attention_forward/pallas_call | solution.py:335
  185.2 4.5 fusion.8.refs_0_
  189.6 8.2 collective-permute-done.21.refs_1_
  198.0 6.6 join.8
  208.6 6.6 collective-permute-done.25
  225.9 16.4 %ffn_forward.2 = (f32[512,960]{1,0:T(8,128)}, bf16[512,960]{1,0:T(8,128)(2,1)}, f32[512,1]{1,0:T(8,128)}, f32[512,2560]{1,0:T(8,128)}, f32[512,2560]{1,0:T(8,128)}) custom-call(f32[512,960]{1,0:T(8,128)} %fusion.8.refs_0_, f32[1,960]{1,0:T(1,128)} %broadcast_in_dim.9.refs_1_, bf16[3,640,1024]{2,1,0:T(8,128)(2,1)} %get-tuple-element.229.refs_2_.refs_4_, ...), custom_call_target="tpu_custom_call" | custom-call | tf_op jit(solution)/shard_map/ffn_forward/pallas_call | solution.py:185
  242.4 23.7 %collective-permute-done.30.refs_2_ = bf16[3,80,1024]{2,1,0:T(8,128)(2,1)} collective-permute-done((bf16[3,80,1024]{2,1,0:T(8,128)(2,1)S(1)}, bf16[3,80,1024]{2,1,0:T(8,128)(2,1)}, u32[]{:S(2)}, u32[]{:S(2)}) %collective-permute-start.30) | collective-permute-done | bytes 491552 | tf_op jit(solution)/shard_map/ppermute | solution.py:486
  279.1 4.2 reshape.401
  288.0 6.4 qkv_forward.3
  296.6 3.2 join.10
  306.2 13.7 %collective-permute-done.36 = bf16[2,256,640]{2,1,0:T(8,128)(2,1)} collective-permute-done((bf16[2,256,640]{2,1,0:T(8,128)(2,1)}, bf16[2,256,640]{2,1,0:T(8,128)(2,1)}, u32[]{:S(2)}, u32[]{:S(2)}) %collective-permute-start.36) | collective-permute-done | bytes 655392 | tf_op jit(solution)/shard_map/ppermute | solution.py:486
  323.4 20.0 %attention_forward.3 = (bf16[512,960]{1,0:T(8,128)(2,1)}, f32[15,1,512]{2,1,0:T(1,128)}) custom-call(bf16[512,1280]{1,0:T(8,128)(2,1)} %get-tuple-element.256.q_ref, bf16[1024,640]{1,0:T(8,128)(2,1)} %pad_maximum_fusion.16.kv_ref, s32[1024,2]{1,0:T(8,128)} %copy.70.key_info, s32[2,512]{1,0:T(2,128)} %add_bitcast_fusion.2.query_info), custom_call_target="tpu_custom_call" | custom-call | tf_op jit(solution)/shard_map/attention_forward/pallas_call | solution.py:335
  343.4 3.8 fusion.11.refs_0_
  347.2 6.5 join.11
  356.8 4.1 collective-permute-done.40.refs_3_.refs_5_
  361.0 5.6 collective-permute-done.41.refs_5_.refs_7_
  366.6 16.6 %ffn_forward.3 = (f32[512,960]{1,0:T(8,128)}, bf16[512,960]{1,0:T(8,128)(2,1)}, f32[512,1]{1,0:T(8,128)}, f32[512,2560]{1,0:T(8,128)}, f32[512,2560]{1,0:T(8,128)}) custom-call(f32[512,960]{1,0:T(8,128)} %fusion.11.refs_0_, f32[1,960]{1,0:T(1,128)} %broadcast_in_dim.22.refs_1_, bf16[3,640,1024]{2,1,0:T(8,128)(2,1)} %get-tuple-element.267.refs_2_.refs_4_, ...), custom_call_target="tpu_custom_call" | custom-call | tf_op jit(solution)/shard_map/ffn_forward/pallas_call | solution.py:185
  383.2 27.9 %ffn_backward.2 = (bf16[3,640,1024]{2,1,0:T(8,128)(2,1)}, bf16[3,640,1024]{2,1,0:T(8,128)(2,1)}, bf16[3,640,1024]{2,1,0:T(8,128)(2,1)}, bf16[3,640,1024]{2,1,0:T(8,128)(2,1)}, f32[512,960]{1,0:T(8,128)}) custom-call(f32[512,960]{1,0:T(8,128)} %bitcast.216, bf16[512,960]{1,0:T(8,128)(2,1)} %get-tuple-element.275.refs_1_, ...), custom_call_target="tpu_custom_call" | custom-call | tf_op jit(solution)/shard_map/ffn_backward/pallas_call | solution.py:267
  421.1 2.9 collective-permute-done.43
  424.0 5.8 add_convert_fusion.4
  430.5 5.5 add_convert_fusion.5
  440.0 29.1 %attention_backward.2 = (f32[512,960]{1,0:T(8,128)}, f32[1024,640]{1,0:T(8,128)}) custom-call(bf16[512,1280]{1,0:T(8,128)(2,1)} %get-tuple-element.256.q_ref, bf16[1024,640]{1,0:T(8,128)(2,1)} %pad_maximum_fusion.16.kv_ref, bf16[512,960]{1,0:T(8,128)(2,1)} %fusion.17.og_ref, f32[15,1,512]{2,1,0:T(1,128)} %get-tuple-element.282.lse_ref, ...), custom_call_target="tpu_custom_call" | custom-call | tf_op jit(solution)/shard_map/attention_backward/pallas_call | solution.py:407
  470.7 15.9 %collective-permute-done.45 = bf16[2,256,640]{2,1,0:T(8,128)(2,1)S(1)} collective-permute-done((bf16[2,256,640]{2,1,0:T(8,128)(2,1)S(1)}, bf16[2,256,640]{2,1,0:T(8,128)(2,1)S(1)}, u32[]{:S(2)}, u32[]{:S(2)}) %collective-permute-start.45) | collective-permute-done | bytes 655392 | tf_op jit(solution)/shard_map/ppermute | solution.py:486
  495.7 13.1 %qkv_backward.2 = (bf16[960,1280]{1,0:T(8,128)(2,1)}, bf16[960,1280]{1,0:T(8,128)(2,1)}, f32[1,960]{1,0:T(1,128)}, f32[512,960]{1,0:T(8,128)}) custom-call(f32[512,960]{1,0:T(8,128)} %get-tuple-element.293.dq_ref, f32[512,640]{1,0:T(8,128)} %bitcast.226, f32[512,960]{1,0:T(8,128)} %get-tuple-element.244.x_ref, ...), custom_call_target="tpu_custom_call" | custom-call | tf_op jit(solution)/shard_map/qkv_backward/pallas_call | solution.py:131
  509.7 4.1 collective-permute-done.49
  517.3 2.7 concatenate.157
  521.7 4.4 reshape.406
  538.8 27.3 %ffn_backward.3 = (bf16[3,640,1024]{2,1,0:T(8,128)(2,1)}, bf16[3,640,1024]{2,1,0:T(8,128)(2,1)}, bf16[3,640,1024]{2,1,0:T(8,128)(2,1)}, bf16[3,640,1024]{2,1,0:T(8,128)(2,1)}, f32[512,960]{1,0:T(8,128)}) custom-call(f32[512,960]{1,0:T(8,128)} %get-tuple-element.302.refs_0_, bf16[512,960]{1,0:T(8,128)(2,1)} %get-tuple-element.304.refs_1_, ...), custom_call_target="tpu_custom_call" | custom-call | tf_op jit(solution)/shard_map/ffn_backward/pallas_call | solution.py:267
  566.1 12.1 %collective-permute-done.53 = bf16[3,80,1024]{2,1,0:T(8,128)(2,1)} collective-permute-done((bf16[3,80,1024]{2,1,0:T(8,128)(2,1)}, bf16[3,80,1024]{2,1,0:T(8,128)(2,1)}, u32[]{:S(2)}, u32[]{:S(2)}) %collective-permute-start.53) | collective-permute-done | bytes 491552 | tf_op jit(solution)/shard_map/ppermute | solution.py:486
  581.9 3.2 copy.94
  585.1 2.7 add_convert_fusion.10
  599.2 5.5 collective-permute-done.58
  604.7 3.5 collective-permute-done.57
  609.0 6.2 add_convert_fusion
  616.0 5.5 add_convert_fusion.3
  625.2 29.5 %attention_backward.3 = (f32[512,960]{1,0:T(8,128)}, f32[1024,640]{1,0:T(8,128)}) custom-call(bf16[512,1280]{1,0:T(8,128)(2,1)} %get-tuple-element.216.q_ref, bf16[1024,640]{1,0:T(8,128)(2,1)} %pad_maximum_fusion.13.kv_ref, bf16[512,960]{1,0:T(8,128)(2,1)} %fusion.14.og_ref, f32[15,1,512]{2,1,0:T(1,128)} %get-tuple-element.323.lse_ref, ...), custom_call_target="tpu_custom_call" | custom-call | tf_op jit(solution)/shard_map/attention_backward/pallas_call | solution.py:407
  656.4 2.8 collective-permute-done.60
  659.2 6.0 collective-permute-done.59
  668.2 3.8 add_convert_fusion.12
  672.5 3.7 add_convert_fusion.13
  677.1 2.8 collective-permute-done.61
  681.4 13.0 %qkv_backward.3 = (bf16[960,1280]{1,0:T(8,128)(2,1)}, bf16[960,1280]{1,0:T(8,128)(2,1)}, f32[1,960]{1,0:T(1,128)}, f32[512,960]{1,0:T(8,128)}) custom-call(f32[512,960]{1,0:T(8,128)} %get-tuple-element.334.dq_ref, f32[512,640]{1,0:T(8,128)} %bitcast.227, f32[512,960]{1,0:T(8,128)} %bitcast.218, bf16[512,960]{1,0:T(8,128)(2,1)} %get-tuple-element.336.normed_ref, ...), custom_call_target="tpu_custom_call" | custom-call | tf_op jit(solution)/shard_map/qkv_backward/pallas_call | solution.py:131
  695.3 2.7 concatenate.163
  703.1 4.4 reshape.410
  719.0 3.8 stack_reshape.23
  737.3 3.0 add_convert_fusion.8
  740.3 3.2 add_convert_fusion.9
  758.3 22.1 %collective-permute-start.79 = (bf16[3,80,1024]{2,1,0:T(8,128)(2,1)}, bf16[3,80,1024]{2,1,0:T(8,128)(2,1)}, u32[]{:S(2)}, u32[]{:S(2)}) collective-permute-start(bf16[3,80,1024]{2,1,0:T(8,128)(2,1)} %add_convert_fusion.26), channel_id=1, source_target_pairs={{0,1},{1,0},{2,3},{3,2},{4,5},{5,4},{6,7},{7,6},{8,9},{9,8},{10,11... | collective-permute-start | bytes 1474568 | tf_op jit(solution)/shard_map/ppermute | solution.py:486
  791.0 7.4 collective-permute-done.80
  (519 shorter events, 267.5 us)
Async XLA Ops:
  9.4 26.8 %collective-permute-start.2 = (bf16[32,2560]{1,0:T(8,128)(2,1)}, bf16[32,2560]{1,0:T(8,128)(2,1)}, u32[]{:S(2)}, u32[]{:S(2)}) collective-permute-start(bf16[32,2560]{1,0:T(8,128)(2,1)} %fusion.47), channel_id=1, source_target_pairs={{0,3},{1,2},{2,1},{3,0},{4,7},{5,6},{6,5},{7,4},{8,11},{9,10},{10,... | collective-permute-start | bytes 491528 | tf_op jit(solution)/shard_map/ppermute | solution.py:486
  14.4 21.8 %collective-permute-start.1 = (bf16[32,2560]{1,0:T(8,128)(2,1)}, bf16[32,2560]{1,0:T(8,128)(2,1)}, u32[]{:S(2)}, u32[]{:S(2)}) collective-permute-start(bf16[32,2560]{1,0:T(8,128)(2,1)} %fusion.47), channel_id=1, source_target_pairs={{0,2},{1,3},{2,0},{3,1},{4,6},{5,7},{6,4},{7,5},{8,10},{9,11},{10,... | collective-permute-start | bytes 491528 | tf_op jit(solution)/shard_map/ppermute | solution.py:486
  14.4 21.8 %collective-permute-start = (bf16[32,2560]{1,0:T(8,128)(2,1)}, bf16[32,2560]{1,0:T(8,128)(2,1)}, u32[]{:S(2)}, u32[]{:S(2)}) collective-permute-start(bf16[32,2560]{1,0:T(8,128)(2,1)} %fusion.47), channel_id=1, source_target_pairs={{0,1},{1,0},{2,3},{3,2},{4,5},{5,4},{6,7},{7,6},{8,9},{9,8},{10,11... | collective-permute-start | bytes 491528 | tf_op jit(solution)/shard_map/ppermute | solution.py:486
  15.0 21.2 %collective-permute-start.3 = (s32[256,2]{0,1:T(2,128)S(1)}, s32[256,2]{0,1:T(2,128)}, u32[]{:S(2)}, u32[]{:S(2)}) collective-permute-start(s32[256,2]{0,1:T(2,128)S(1)} %select_bitcast_fusion.12), channel_id=1, source_target_pairs={{0,3},{1,2},{2,1},{3,0},{4,7},{5,6},{6,5},{7,4},{8,11},{9,10},{10,... | collective-permute-start | bytes 6152 | tf_op jit(solution)/shard_map/ppermute | solution.py:486
  48.5 16.0 %collective-permute-start.6 = (bf16[1,2,1,4,32,1280]{5,4,3,2,1,0:T(8,128)(2,1)S(1)}, bf16[1,2,1,4,32,1280]{5,4,3,2,1,0:T(8,128)(2,1)S(1)}, u32[]{:S(2)}, u32[]{:S(2)}) collective-permute-start(bf16[1,2,1,4,32,1280]{5,4,3,2,1,0:T(8,128)(2,1)S(1)} %pad_maximum_fusion.19), channel_id=1, source_target_pairs={{0,16},{1,17},{2,18},{3,19},{4,20},{5,21},{6,22},{7,23},{8,24},{9,... | collective-permute-start | bytes 1966088 | tf_op jit(solution)/shard_map/ppermute | solution.py:486
  51.2 14.1 %collective-permute-start.7 = (bf16[2,1,1,4,32,1280]{5,4,3,2,1,0:T(8,128)(2,1)S(1)}, bf16[2,1,1,4,32,1280]{5,4,3,2,1,0:T(8,128)(2,1)S(1)}, u32[]{:S(2)}, u32[]{:S(2)}) collective-permute-start(bf16[2,1,1,4,32,1280]{5,4,3,2,1,0:T(8,128)(2,1)S(1)} %pad_maximum_fusion.20), channel_id=1, source_target_pairs={{0,8},{1,9},{2,10},{3,11},{4,12},{5,13},{6,14},{7,15},{8,0},{9,1},... | collective-permute-start | bytes 1966088 | tf_op jit(solution)/shard_map/ppermute | solution.py:486
  66.9 18.1 %collective-permute-start.9 = (bf16[2,2,1,4,32,1280]{5,4,3,2,1,0:T(8,128)(2,1)}, bf16[2,2,1,4,32,1280]{5,4,3,2,1,0:T(8,128)(2,1)}, u32[]{:S(2)}, u32[]{:S(2)}) collective-permute-start(bf16[2,2,1,4,32,1280]{5,4,3,2,1,0:T(8,128)(2,1)} %pad_maximum_fusion.11), channel_id=1, source_target_pairs={{0,4},{1,5},{2,6},{3,7},{4,0},{5,1},{6,2},{7,3},{8,12},{9,13},{10,... | collective-permute-start | bytes 3932168 | tf_op jit(solution)/shard_map/ppermute | solution.py:486
  68.1 17.0 %collective-permute-start.10 = (bf16[2,2,1,4,32,1280]{5,4,3,2,1,0:T(8,128)(2,1)}, bf16[2,2,1,4,32,1280]{5,4,3,2,1,0:T(8,128)(2,1)}, u32[]{:S(2)}, u32[]{:S(2)}) collective-permute-start(bf16[2,2,1,4,32,1280]{5,4,3,2,1,0:T(8,128)(2,1)} %pad_maximum_fusion.12), channel_id=1, source_target_pairs={{0,4},{1,5},{2,6},{3,7},{4,0},{5,1},{6,2},{7,3},{8,12},{9,13},{10,... | collective-permute-start | bytes 3932168 | tf_op jit(solution)/shard_map/ppermute | solution.py:486
  71.8 38.8 %collective-permute-start.13 = (bf16[3,80,1024]{2,1,0:T(8,128)(2,1)}, bf16[3,80,1024]{2,1,0:T(8,128)(2,1)}, u32[]{:S(2)}, u32[]{:S(2)}) collective-permute-start(bf16[3,80,1024]{2,1,0:T(8,128)(2,1)} %pad_bitcast_fusion.1.refs_0_), channel_id=1, source_target_pairs={{0,3},{1,2},{2,1},{3,0},{4,7},{5,6},{6,5},{7,4},{8,11},{9,10},{10,... | collective-permute-start | bytes 1474568 | tf_op jit(solution)/shard_map/ppermute | solution.py:486
  72.2 46.5 %collective-permute-start.12 = (bf16[3,80,1024]{2,1,0:T(8,128)(2,1)}, bf16[3,80,1024]{2,1,0:T(8,128)(2,1)}, u32[]{:S(2)}, u32[]{:S(2)}) collective-permute-start(bf16[3,80,1024]{2,1,0:T(8,128)(2,1)} %pad_bitcast_fusion.1.refs_0_), channel_id=1, source_target_pairs={{0,2},{1,3},{2,0},{3,1},{4,6},{5,7},{6,4},{7,5},{8,10},{9,11},{10,... | collective-permute-start | bytes 1474568 | tf_op jit(solution)/shard_map/ppermute | solution.py:486
  82.3 36.4 %collective-permute-start.11 = (bf16[3,80,1024]{2,1,0:T(8,128)(2,1)}, bf16[3,80,1024]{2,1,0:T(8,128)(2,1)}, u32[]{:S(2)}, u32[]{:S(2)}) collective-permute-start(bf16[3,80,1024]{2,1,0:T(8,128)(2,1)} %pad_bitcast_fusion.1.refs_0_), channel_id=1, source_target_pairs={{0,1},{1,0},{2,3},{3,2},{4,5},{5,4},{6,7},{7,6},{8,9},{9,8},{10,11... | collective-permute-start | bytes 1474568 | tf_op jit(solution)/shard_map/ppermute | solution.py:486
  122.1 17.0 %collective-permute-start.14 = (bf16[2,256,640]{2,1,0:T(8,128)(2,1)}, bf16[2,256,640]{2,1,0:T(8,128)(2,1)}, u32[]{:S(2)}, u32[]{:S(2)}) collective-permute-start(bf16[2,256,640]{2,1,0:T(8,128)(2,1)} %bitcast.28), channel_id=1, source_target_pairs={{0,1},{1,0},{2,3},{3,2},{4,5},{5,4},{6,7},{7,6},{8,9},{9,8},{10,11... | collective-permute-start | bytes 1966088 | tf_op jit(solution)/shard_map/ppermute | solution.py:486
  124.5 24.0 %collective-permute-start.15 = (bf16[3,160,1024]{2,1,0:T(8,128)(2,1)}, bf16[3,160,1024]{2,1,0:T(8,128)(2,1)S(1)}, u32[]{:S(2)}, u32[]{:S(2)}) collective-permute-start(bf16[3,160,1024]{2,1,0:T(8,128)(2,1)} %get-tuple-element.214.refs_0_), channel_id=1, source_target_pairs={{0,8},{1,9},{2,10},{3,11},{4,12},{5,13},{6,14},{7,15},{8,0},{9,1},... | collective-permute-start | bytes 2949128 | tf_op jit(solution)/shard_map/ppermute | solution.py:486
  126.0 23.6 %collective-permute-start.16 = (bf16[3,160,1024]{2,1,0:T(8,128)(2,1)}, bf16[3,160,1024]{2,1,0:T(8,128)(2,1)S(1)}, u32[]{:S(2)}, u32[]{:S(2)}) collective-permute-start(bf16[3,160,1024]{2,1,0:T(8,128)(2,1)} %get-tuple-element.215.refs_2_), channel_id=1, source_target_pairs={{0,16},{1,17},{2,18},{3,19},{4,20},{5,21},{6,22},{7,23},{8,24},{9,... | collective-permute-start | bytes 2949128 | tf_op jit(solution)/shard_map/ppermute | solution.py:486
  153.8 44.0 %collective-permute-start.21 = (bf16[3,320,1024]{2,1,0:T(8,128)(2,1)}, bf16[3,320,1024]{2,1,0:T(8,128)(2,1)}, u32[]{:S(2)}, u32[]{:S(2)}) collective-permute-start(bf16[3,320,1024]{2,1,0:T(8,128)(2,1)} %get-tuple-element.224.refs_0_), channel_id=1, source_target_pairs={{0,16},{1,17},{2,18},{3,19},{4,20},{5,21},{6,22},{7,23},{8,24},{9,... | collective-permute-start | bytes 5898248 | tf_op jit(solution)/shard_map/ppermute | solution.py:486
  154.4 43.7 %collective-permute-start.22 = (bf16[3,320,1024]{2,1,0:T(8,128)(2,1)}, bf16[3,320,1024]{2,1,0:T(8,128)(2,1)}, u32[]{:S(2)}, u32[]{:S(2)}) collective-permute-start(bf16[3,320,1024]{2,1,0:T(8,128)(2,1)} %get-tuple-element.225.refs_2_), channel_id=1, source_target_pairs={{0,8},{1,9},{2,10},{3,11},{4,12},{5,13},{6,14},{7,15},{8,0},{9,1},... | collective-permute-start | bytes 5898248 | tf_op jit(solution)/shard_map/ppermute | solution.py:486
  160.4 29.3 %collective-permute-start.20 = (bf16[32,2560]{1,0:T(8,128)(2,1)S(1)}, bf16[32,2560]{1,0:T(8,128)(2,1)S(1)}, u32[]{:S(2)}, u32[]{:S(2)}) collective-permute-start(bf16[32,2560]{1,0:T(8,128)(2,1)S(1)} %fusion.45), channel_id=1, source_target_pairs={{0,3},{1,2},{2,1},{3,0},{4,7},{5,6},{6,5},{7,4},{8,11},{9,10},{10,... | collective-permute-start | bytes 491528 | tf_op jit(solution)/shard_map/ppermute | solution.py:486
  161.1 28.5 %collective-permute-start.19 = (bf16[32,2560]{1,0:T(8,128)(2,1)S(1)}, bf16[32,2560]{1,0:T(8,128)(2,1)S(1)}, u32[]{:S(2)}, u32[]{:S(2)}) collective-permute-start(bf16[32,2560]{1,0:T(8,128)(2,1)S(1)} %fusion.45), channel_id=1, source_target_pairs={{0,2},{1,3},{2,0},{3,1},{4,6},{5,7},{6,4},{7,5},{8,10},{9,11},{10,... | collective-permute-start | bytes 491528 | tf_op jit(solution)/shard_map/ppermute | solution.py:486
  163.6 26.0 %collective-permute-start.18 = (bf16[32,2560]{1,0:T(8,128)(2,1)S(1)}, bf16[32,2560]{1,0:T(8,128)(2,1)S(1)}, u32[]{:S(2)}, u32[]{:S(2)}) collective-permute-start(bf16[32,2560]{1,0:T(8,128)(2,1)S(1)} %fusion.45), channel_id=1, source_target_pairs={{0,1},{1,0},{2,3},{3,2},{4,5},{5,4},{6,7},{7,6},{8,9},{9,8},{10,11... | collective-permute-start | bytes 491528 | tf_op jit(solution)/shard_map/ppermute | solution.py:486
  217.7 48.5 %collective-permute-start.27 = (bf16[1,2,1,4,32,1280]{5,4,3,2,1,0:T(8,128)(2,1)S(1)}, bf16[1,2,1,4,32,1280]{5,4,3,2,1,0:T(8,128)(2,1)}, u32[]{:S(2)}, u32[]{:S(2)}) collective-permute-start(bf16[1,2,1,4,32,1280]{5,4,3,2,1,0:T(8,128)(2,1)S(1)} %pad_maximum_fusion.21), channel_id=1, source_target_pairs={{0,16},{1,17},{2,18},{3,19},{4,20},{5,21},{6,22},{7,23},{8,24},{9,... | collective-permute-start | bytes 1966088 | tf_op jit(solution)/shard_map/ppermute | solution.py:486
  219.3 46.8 %collective-permute-start.28 = (bf16[2,1,1,4,32,1280]{5,4,3,2,1,0:T(8,128)(2,1)S(1)}, bf16[2,1,1,4,32,1280]{5,4,3,2,1,0:T(8,128)(2,1)}, u32[]{:S(2)}, u32[]{:S(2)}) collective-permute-start(bf16[2,1,1,4,32,1280]{5,4,3,2,1,0:T(8,128)(2,1)S(1)} %pad_maximum_fusion.22), channel_id=1, source_target_pairs={{0,8},{1,9},{2,10},{3,11},{4,12},{5,13},{6,14},{7,15},{8,0},{9,1},... | collective-permute-start | bytes 1966088 | tf_op jit(solution)/shard_map/ppermute | solution.py:486
  220.9 21.5 %collective-permute-start.31 = (bf16[3,80,1024]{2,1,0:T(8,128)(2,1)S(1)}, bf16[3,80,1024]{2,1,0:T(8,128)(2,1)}, u32[]{:S(2)}, u32[]{:S(2)}) collective-permute-start(bf16[3,80,1024]{2,1,0:T(8,128)(2,1)S(1)} %copy-done.51), channel_id=1, source_target_pairs={{0,3},{1,2},{2,1},{3,0},{4,7},{5,6},{6,5},{7,4},{8,11},{9,10},{10,... | collective-permute-start | bytes 1474568 | tf_op jit(solution)/shard_map/ppermute | solution.py:486
  221.3 44.9 %collective-permute-start.30 = (bf16[3,80,1024]{2,1,0:T(8,128)(2,1)S(1)}, bf16[3,80,1024]{2,1,0:T(8,128)(2,1)}, u32[]{:S(2)}, u32[]{:S(2)}) collective-permute-start(bf16[3,80,1024]{2,1,0:T(8,128)(2,1)S(1)} %copy-done.51), channel_id=1, source_target_pairs={{0,2},{1,3},{2,0},{3,1},{4,6},{5,7},{6,4},{7,5},{8,10},{9,11},{10,... | collective-permute-start | bytes 1474568 | tf_op jit(solution)/shard_map/ppermute | solution.py:486
  223.8 42.4 %collective-permute-start.29 = (bf16[3,80,1024]{2,1,0:T(8,128)(2,1)S(1)}, bf16[3,80,1024]{2,1,0:T(8,128)(2,1)}, u32[]{:S(2)}, u32[]{:S(2)}) collective-permute-start(bf16[3,80,1024]{2,1,0:T(8,128)(2,1)S(1)} %copy-done.51), channel_id=1, source_target_pairs={{0,1},{1,0},{2,3},{3,2},{4,5},{5,4},{6,7},{7,6},{8,9},{9,8},{10,11... | collective-permute-start | bytes 1474568 | tf_op jit(solution)/shard_map/ppermute | solution.py:486
  271.8 24.5 %collective-permute-start.34 = (bf16[3,160,1024]{2,1,0:T(8,128)(2,1)}, bf16[3,160,1024]{2,1,0:T(8,128)(2,1)}, u32[]{:S(2)}, u32[]{:S(2)}) collective-permute-start(bf16[3,160,1024]{2,1,0:T(8,128)(2,1)} %get-tuple-element.252.refs_0_), channel_id=1, source_target_pairs={{0,8},{1,9},{2,10},{3,11},{4,12},{5,13},{6,14},{7,15},{8,0},{9,1},... | collective-permute-start | bytes 2949128 | tf_op jit(solution)/shard_map/ppermute | solution.py:486
  272.4 24.1 %collective-permute-start.35 = (bf16[3,160,1024]{2,1,0:T(8,128)(2,1)}, bf16[3,160,1024]{2,1,0:T(8,128)(2,1)}, u32[]{:S(2)}, u32[]{:S(2)}) collective-permute-start(bf16[3,160,1024]{2,1,0:T(8,128)(2,1)} %get-tuple-element.253.refs_2_), channel_id=1, source_target_pairs={{0,16},{1,17},{2,18},{3,19},{4,20},{5,21},{6,22},{7,23},{8,24},{9,... | collective-permute-start | bytes 2949128 | tf_op jit(solution)/shard_map/ppermute | solution.py:486
  299.8 47.4 %collective-permute-start.37 = (bf16[3,320,1024]{2,1,0:T(8,128)(2,1)}, bf16[3,320,1024]{2,1,0:T(8,128)(2,1)}, u32[]{:S(2)}, u32[]{:S(2)}) collective-permute-start(bf16[3,320,1024]{2,1,0:T(8,128)(2,1)} %get-tuple-element.261.refs_0_), channel_id=1, source_target_pairs={{0,16},{1,17},{2,18},{3,19},{4,20},{5,21},{6,22},{7,23},{8,24},{9,... | collective-permute-start | bytes 5898248 | tf_op jit(solution)/shard_map/ppermute | solution.py:486
  300.6 46.6 %collective-permute-start.38 = (bf16[3,320,1024]{2,1,0:T(8,128)(2,1)}, bf16[3,320,1024]{2,1,0:T(8,128)(2,1)}, u32[]{:S(2)}, u32[]{:S(2)}) collective-permute-start(bf16[3,320,1024]{2,1,0:T(8,128)(2,1)} %get-tuple-element.262.refs_2_), channel_id=1, source_target_pairs={{0,8},{1,9},{2,10},{3,11},{4,12},{5,13},{6,14},{7,15},{8,0},{9,1},... | collective-permute-start | bytes 5898248 | tf_op jit(solution)/shard_map/ppermute | solution.py:486
  304.2 15.7 %collective-permute-start.36 = (bf16[2,256,640]{2,1,0:T(8,128)(2,1)}, bf16[2,256,640]{2,1,0:T(8,128)(2,1)}, u32[]{:S(2)}, u32[]{:S(2)}) collective-permute-start(bf16[2,256,640]{2,1,0:T(8,128)(2,1)} %bitcast.50), channel_id=1, source_target_pairs={{0,1},{1,0},{2,3},{3,2},{4,5},{5,4},{6,7},{7,6},{8,9},{9,8},{10,11... | collective-permute-start | bytes 1966088 | tf_op jit(solution)/shard_map/ppermute | solution.py:486
  322.2 25.0 %collective-permute-start.39 = (bf16[256,960]{1,0:T(8,128)(2,1)}, bf16[256,960]{1,0:T(8,128)(2,1)S(1)}, u32[]{:S(2)}, u32[]{:S(2)}) collective-permute-start(bf16[256,960]{1,0:T(8,128)(2,1)} %fusion.37), channel_id=1, source_target_pairs={{0,3},{1,2},{2,1},{3,0},{4,7},{5,6},{6,5},{7,4},{8,11},{9,10},{10,... | collective-permute-start | bytes 1474568 | tf_op jit(solution)/shard_map/ppermute | solution.py:486
  429.8 59.3 %collective-permute-start.47 = (bf16[3,320,1024]{2,1,0:T(8,128)(2,1)}, bf16[3,320,1024]{2,1,0:T(8,128)(2,1)S(1)}, u32[]{:S(2)}, u32[]{:S(2)}) collective-permute-start(bf16[3,320,1024]{2,1,0:T(8,128)(2,1)} %get-tuple-element.421), channel_id=1, source_target_pairs={{0,8},{1,9},{2,10},{3,11},{4,12},{5,13},{6,14},{7,15},{8,0},{9,1},... | collective-permute-start | bytes 5898248 | tf_op jit(solution)/shard_map/ppermute | solution.py:486
  436.0 53.1 %collective-permute-start.46 = (bf16[3,320,1024]{2,1,0:T(8,128)(2,1)}, bf16[3,320,1024]{2,1,0:T(8,128)(2,1)S(1)}, u32[]{:S(2)}, u32[]{:S(2)}) collective-permute-start(bf16[3,320,1024]{2,1,0:T(8,128)(2,1)} %get-tuple-element.423), channel_id=1, source_target_pairs={{0,16},{1,17},{2,18},{3,19},{4,20},{5,21},{6,22},{7,23},{8,24},{9,... | collective-permute-start | bytes 5898248 | tf_op jit(solution)/shard_map/ppermute | solution.py:486
  437.4 31.8 %collective-permute-start.44 = (bf16[256,960]{1,0:T(8,128)(2,1)}, bf16[256,960]{1,0:T(8,128)(2,1)}, u32[]{:S(2)}, u32[]{:S(2)}) collective-permute-start(bf16[256,960]{1,0:T(8,128)(2,1)} %select_convert_fusion.1), channel_id=1, source_target_pairs={{0,3},{1,2},{2,1},{3,0},{4,7},{5,6},{6,5},{7,4},{8,11},{9,10},{10,... | collective-permute-start | bytes 1474568 | tf_op jit(solution)/shard_map/ppermute | solution.py:486
  470.6 16.0 %collective-permute-start.45 = (bf16[2,256,640]{2,1,0:T(8,128)(2,1)S(1)}, bf16[2,256,640]{2,1,0:T(8,128)(2,1)S(1)}, u32[]{:S(2)}, u32[]{:S(2)}) collective-permute-start(bf16[2,256,640]{2,1,0:T(8,128)(2,1)S(1)} %fusion.34), channel_id=1, source_target_pairs={{0,1},{1,0},{2,3},{3,2},{4,5},{5,4},{6,7},{7,6},{8,9},{9,8},{10,11... | collective-permute-start | bytes 1966088 | tf_op jit(solution)/shard_map/ppermute | solution.py:486
  491.4 22.4 %collective-permute-start.49 = (bf16[3,160,1024]{2,1,0:T(8,128)(2,1)}, bf16[3,160,1024]{2,1,0:T(8,128)(2,1)}, u32[]{:S(2)}, u32[]{:S(2)}) collective-permute-start(bf16[3,160,1024]{2,1,0:T(8,128)(2,1)} %get-tuple-element.429), channel_id=1, source_target_pairs={{0,16},{1,17},{2,18},{3,19},{4,20},{5,21},{6,22},{7,23},{8,24},{9,... | collective-permute-start | bytes 2949128 | tf_op jit(solution)/shard_map/ppermute | solution.py:486
  494.3 22.0 %collective-permute-start.48 = (bf16[3,160,1024]{2,1,0:T(8,128)(2,1)}, bf16[3,160,1024]{2,1,0:T(8,128)(2,1)S(1)}, u32[]{:S(2)}, u32[]{:S(2)}) collective-permute-start(bf16[3,160,1024]{2,1,0:T(8,128)(2,1)} %get-tuple-element.431), channel_id=1, source_target_pairs={{0,8},{1,9},{2,10},{3,11},{4,12},{5,13},{6,14},{7,15},{8,0},{9,1},... | collective-permute-start | bytes 2949128 | tf_op jit(solution)/shard_map/ppermute | solution.py:486
  521.7 56.6 %collective-permute-start.50 = (bf16[2,2,1,4,32,1280]{5,4,3,2,1,0:T(8,128)(2,1)}, bf16[2,2,1,4,32,1280]{5,4,3,2,1,0:T(8,128)(2,1)}, u32[]{:S(2)}, u32[]{:S(2)}) collective-permute-start(bf16[2,2,1,4,32,1280]{5,4,3,2,1,0:T(8,128)(2,1)} %broadcast_select_fusion.3), channel_id=1, source_target_pairs={{0,4},{1,5},{2,6},{3,7},{4,0},{5,1},{6,2},{7,3},{8,12},{9,13},{10,... | collective-permute-start | bytes 3932168 | tf_op jit(solution)/shard_map/ppermute | solution.py:486
  530.0 48.2 %collective-permute-start.51 = (bf16[2,2,1,4,32,1280]{5,4,3,2,1,0:T(8,128)(2,1)}, bf16[2,2,1,4,32,1280]{5,4,3,2,1,0:T(8,128)(2,1)}, u32[]{:S(2)}, u32[]{:S(2)}) collective-permute-start(bf16[2,2,1,4,32,1280]{5,4,3,2,1,0:T(8,128)(2,1)} %broadcast_select_fusion.2), channel_id=1, source_target_pairs={{0,4},{1,5},{2,6},{3,7},{4,0},{5,1},{6,2},{7,3},{8,12},{9,13},{10,... | collective-permute-start | bytes 3932168 | tf_op jit(solution)/shard_map/ppermute | solution.py:486
  533.1 33.0 %collective-permute-start.54 = (bf16[3,80,1024]{2,1,0:T(8,128)(2,1)}, bf16[3,80,1024]{2,1,0:T(8,128)(2,1)S(1)}, u32[]{:S(2)}, u32[]{:S(2)}) collective-permute-start(bf16[3,80,1024]{2,1,0:T(8,128)(2,1)} %get-tuple-element.450), channel_id=1, source_target_pairs={{0,3},{1,2},{2,1},{3,0},{4,7},{5,6},{6,5},{7,4},{8,11},{9,10},{10,... | collective-permute-start | bytes 1474568 | tf_op jit(solution)/shard_map/ppermute | solution.py:486
  534.3 44.0 %collective-permute-start.53 = (bf16[3,80,1024]{2,1,0:T(8,128)(2,1)}, bf16[3,80,1024]{2,1,0:T(8,128)(2,1)}, u32[]{:S(2)}, u32[]{:S(2)}) collective-permute-start(bf16[3,80,1024]{2,1,0:T(8,128)(2,1)} %get-tuple-element.451), channel_id=1, source_target_pairs={{0,2},{1,3},{2,0},{3,1},{4,6},{5,7},{6,4},{7,5},{8,10},{9,11},{10,... | collective-permute-start | bytes 1474568 | tf_op jit(solution)/shard_map/ppermute | solution.py:486
  536.2 42.1 %collective-permute-start.52 = (bf16[3,80,1024]{2,1,0:T(8,128)(2,1)}, bf16[3,80,1024]{2,1,0:T(8,128)(2,1)}, u32[]{:S(2)}, u32[]{:S(2)}) collective-permute-start(bf16[3,80,1024]{2,1,0:T(8,128)(2,1)} %add_convert_fusion.29), channel_id=1, source_target_pairs={{0,1},{1,0},{2,3},{3,2},{4,5},{5,4},{6,7},{7,6},{8,9},{9,8},{10,11... | collective-permute-start | bytes 1474568 | tf_op jit(solution)/shard_map/ppermute | solution.py:486
  578.3 29.9 %collective-permute-start.55 = (bf16[3,640,1024]{2,1,0:T(8,128)(2,1)}, bf16[3,640,1024]{2,1,0:T(8,128)(2,1)}, u32[]{:S(2)}, u32[]{:S(2)}) collective-permute-start(bf16[3,640,1024]{2,1,0:T(8,128)(2,1)} %get-tuple-element.318), channel_id=1, source_target_pairs={{0,4},{1,5},{2,6},{3,7},{4,0},{5,1},{6,2},{7,3},{8,12},{9,13},{10,... | collective-permute-start | bytes 11796488 | tf_op jit(solution)/shard_map/ppermute | solution.py:486
  578.4 30.7 %collective-permute-start.56 = (bf16[3,640,1024]{2,1,0:T(8,128)(2,1)}, bf16[3,640,1024]{2,1,0:T(8,128)(2,1)}, u32[]{:S(2)}, u32[]{:S(2)}) collective-permute-start(bf16[3,640,1024]{2,1,0:T(8,128)(2,1)} %get-tuple-element.319), channel_id=1, source_target_pairs={{0,4},{1,5},{2,6},{3,7},{4,0},{5,1},{6,2},{7,3},{8,12},{9,13},{10,... | collective-permute-start | bytes 11796488 | tf_op jit(solution)/shard_map/ppermute | solution.py:486
  587.9 16.8 %collective-permute-start.58 = (bf16[2,1,1,4,32,1280]{5,4,3,2,1,0:T(8,128)(2,1)S(1)}, bf16[2,1,1,4,32,1280]{5,4,3,2,1,0:T(8,128)(2,1)S(1)}, u32[]{:S(2)}, u32[]{:S(2)}) collective-permute-start(bf16[2,1,1,4,32,1280]{5,4,3,2,1,0:T(8,128)(2,1)S(1)} %broadcast_select_fusion.13), channel_id=1, source_target_pairs={{0,8},{1,9},{2,10},{3,11},{4,12},{5,13},{6,14},{7,15},{8,0},{9,1},... | collective-permute-start | bytes 1966088 | tf_op jit(solution)/shard_map/ppermute | solution.py:486
  591.7 16.5 %collective-permute-start.57 = (bf16[1,2,1,4,32,1280]{5,4,3,2,1,0:T(8,128)(2,1)S(1)}, bf16[1,2,1,4,32,1280]{5,4,3,2,1,0:T(8,128)(2,1)S(1)}, u32[]{:S(2)}, u32[]{:S(2)}) collective-permute-start(bf16[1,2,1,4,32,1280]{5,4,3,2,1,0:T(8,128)(2,1)S(1)} %broadcast_select_fusion.19), channel_id=1, source_target_pairs={{0,16},{1,17},{2,18},{3,19},{4,20},{5,21},{6,22},{7,23},{8,24},{9,... | collective-permute-start | bytes 1966088 | tf_op jit(solution)/shard_map/ppermute | solution.py:486
  615.3 44.0 %collective-permute-start.60 = (bf16[3,320,1024]{2,1,0:T(8,128)(2,1)}, bf16[3,320,1024]{2,1,0:T(8,128)(2,1)}, u32[]{:S(2)}, u32[]{:S(2)}) collective-permute-start(bf16[3,320,1024]{2,1,0:T(8,128)(2,1)} %get-tuple-element.417), channel_id=1, source_target_pairs={{0,8},{1,9},{2,10},{3,11},{4,12},{5,13},{6,14},{7,15},{8,0},{9,1},... | collective-permute-start | bytes 5898248 | tf_op jit(solution)/shard_map/ppermute | solution.py:486
  621.5 43.8 %collective-permute-start.59 = (bf16[3,320,1024]{2,1,0:T(8,128)(2,1)}, bf16[3,320,1024]{2,1,0:T(8,128)(2,1)}, u32[]{:S(2)}, u32[]{:S(2)}) collective-permute-start(bf16[3,320,1024]{2,1,0:T(8,128)(2,1)} %get-tuple-element.418), channel_id=1, source_target_pairs={{0,16},{1,17},{2,18},{3,19},{4,20},{5,21},{6,22},{7,23},{8,24},{9,... | collective-permute-start | bytes 5898248 | tf_op jit(solution)/shard_map/ppermute | solution.py:486
  665.4 14.5 %collective-permute-start.61 = (bf16[2,256,640]{2,1,0:T(8,128)(2,1)S(1)}, bf16[2,256,640]{2,1,0:T(8,128)(2,1)S(1)}, u32[]{:S(2)}, u32[]{:S(2)}) collective-permute-start(bf16[2,256,640]{2,1,0:T(8,128)(2,1)S(1)} %fusion.35), channel_id=1, source_target_pairs={{0,1},{1,0},{2,3},{3,2},{4,5},{5,4},{6,7},{7,6},{8,9},{9,8},{10,11... | collective-permute-start | bytes 1966088 | tf_op jit(solution)/shard_map/ppermute | solution.py:486
  665.5 15.7 %collective-permute-start.63 = (bf16[1,1,1,4,32,1280]{5,4,3,2,1,0:T(8,128)(2,1)S(1)}, bf16[1,1,1,4,32,1280]{5,4,3,2,1,0:T(8,128)(2,1)S(1)}, u32[]{:S(2)}, u32[]{:S(2)}) collective-permute-start(bf16[1,1,1,4,32,1280]{5,4,3,2,1,0:T(8,128)(2,1)S(1)} %broadcast_select_fusion.27), channel_id=1, source_target_pairs={{0,16},{1,17},{2,18},{3,19},{4,20},{5,21},{6,22},{7,23},{8,24},{9,... | collective-permute-start | bytes 983048 | tf_op jit(solution)/shard_map/ppermute | solution.py:486
  667.0 14.1 %collective-permute-start.62 = (bf16[1,1,1,4,32,1280]{5,4,3,2,1,0:T(8,128)(2,1)S(1)}, bf16[1,1,1,4,32,1280]{5,4,3,2,1,0:T(8,128)(2,1)S(1)}, u32[]{:S(2)}, u32[]{:S(2)}) collective-permute-start(bf16[1,1,1,4,32,1280]{5,4,3,2,1,0:T(8,128)(2,1)S(1)} %broadcast_select_fusion.33), channel_id=1, source_target_pairs={{0,8},{1,9},{2,10},{3,11},{4,12},{5,13},{6,14},{7,15},{8,0},{9,1},... | collective-permute-start | bytes 983048 | tf_op jit(solution)/shard_map/ppermute | solution.py:486
  672.0 64.1 %collective-permute-start.65 = (bf16[3,160,1024]{2,1,0:T(8,128)(2,1)}, bf16[3,160,1024]{2,1,0:T(8,128)(2,1)}, u32[]{:S(2)}, u32[]{:S(2)}) collective-permute-start(bf16[3,160,1024]{2,1,0:T(8,128)(2,1)} %get-tuple-element.425), channel_id=1, source_target_pairs={{0,16},{1,17},{2,18},{3,19},{4,20},{5,21},{6,22},{7,23},{8,24},{9,... | collective-permute-start | bytes 2949128 | tf_op jit(solution)/shard_map/ppermute | solution.py:486
  676.2 59.9 %collective-permute-start.64 = (bf16[3,160,1024]{2,1,0:T(8,128)(2,1)}, bf16[3,160,1024]{2,1,0:T(8,128)(2,1)}, u32[]{:S(2)}, u32[]{:S(2)}) collective-permute-start(bf16[3,160,1024]{2,1,0:T(8,128)(2,1)} %get-tuple-element.427), channel_id=1, source_target_pairs={{0,8},{1,9},{2,10},{3,11},{4,12},{5,13},{6,14},{7,15},{8,0},{9,1},... | collective-permute-start | bytes 2949128 | tf_op jit(solution)/shard_map/ppermute | solution.py:486
  698.7 14.4 %collective-permute-start.70 = (bf16[32,1280]{1,0:T(8,128)(2,1)}, bf16[32,1280]{1,0:T(8,128)(2,1)S(1)}, u32[]{:S(2)}, u32[]{:S(2)}) collective-permute-start(bf16[32,1280]{1,0:T(8,128)(2,1)} %get-tuple-element.497), channel_id=1, source_target_pairs={{0,3},{1,2},{2,1},{3,0},{4,7},{5,6},{6,5},{7,4},{8,11},{9,10},{10,... | collective-permute-start | bytes 245768 | tf_op jit(solution)/shard_map/ppermute | solution.py:486
  700.5 13.9 %collective-permute-start.68 = (bf16[32,1280]{1,0:T(8,128)(2,1)}, bf16[32,1280]{1,0:T(8,128)(2,1)}, u32[]{:S(2)}, u32[]{:S(2)}) collective-permute-start(bf16[32,1280]{1,0:T(8,128)(2,1)} %get-tuple-element.499), channel_id=1, source_target_pairs={{0,1},{1,0},{2,3},{3,2},{4,5},{5,4},{6,7},{7,6},{8,9},{9,8},{10,11... | collective-permute-start | bytes 245768 | tf_op jit(solution)/shard_map/ppermute | solution.py:486
  713.2 22.9 %collective-permute-start.66 = (bf16[2,2,1,4,32,1280]{5,4,3,2,1,0:T(8,128)(2,1)}, bf16[2,2,1,4,32,1280]{5,4,3,2,1,0:T(8,128)(2,1)}, u32[]{:S(2)}, u32[]{:S(2)}) collective-permute-start(bf16[2,2,1,4,32,1280]{5,4,3,2,1,0:T(8,128)(2,1)} %broadcast_select_fusion.1), channel_id=1, source_target_pairs={{0,4},{1,5},{2,6},{3,7},{4,0},{5,1},{6,2},{7,3},{8,12},{9,13},{10,... | collective-permute-start | bytes 3932168 | tf_op jit(solution)/shard_map/ppermute | solution.py:486
  713.2 22.9 %collective-permute-start.67 = (bf16[2,2,1,4,32,1280]{5,4,3,2,1,0:T(8,128)(2,1)}, bf16[2,2,1,4,32,1280]{5,4,3,2,1,0:T(8,128)(2,1)}, u32[]{:S(2)}, u32[]{:S(2)}) collective-permute-start(bf16[2,2,1,4,32,1280]{5,4,3,2,1,0:T(8,128)(2,1)} %broadcast_select_fusion), channel_id=1, source_target_pairs={{0,4},{1,5},{2,6},{3,7},{4,0},{5,1},{6,2},{7,3},{8,12},{9,13},{10,... | collective-permute-start | bytes 3932168 | tf_op jit(solution)/shard_map/ppermute | solution.py:486
  733.6 24.7 %collective-permute-start.76 = (bf16[256,960]{1,0:T(8,128)(2,1)}, bf16[256,960]{1,0:T(8,128)(2,1)}, u32[]{:S(2)}, u32[]{:S(2)}) collective-permute-start(bf16[256,960]{1,0:T(8,128)(2,1)} %select_convert_fusion), channel_id=1, source_target_pairs={{0,3},{1,2},{2,1},{3,0},{4,7},{5,6},{6,5},{7,4},{8,11},{9,10},{10,... | collective-permute-start | bytes 1474568 | tf_op jit(solution)/shard_map/ppermute | solution.py:486
  746.7 33.6 %collective-permute-start.75 = (bf16[2,1,1,4,32,1280]{5,4,3,2,1,0:T(8,128)(2,1)}, bf16[2,1,1,4,32,1280]{5,4,3,2,1,0:T(8,128)(2,1)}, u32[]{:S(2)}, u32[]{:S(2)}) collective-permute-start(bf16[2,1,1,4,32,1280]{5,4,3,2,1,0:T(8,128)(2,1)} %broadcast_select_fusion.12), channel_id=1, source_target_pairs={{0,8},{1,9},{2,10},{3,11},{4,12},{5,13},{6,14},{7,15},{8,0},{9,1},... | collective-permute-start | bytes 1966088 | tf_op jit(solution)/shard_map/ppermute | solution.py:486
  747.7 32.6 %collective-permute-start.74 = (bf16[1,2,1,4,32,1280]{5,4,3,2,1,0:T(8,128)(2,1)S(1)}, bf16[1,2,1,4,32,1280]{5,4,3,2,1,0:T(8,128)(2,1)}, u32[]{:S(2)}, u32[]{:S(2)}) collective-permute-start(bf16[1,2,1,4,32,1280]{5,4,3,2,1,0:T(8,128)(2,1)S(1)} %broadcast_select_fusion.18), channel_id=1, source_target_pairs={{0,16},{1,17},{2,18},{3,19},{4,20},{5,21},{6,22},{7,23},{8,24},{9,... | collective-permute-start | bytes 1966088 | tf_op jit(solution)/shard_map/ppermute | solution.py:486
  752.7 38.3 %collective-permute-start.81 = (bf16[3,80,1024]{2,1,0:T(8,128)(2,1)}, bf16[3,80,1024]{2,1,0:T(8,128)(2,1)}, u32[]{:S(2)}, u32[]{:S(2)}) collective-permute-start(bf16[3,80,1024]{2,1,0:T(8,128)(2,1)} %get-tuple-element.448), channel_id=1, source_target_pairs={{0,3},{1,2},{2,1},{3,0},{4,7},{5,6},{6,5},{7,4},{8,11},{9,10},{10,... | collective-permute-start | bytes 1474568 | tf_op jit(solution)/shard_map/ppermute | solution.py:486
  754.0 44.4 %collective-permute-start.80 = (bf16[3,80,1024]{2,1,0:T(8,128)(2,1)}, bf16[3,80,1024]{2,1,0:T(8,128)(2,1)}, u32[]{:S(2)}, u32[]{:S(2)}) collective-permute-start(bf16[3,80,1024]{2,1,0:T(8,128)(2,1)} %get-tuple-element.449), channel_id=1, source_target_pairs={{0,2},{1,3},{2,0},{3,1},{4,6},{5,7},{6,4},{7,5},{8,10},{9,11},{10,... | collective-permute-start | bytes 1474568 | tf_op jit(solution)/shard_map/ppermute | solution.py:486
  758.3 40.1 %collective-permute-start.79 = (bf16[3,80,1024]{2,1,0:T(8,128)(2,1)}, bf16[3,80,1024]{2,1,0:T(8,128)(2,1)}, u32[]{:S(2)}, u32[]{:S(2)}) collective-permute-start(bf16[3,80,1024]{2,1,0:T(8,128)(2,1)} %add_convert_fusion.26), channel_id=1, source_target_pairs={{0,1},{1,0},{2,3},{3,2},{4,5},{5,4},{6,7},{7,6},{8,9},{9,8},{10,11... | collective-permute-start | bytes 1474568 | tf_op jit(solution)/shard_map/ppermute | solution.py:486
  803.7 13.9 %collective-permute-start.82 = (bf16[32,1280]{1,0:T(8,128)(2,1)}, bf16[32,1280]{1,0:T(8,128)(2,1)}, u32[]{:S(2)}, u32[]{:S(2)}) collective-permute-start(bf16[32,1280]{1,0:T(8,128)(2,1)} %get-tuple-element.492), channel_id=1, source_target_pairs={{0,1},{1,0},{2,3},{3,2},{4,5},{5,4},{6,7},{7,6},{8,9},{9,8},{10,11... | collective-permute-start | bytes 245768 | tf_op jit(solution)/shard_map/ppermute | solution.py:486
  803.7 13.9 %collective-permute-start.83 = (bf16[32,1280]{1,0:T(8,128)(2,1)}, bf16[32,1280]{1,0:T(8,128)(2,1)}, u32[]{:S(2)}, u32[]{:S(2)}) collective-permute-start(bf16[32,1280]{1,0:T(8,128)(2,1)} %get-tuple-element.493), channel_id=1, source_target_pairs={{0,2},{1,3},{2,0},{3,1},{4,6},{5,7},{6,4},{7,5},{8,10},{9,11},{10,... | collective-permute-start | bytes 245768 | tf_op jit(solution)/shard_map/ppermute | solution.py:486
  (103 other events, 830.5 us)
